TPU v7x, 256 devices: a whole 4x4x8 slice. The times are simulated.
256 devices in a mesh: tmpl: 4 (over y), freq: 64 (over x, z, core).
Axes of the slice: x: 4, y: 4, z: 8, core: 2. Of those that a mesh axis runs over, the one named last changes fastest.
Arguments:
- strain: float32 [64, 524288], P('tmpl', 'freq'), may hold values from -6 to 6
- psd: float32 [512, 512], P(None, 'freq'), may hold values from 0.1 to 10
- templates: bfloat16 [1024, 2, 512, 512], P('tmpl', None, 'freq'), may hold values from -0.0234375 to 0.0234375
- cutoffs: int32 [1024], P('tmpl'), may hold values from 1 to 512, as said below
- lags: int32 [16], replicated, may hold values from 0 to 524287
Outputs:
- intersections: float32 [64, 32, 1024], P('freq', None, 'tmpl')
Inputs may be any that keep to these rules, and one draw needn't show every extreme that they name: `cutoffs`: the cutoff counts do not increase along the template index.
All inputs are finite; a program needn't handle non-finite values.
Results may differ from a plain program's by a relative error of at most 0.004.
Values may be sent and summed in bfloat16 or wider, within the bound.
A program may use at most 128 MiB of HBM per device.

v0:
```python
import math

import jax
import jax.numpy as jnp
from jax import lax
from jax.sharding import PartitionSpec as P

A = 512
B = 1024
LEN = 524288
NB = 512


two_pi = 2.0 * math.pi


def cos_sin_table(row_ids, col_ids, modulus):
    product = row_ids[:, None] * col_ids[None, :] % modulus
    phase_angle = product.astype(jnp.float32) * (two_pi / modulus)
    return (jnp.cos(phase_angle), jnp.sin(phase_angle))


def on_device(strain, psd, templates, cutoffs, lags):
    freq_count = lax.axis_size("freq")
    freq_index = lax.axis_index("freq")
    seg_local = strain.shape[0]
    step_time = B // freq_count
    highest = lax.Precision.HIGHEST
    first_cos, first_sin = cos_sin_table(
        jnp.arange(A, dtype=jnp.int32), jnp.arange(A, dtype=jnp.int32), A
    )
    first_table = jnp.concatenate([first_cos, -first_sin], axis=0)
    time_ids = freq_index * step_time + jnp.arange(step_time, dtype=jnp.int32)
    twist_cos, twist_sin = cos_sin_table(jnp.arange(A, dtype=jnp.int32), time_ids, LEN)
    slab_blocks = strain.reshape(seg_local, A // freq_count, B)
    both_parts = jnp.einsum(
        "kn,snb->skb",
        first_table,
        lax.all_to_all(slab_blocks, "freq", split_axis=2, concat_axis=1, tiled=True),
        precision=highest,
    )
    half_rows = first_table.shape[0] // 2
    real_part = both_parts[:, :half_rows]
    imag_part = both_parts[:, half_rows:]
    second_cos, second_sin = cos_sin_table(
        jnp.arange(B, dtype=jnp.int32), jnp.arange(NB, dtype=jnp.int32), B
    )
    rotation = jnp.concatenate(
        [
            jnp.concatenate([second_cos, -second_sin], axis=1),
            jnp.concatenate([second_sin, second_cos], axis=1),
        ],
        axis=0,
    )
    amplitude = jnp.sqrt(LEN * psd)
    real_in = lax.all_to_all(
        real_part * twist_cos + imag_part * twist_sin,
        "freq",
        split_axis=1,
        concat_axis=2,
        tiled=True,
    )
    imag_in = lax.all_to_all(
        imag_part * twist_cos - real_part * twist_sin,
        "freq",
        split_axis=1,
        concat_axis=2,
        tiled=True,
    )
    joined = jnp.concatenate([real_in, imag_in], axis=2)
    both_out = jnp.einsum("spc,cm->smp", joined, rotation, precision=highest)
    both_out = both_out.reshape(joined.shape[0], 2, NB, joined.shape[1])
    whitened = (both_out / amplitude).astype(jnp.bfloat16)
    local_data = lax.all_to_all(whitened, "freq", split_axis=2, concat_axis=3, tiled=True)
    first_block = freq_index * (NB // freq_count)
    position = jnp.arange(A, dtype=jnp.int32)
    blocks_here = local_data.shape[2]
    width_here = local_data.shape[3]
    per_span = min(blocks_here, max(1, 512 // width_here))
    span_total = blocks_here // per_span
    tmpl_local = templates.shape[0]
    group_size = min(128, tmpl_local)
    group_total = tmpl_local // group_size
    group_top = jnp.max(cutoffs.reshape(group_total, group_size), axis=1)
    lag_total = lags.shape[0]

    def multiply(lhs_rows, tmpl_cols):
        return lax.dot_general(
            lhs_rows, tmpl_cols, (((1,), (1,)), ((), ())), preferred_element_type=jnp.float32
        )

    def skipped(lhs_rows, tmpl_cols):
        return jnp.zeros((lhs_rows.shape[0], tmpl_cols.shape[0]), jnp.float32)

    seg_piece = lax.all_gather(local_data, "tmpl", axis=0, tiled=True)
    seg_count = seg_piece.shape[0]

    def one_span(span_idx, running):
        offset = span_idx * per_span
        block_ids = first_block + offset + jnp.arange(per_span, dtype=jnp.int32)
        data_part = lax.dynamic_slice_in_dim(seg_piece, offset, per_span, 2).astype(jnp.float32)
        tmpl_part = lax.dynamic_slice_in_dim(templates, offset, per_span, 2)
        phase_int = (A * (lags[:, None] * block_ids[None, :] % B))[:, :, None] + (
            lags[:, None] * position[None, :] % LEN
        )[:, None, :]
        phase_angle = (phase_int % LEN).astype(jnp.float32) * (two_pi / LEN)
        lag_cos = jnp.cos(phase_angle)[None]
        lag_sin = jnp.sin(phase_angle)[None]
        data_real = data_part[:, 0][:, None]
        data_imag = data_part[:, 1][:, None]
        real_q = (data_real * lag_cos - data_imag * lag_sin).astype(jnp.bfloat16)
        imag_q = (data_real * lag_sin + data_imag * lag_cos).astype(jnp.bfloat16)
        real_rows = jnp.stack([real_q, imag_q], axis=2)
        imag_rows = jnp.stack([imag_q, -real_q], axis=2)
        lhs_rows = jnp.stack([real_rows, imag_rows], axis=1).reshape(
            seg_count * 2 * lag_total, 2 * per_span * width_here
        )
        keep_mask = (block_ids[None, :] < cutoffs[:, None]).astype(jnp.bfloat16)
        masked = (tmpl_part * keep_mask[:, None, :, None]).reshape(
            tmpl_local, 2 * per_span * width_here
        )
        outputs = []
        for group_idx in range(group_total):
            tmpl_cols = masked[group_idx * group_size : (group_idx + 1) * group_size]
            outputs.append(
                lax.cond(
                    group_top[group_idx] > block_ids[0], multiply, skipped, lhs_rows, tmpl_cols
                )
            )
        return running + jnp.concatenate(outputs, axis=1)

    start_sum = jnp.zeros((seg_count * 2 * lag_total, tmpl_local), jnp.float32)
    running = lax.fori_loop(0, span_total, one_span, start_sum)
    partial_sums = running.reshape(seg_count, 2 * lag_total, tmpl_local)
    return lax.psum_scatter(partial_sums, "freq", scatter_dimension=0, tiled=True)


def solution(mesh):
    placed = (P("tmpl", "freq"), P(None, "freq"), P("tmpl", None, "freq", None), P("tmpl"), P())
    return jax.shard_map(
        on_device, mesh=mesh, in_specs=placed, out_specs=P("freq", None, "tmpl"), check_vma=False
    )
```

profile of v0, /device:TPU:1, one launch (start us, length us, event | category | flops | bytes accessed | tf_op | source)
XLA Modules:
  0.0 700.1 jit_solution(18072741686901560476)
XLA Ops:
  10.6 4.2 reshape.319
  14.8 13.3 %all-to-all-start = ((f32[64,1,2048]{2,1,0:T(1,128)}), f32[64,1,2048]{2,1,0:T(1,128)S(1)}, u32[]{:S(2)}, u32[]{:S(2)}) async-start(f32[64,1,2048]{2,1,0:T(1,128)} %reshape.319), calls=%async_computation | async-start | bytes 1048576 | tf_op jit(solution)/shard_map/all_to_all | solution.py:39
  28.1 4.1 sine_negate_fusion
  32.5 12.8 %all-to-all-done = f32[64,1,2048]{2,1,0:T(1,128)S(1)} async-done(((f32[64,1,2048]{2,1,0:T(1,128)}), f32[64,1,2048]{2,1,0:T(1,128)S(1)}, u32[]{:S(2)}, u32[]{:S(2)}) %all-to-all-start) | async-done | bytes 524320 | tf_op jit(solution)/shard_map/all_to_all | solution.py:39
  50.5 6.0 copy.125
  61.5 3.6 copy.127
  65.1 4.2 reshape.323
  69.3 6.3 all-to-all-start.1
  75.6 3.6 copy.130
  79.2 4.2 reshape.321
  83.5 9.5 %all-to-all-done.1 = f32[64,1,2048]{2,1,0:T(1,128)S(1)} async-done(((f32[64,1,2048]{2,1,0:T(1,128)}), f32[64,1,2048]{2,1,0:T(1,128)S(1)}, u32[]{:S(2)}, u32[]{:S(2)}) %all-to-all-start.1) | async-done | bytes 524320 | tf_op jit(solution)/shard_map/all_to_all | solution.py:56
  92.9 6.5 all-to-all-start.2
  99.5 9.0 %fusion.40 = (f32[1024,512]{1,0:T(8,128)S(1)}, f32[1024,512]{1,0:T(8,128)}) fusion(), kind=kLoop, calls=%fused_computation.69 | loop fusion | flops 7340032 | bytes 4194304 | tf_op jit(solution)/shard_map/sin | solution.py:20
  108.5 8.6 %fusion.43 = f32[1024,512]{1,0:T(8,128)} fusion(), kind=kLoop, calls=%fused_computation.72 | loop fusion | flops 7864320 | bytes 2097152 | tf_op jit(solution)/shard_map/neg | solution.py:50
  121.7 6.6 copy.145
  128.3 4.7 reshape.317
  138.9 6.6 copy.147
  145.5 4.7 reshape.318
  150.2 9.3 %fusion.31 = f32[16,1024,8]{1,0,2:T(8,128)S(1)} fusion(f32[1024,512]{1,0:T(8,128)} %get-tuple-element.412, f32[1024,512]{1,0:T(8,128)S(1)} %get-tuple-element.411, f32[1024,512]{1,0:T(8,128)} %fusion.43, f32[16,8,1024]{2,0,1:T(8,128)S(1)} %reshape.318, f32[16,8,1024]{2,0,1:T(8,128)S(1)} %reshape.317), kind=kOutput, calls=%fused_computation.59 | convolution fusion | flops 3227779072 | bytes 7864320 | tf_op jit(solution)/shard_map/spc,cm->smp/dot_general | solution.py:71
  164.2 22.1 %all_to_all.72 = bf16[64,2,1024]{2,1,0:T(2,128)(2,1)S(1)} all-to-all(bf16[64,2,1024]{2,1,0:T(2,128)(2,1)S(1)} %reshape.325), channel_id=1, replica_groups=mesh['tmpl'=4,'freq'=64] {'freq'}, dimensions={0} | all-to-all | bytes 524288 | tf_op jit(solution)/shard_map/all_to_all | solution.py:74
  192.4 7.5 %copy.141 = bf16[256,2,8,512]{0,3,1,2:T(8,128)(2,1)} copy(bf16[256,2,8,512]{3,2,1,0:T(8,128)(2,1)} %param.13) | data formatting | bytes 8388608
  200.0 14.9 %all-gather.2.cloned.1.call-done = bf16[64,2,8,512]{3,2,1,0:T(8,128)(2,1)} async-done(((bf16[16,2,8,512]{3,2,1,0:T(8,128)(2,1)}), bf16[64,2,8,512]{3,2,1,0:T(8,128)(2,1)}) %all-gather.2.cloned.1.call-update) | async-done | bytes 1048592 | tf_op jit(solution)/shard_map/all_gather | solution.py:95
  217.7 340.2 %while.17 = (s32[]{:T(128)}, f32[2048,256]{1,0:T(8,128)}, s32[2]{0:T(128)S(1)}, s32[]{:T(128)}, bf16[64,2,8,512]{3,0,2,1:T(8,128)(2,1)}, /*index=5*/s32[16]{0:T(...) while((s32[]{:T(128)}, f32[2048,256]{1,0:T(8,128)}, ...), condition=%wide.region_6.7_spmd.clone, body=%wide.region_1.6_spmd.clone.sunk | while | flops 1091060480 | bytes 48302564 | solution.py:133
  219.1 4.8 fusion.71
  226.7 10.4 %maximum_bitcast_fusion.7 = (bf16[64,1,16,2,1,512]{5,3,2,1,0,4:T(2,128)(2,1)S(1)}, bf16[64,1,16,2,1,512]{5,3,2,1,0,4:T(2,128)(2,1)}) fusion(bf16[64,16,1,1,512]{4,2,1,0,3:T(2,128)(2,1)S(1)} %add_convert_fusion.2, bf16[64,16,1,1,512]{4,2,1,0,3:T(2,128)(2,1)S(1)} %get-tuple-element.477, bf16[64,16,1,1,512]{4,2,1,0,3:T(2,128)(2,1)S(1)} %get-tuple-element.478), kind=kLoop, calls=%fused_computation.2.clone.1 | loop fusion | flops 8388608 | bytes 7340032 | tf_op jit(solution)/shard_map/while/body/eval_jaxpr/stack | solution.py:115
  237.1 7.2 %pad_maximum_fusion.2 = bf16[64,2,16,2,1,512]{5,3,2,1,0,4:T(2,128)(2,1)S(1)} fusion(bf16[64,1,16,2,1,512]{5,3,2,1,0,4:T(2,128)(2,1)} %get-tuple-element.479, bf16[64,1,16,2,1,512]{5,3,2,1,0,4:T(2,128)(2,1)S(1)} %get-tuple-element.480), kind=kLoop, calls=%fused_computation.1.clone.1 | loop fusion | flops 2097152 | bytes 8388608 | tf_op jit(solution)/shard_map/while/body/eval_jaxpr/stack | solution.py:115
  249.8 3.5 conditional.7
  254.0 3.5 conditional.6
  260.2 4.8 fusion.71
  267.9 10.4 %maximum_bitcast_fusion.7 = (bf16[64,1,16,2,1,512]{5,3,2,1,0,4:T(2,128)(2,1)S(1)}, bf16[64,1,16,2,1,512]{5,3,2,1,0,4:T(2,128)(2,1)}) fusion(bf16[64,16,1,1,512]{4,2,1,0,3:T(2,128)(2,1)S(1)} %add_convert_fusion.2, bf16[64,16,1,1,512]{4,2,1,0,3:T(2,128)(2,1)S(1)} %get-tuple-element.477, bf16[64,16,1,1,512]{4,2,1,0,3:T(2,128)(2,1)S(1)} %get-tuple-element.478), kind=kLoop, calls=%fused_computation.2.clone.1 | loop fusion | flops 8388608 | bytes 7340032 | tf_op jit(solution)/shard_map/while/body/eval_jaxpr/stack | solution.py:115
  278.2 7.2 %pad_maximum_fusion.2 = bf16[64,2,16,2,1,512]{5,3,2,1,0,4:T(2,128)(2,1)S(1)} fusion(bf16[64,1,16,2,1,512]{5,3,2,1,0,4:T(2,128)(2,1)} %get-tuple-element.479, bf16[64,1,16,2,1,512]{5,3,2,1,0,4:T(2,128)(2,1)S(1)} %get-tuple-element.480), kind=kLoop, calls=%fused_computation.1.clone.1 | loop fusion | flops 2097152 | bytes 8388608 | tf_op jit(solution)/shard_map/while/body/eval_jaxpr/stack | solution.py:115
  291.0 3.5 conditional.7
  295.1 3.5 conditional.6
  303.0 4.8 fusion.71
  310.6 10.4 %maximum_bitcast_fusion.7 = (bf16[64,1,16,2,1,512]{5,3,2,1,0,4:T(2,128)(2,1)S(1)}, bf16[64,1,16,2,1,512]{5,3,2,1,0,4:T(2,128)(2,1)}) fusion(bf16[64,16,1,1,512]{4,2,1,0,3:T(2,128)(2,1)S(1)} %add_convert_fusion.2, bf16[64,16,1,1,512]{4,2,1,0,3:T(2,128)(2,1)S(1)} %get-tuple-element.477, bf16[64,16,1,1,512]{4,2,1,0,3:T(2,128)(2,1)S(1)} %get-tuple-element.478), kind=kLoop, calls=%fused_computation.2.clone.1 | loop fusion | flops 8388608 | bytes 7340032 | tf_op jit(solution)/shard_map/while/body/eval_jaxpr/stack | solution.py:115
  320.9 7.2 %pad_maximum_fusion.2 = bf16[64,2,16,2,1,512]{5,3,2,1,0,4:T(2,128)(2,1)S(1)} fusion(bf16[64,1,16,2,1,512]{5,3,2,1,0,4:T(2,128)(2,1)} %get-tuple-element.479, bf16[64,1,16,2,1,512]{5,3,2,1,0,4:T(2,128)(2,1)S(1)} %get-tuple-element.480), kind=kLoop, calls=%fused_computation.1.clone.1 | loop fusion | flops 2097152 | bytes 8388608 | tf_op jit(solution)/shard_map/while/body/eval_jaxpr/stack | solution.py:115
  333.7 3.5 conditional.7
  337.8 3.5 conditional.6
  345.7 4.8 fusion.71
  353.3 10.4 %maximum_bitcast_fusion.7 = (bf16[64,1,16,2,1,512]{5,3,2,1,0,4:T(2,128)(2,1)S(1)}, bf16[64,1,16,2,1,512]{5,3,2,1,0,4:T(2,128)(2,1)}) fusion(bf16[64,16,1,1,512]{4,2,1,0,3:T(2,128)(2,1)S(1)} %add_convert_fusion.2, bf16[64,16,1,1,512]{4,2,1,0,3:T(2,128)(2,1)S(1)} %get-tuple-element.477, bf16[64,16,1,1,512]{4,2,1,0,3:T(2,128)(2,1)S(1)} %get-tuple-element.478), kind=kLoop, calls=%fused_computation.2.clone.1 | loop fusion | flops 8388608 | bytes 7340032 | tf_op jit(solution)/shard_map/while/body/eval_jaxpr/stack | solution.py:115
  363.6 7.2 %pad_maximum_fusion.2 = bf16[64,2,16,2,1,512]{5,3,2,1,0,4:T(2,128)(2,1)S(1)} fusion(bf16[64,1,16,2,1,512]{5,3,2,1,0,4:T(2,128)(2,1)} %get-tuple-element.479, bf16[64,1,16,2,1,512]{5,3,2,1,0,4:T(2,128)(2,1)S(1)} %get-tuple-element.480), kind=kLoop, calls=%fused_computation.1.clone.1 | loop fusion | flops 2097152 | bytes 8388608 | tf_op jit(solution)/shard_map/while/body/eval_jaxpr/stack | solution.py:115
  376.4 3.5 conditional.7
  380.5 3.5 conditional.6
  388.4 4.8 fusion.71
  396.0 10.4 %maximum_bitcast_fusion.7 = (bf16[64,1,16,2,1,512]{5,3,2,1,0,4:T(2,128)(2,1)S(1)}, bf16[64,1,16,2,1,512]{5,3,2,1,0,4:T(2,128)(2,1)}) fusion(bf16[64,16,1,1,512]{4,2,1,0,3:T(2,128)(2,1)S(1)} %add_convert_fusion.2, bf16[64,16,1,1,512]{4,2,1,0,3:T(2,128)(2,1)S(1)} %get-tuple-element.477, bf16[64,16,1,1,512]{4,2,1,0,3:T(2,128)(2,1)S(1)} %get-tuple-element.478), kind=kLoop, calls=%fused_computation.2.clone.1 | loop fusion | flops 8388608 | bytes 7340032 | tf_op jit(solution)/shard_map/while/body/eval_jaxpr/stack | solution.py:115
  406.3 7.2 %pad_maximum_fusion.2 = bf16[64,2,16,2,1,512]{5,3,2,1,0,4:T(2,128)(2,1)S(1)} fusion(bf16[64,1,16,2,1,512]{5,3,2,1,0,4:T(2,128)(2,1)} %get-tuple-element.479, bf16[64,1,16,2,1,512]{5,3,2,1,0,4:T(2,128)(2,1)S(1)} %get-tuple-element.480), kind=kLoop, calls=%fused_computation.1.clone.1 | loop fusion | flops 2097152 | bytes 8388608 | tf_op jit(solution)/shard_map/while/body/eval_jaxpr/stack | solution.py:115
  419.1 3.5 conditional.7
  423.2 3.5 conditional.6
  431.0 4.8 fusion.71
  438.7 10.4 %maximum_bitcast_fusion.7 = (bf16[64,1,16,2,1,512]{5,3,2,1,0,4:T(2,128)(2,1)S(1)}, bf16[64,1,16,2,1,512]{5,3,2,1,0,4:T(2,128)(2,1)}) fusion(bf16[64,16,1,1,512]{4,2,1,0,3:T(2,128)(2,1)S(1)} %add_convert_fusion.2, bf16[64,16,1,1,512]{4,2,1,0,3:T(2,128)(2,1)S(1)} %get-tuple-element.477, bf16[64,16,1,1,512]{4,2,1,0,3:T(2,128)(2,1)S(1)} %get-tuple-element.478), kind=kLoop, calls=%fused_computation.2.clone.1 | loop fusion | flops 8388608 | bytes 7340032 | tf_op jit(solution)/shard_map/while/body/eval_jaxpr/stack | solution.py:115
  449.0 7.2 %pad_maximum_fusion.2 = bf16[64,2,16,2,1,512]{5,3,2,1,0,4:T(2,128)(2,1)S(1)} fusion(bf16[64,1,16,2,1,512]{5,3,2,1,0,4:T(2,128)(2,1)} %get-tuple-element.479, bf16[64,1,16,2,1,512]{5,3,2,1,0,4:T(2,128)(2,1)S(1)} %get-tuple-element.480), kind=kLoop, calls=%fused_computation.1.clone.1 | loop fusion | flops 2097152 | bytes 8388608 | tf_op jit(solution)/shard_map/while/body/eval_jaxpr/stack | solution.py:115
  461.8 3.5 conditional.7
  465.9 3.5 conditional.6
  473.8 4.8 fusion.71
  481.4 10.4 %maximum_bitcast_fusion.7 = (bf16[64,1,16,2,1,512]{5,3,2,1,0,4:T(2,128)(2,1)S(1)}, bf16[64,1,16,2,1,512]{5,3,2,1,0,4:T(2,128)(2,1)}) fusion(bf16[64,16,1,1,512]{4,2,1,0,3:T(2,128)(2,1)S(1)} %add_convert_fusion.2, bf16[64,16,1,1,512]{4,2,1,0,3:T(2,128)(2,1)S(1)} %get-tuple-element.477, bf16[64,16,1,1,512]{4,2,1,0,3:T(2,128)(2,1)S(1)} %get-tuple-element.478), kind=kLoop, calls=%fused_computation.2.clone.1 | loop fusion | flops 8388608 | bytes 7340032 | tf_op jit(solution)/shard_map/while/body/eval_jaxpr/stack | solution.py:115
  491.7 7.2 %pad_maximum_fusion.2 = bf16[64,2,16,2,1,512]{5,3,2,1,0,4:T(2,128)(2,1)S(1)} fusion(bf16[64,1,16,2,1,512]{5,3,2,1,0,4:T(2,128)(2,1)} %get-tuple-element.479, bf16[64,1,16,2,1,512]{5,3,2,1,0,4:T(2,128)(2,1)S(1)} %get-tuple-element.480), kind=kLoop, calls=%fused_computation.1.clone.1 | loop fusion | flops 2097152 | bytes 8388608 | tf_op jit(solution)/shard_map/while/body/eval_jaxpr/stack | solution.py:115
  504.5 3.5 conditional.7
  508.6 3.5 conditional.6
  516.5 4.8 fusion.71
  524.1 10.4 %maximum_bitcast_fusion.7 = (bf16[64,1,16,2,1,512]{5,3,2,1,0,4:T(2,128)(2,1)S(1)}, bf16[64,1,16,2,1,512]{5,3,2,1,0,4:T(2,128)(2,1)}) fusion(bf16[64,16,1,1,512]{4,2,1,0,3:T(2,128)(2,1)S(1)} %add_convert_fusion.2, bf16[64,16,1,1,512]{4,2,1,0,3:T(2,128)(2,1)S(1)} %get-tuple-element.477, bf16[64,16,1,1,512]{4,2,1,0,3:T(2,128)(2,1)S(1)} %get-tuple-element.478), kind=kLoop, calls=%fused_computation.2.clone.1 | loop fusion | flops 8388608 | bytes 7340032 | tf_op jit(solution)/shard_map/while/body/eval_jaxpr/stack | solution.py:115
  534.4 7.2 %pad_maximum_fusion.2 = bf16[64,2,16,2,1,512]{5,3,2,1,0,4:T(2,128)(2,1)S(1)} fusion(bf16[64,1,16,2,1,512]{5,3,2,1,0,4:T(2,128)(2,1)} %get-tuple-element.479, bf16[64,1,16,2,1,512]{5,3,2,1,0,4:T(2,128)(2,1)S(1)} %get-tuple-element.480), kind=kLoop, calls=%fused_computation.1.clone.1 | loop fusion | flops 2097152 | bytes 8388608 | tf_op jit(solution)/shard_map/while/body/eval_jaxpr/stack | solution.py:115
  547.2 3.5 conditional.7
  551.3 3.5 conditional.6
  558.0 135.1 %reduce-scatter.2.cloned.1.call-done = f32[1,32,256]{2,1,0:T(8,128)} async-done(((f32[64,32,256]{2,1,0:T(8,128)}), f32[1,32,256]{2,1,0:T(8,128)}) %reduce-scatter.2.cloned.1.call-update) | async-done | bytes 32784 | tf_op jit(solution)/shard_map/reduce_scatter | solution.py:135
  (148 shorter events, 188.8 us)
Async XLA Ops:
  14.8 30.5 %all-to-all-start = ((f32[64,1,2048]{2,1,0:T(1,128)}), f32[64,1,2048]{2,1,0:T(1,128)S(1)}, u32[]{:S(2)}, u32[]{:S(2)}) async-start(f32[64,1,2048]{2,1,0:T(1,128)} %reshape.319), calls=%async_computation | async-start | bytes 1048576 | tf_op jit(solution)/shard_map/all_to_all | solution.py:39
  69.3 23.6 %all-to-all-start.1 = ((f32[64,1,2048]{2,1,0:T(1,128)}), f32[64,1,2048]{2,1,0:T(1,128)S(1)}, u32[]{:S(2)}, u32[]{:S(2)}) async-start(f32[64,1,2048]{2,1,0:T(1,128)} %reshape.323), calls=%async_computation.1 | async-start | bytes 1048576 | tf_op jit(solution)/shard_map/all_to_all | solution.py:56
  79.2 20.2 %copy-start.1 = (f32[512,8]{0,1:T(8,128)S(1)}, f32[512,8]{0,1:T(8,128)}, u32[]{:S(2)}) copy-start(f32[512,8]{0,1:T(8,128)} %param.12) | copy-start | bytes 49156
  92.9 40.1 %all-to-all-start.2 = ((f32[64,1,2048]{2,1,0:T(1,128)}), f32[64,1,2048]{2,1,0:T(1,128)}, u32[]{:S(2)}, u32[]{:S(2)}) async-start(f32[64,1,2048]{2,1,0:T(1,128)} %reshape.321), calls=%async_computation.2 | async-start | bytes 1048576 | tf_op jit(solution)/shard_map/all_to_all | solution.py:63
  99.4 115.5 %all-gather.2.cloned.1.call-start = ((), (), s32[]{:S(2)}) async-start(), calls=%async_computation.5 | async-start | bytes 1310720 | tf_op jit(solution)/shard_map/all_gather | solution.py:95
  192.3 500.8 %reduce-scatter.2.cloned.1.call-start = ((), (), s32[]{:S(2)}) async-start(), calls=%async_computation.6 | async-start | bytes 2129920 | tf_op jit(solution)/shard_map/reduce_scatter | solution.py:135
  192.3 7.6 %copy-start = (s32[256]{0:T(256)S(1)}, s32[256]{0:T(256)}, u32[]{:S(2)}) copy-start(s32[256]{0:T(256)} %param.14) | copy-start | bytes 3076
  199.9 17.8 %copy-start.2 = (s32[16]{0:T(128)S(1)}, s32[16]{0:T(128)}, u32[]{:S(2)}) copy-start(s32[16]{0:T(128)} %param.15) | copy-start | bytes 196
Sparse Core Ops, SparseCore 0:
  192.4 22.4 all-gather.1
  558.1 134.9 reduce-scatter.1
where the time goes:
time: 710 us; the launch traced here: 700 us
  other arithmetic  272 us (38%)
  waiting for transfers between devices  172 us (24%)
  local copies, waits for them, and re-layouts  116 us (16%)
  matrix products  66.3 us (9%)
  starting transfers between devices  26.1 us (4%)
  blocking collectives  22.1 us (3%)
  between operations  13.8 us (2%)
  loops' own time  11.2 us (2%)
    another operation x16, other arithmetic, one_span(): jnp.stack([real_rows, imag_rows], axis=1)  140 us
    reduce_scatter x1, waiting for transfers between devices, on_device(): lax.psum_scatter(partial_sums, 'freq', scatter_dimension=0, tiled=True)  135 us
    dot_general x16, matrix products, multiply(): lax.dot_general(lhs_rows, tmpl_cols, (((1,), (1,)), ((), ())), preferred_...  55 us
    neg x8, other arithmetic, one_span(): imag_rows = jnp.stack([imag_q, -real_q], axis=2)  38.4 us
    unnamed x17, local copies, waits for them, and re-layouts  36.5 us
    while x8, local copies, waits for them, and re-layouts  25.3 us
    add x8, other arithmetic, one_span(): return running + jnp.concatenate(outputs, axis=1)  23.8 us
    convert_element_type x8, other arithmetic, one_span(): imag_q = (data_real * lag_sin + data_imag * lag_cos).astype(jnp.bfloat16)  22.3 us
  transfers between devices with their start and end apart: 5, of which 4 were waited for; matrix products, arithmetic and copies ran while one was open for 8% of the time, Pallas kernels for 0%

commit v1 on v0

v1 whole, which is shorter than its diff:
```python
import math

import jax
import jax.numpy as jnp
from jax import lax
from jax.experimental import pallas as pl
from jax.experimental.pallas import tpu as pltpu
from jax.sharding import PartitionSpec as P

A = 512
B = 1024
LEN = 524288
NB = 512


two_pi = 2.0 * math.pi


def cos_sin_table(row_ids, col_ids, modulus):
    product = row_ids[:, None] * col_ids[None, :] % modulus
    phase_angle = product.astype(jnp.float32) * (two_pi / modulus)
    return (jnp.cos(phase_angle), jnp.sin(phase_angle))


def intersect_kernel(ph_ref, dat_ref, tm_ref, out_ref, lhs_ref):
    step = pl.program_id(0)
    seg_count = dat_ref.shape[2]
    lag_total = ph_ref.shape[2]
    rows = seg_count * lag_total
    chunk = 8

    @pl.when(step == 0)
    def _():
        out_ref[...] = jnp.zeros_like(out_ref)

    lag_cos = ph_ref[0, 0][None]
    lag_sin = ph_ref[0, 1][None]

    def build(i, carry):
        s0 = pl.multiple_of(i * chunk, chunk)
        data_real = dat_ref[0, 0, pl.ds(s0, chunk), :].astype(jnp.float32)[:, None, :]
        data_imag = dat_ref[0, 1, pl.ds(s0, chunk), :].astype(jnp.float32)[:, None, :]
        real_q = data_real * lag_cos - data_imag * lag_sin
        imag_q = data_real * lag_sin + data_imag * lag_cos
        r0 = pl.multiple_of(i * chunk * lag_total, chunk * lag_total)
        lhs_ref[pl.ds(r0, chunk * lag_total), :] = real_q.reshape(chunk * lag_total, -1).astype(jnp.bfloat16)
        lhs_ref[pl.ds(rows + r0, chunk * lag_total), :] = imag_q.reshape(chunk * lag_total, -1).astype(jnp.bfloat16)
        return carry

    lax.fori_loop(0, seg_count // chunk, build, 0)
    dims = (((1,), (1,)), ((), ()))
    lhs = lhs_ref[...]
    with_re = lax.dot_general(lhs, tm_ref[0, 0], dims, preferred_element_type=jnp.float32)
    with_im = lax.dot_general(lhs, tm_ref[0, 1], dims, preferred_element_type=jnp.float32)
    real_sum = with_re[:rows] + with_im[rows:]
    imag_sum = with_re[rows:] - with_im[:rows]
    width = real_sum.shape[1]
    out_ref[:, 0:lag_total, :] += real_sum.reshape(seg_count, lag_total, width)
    out_ref[:, lag_total:, :] += imag_sum.reshape(seg_count, lag_total, width)


def intersect(seg_piece, templates, cutoffs, lags, first_block):
    seg_count, _, blocks_here, width = seg_piece.shape
    tmpl_local = templates.shape[0]
    lag_total = lags.shape[0]
    block_ids = first_block + jnp.arange(blocks_here, dtype=jnp.int32)
    position = jnp.arange(width, dtype=jnp.int32)
    phase_int = (A * (lags[:, None] * block_ids[None, :] % B))[:, :, None] + (
        lags[:, None] * position[None, :] % LEN
    )[:, None, :]
    phase_angle = (phase_int % LEN).astype(jnp.float32) * (two_pi / LEN)
    phases = jnp.stack([jnp.cos(phase_angle), jnp.sin(phase_angle)], axis=0).transpose(2, 0, 1, 3)
    keep = block_ids[None, None, :, None] < cutoffs[:, None, None, None]
    masked = jnp.where(keep, templates, jnp.zeros_like(templates)).transpose(2, 1, 0, 3)
    data = seg_piece.transpose(2, 1, 0, 3)
    rows = seg_count * lag_total
    flops = 2 * 2 * (2 * rows) * width * tmpl_local * blocks_here
    moved = masked.size * 2 + data.size * 2 + phases.size * 4 + seg_count * 2 * lag_total * tmpl_local * 4
    return pl.pallas_call(
        intersect_kernel,
        out_shape=jax.ShapeDtypeStruct((seg_count, 2 * lag_total, tmpl_local), jnp.float32),
        grid=(blocks_here,),
        in_specs=[
            pl.BlockSpec((1, 2, lag_total, width), lambda j: (j, 0, 0, 0)),
            pl.BlockSpec((1, 2, seg_count, width), lambda j: (j, 0, 0, 0)),
            pl.BlockSpec((1, 2, tmpl_local, width), lambda j: (j, 0, 0, 0)),
        ],
        out_specs=pl.BlockSpec((seg_count, 2 * lag_total, tmpl_local), lambda j: (0, 0, 0)),
        scratch_shapes=[pltpu.VMEM((2 * rows, width), jnp.bfloat16)],
        compiler_params=pltpu.CompilerParams(dimension_semantics=("arbitrary",)),
        cost_estimate=pl.CostEstimate(flops=flops, transcendentals=0, bytes_accessed=moved),
    )(phases, data, masked)


def on_device(strain, psd, templates, cutoffs, lags):
    freq_count = lax.axis_size("freq")
    freq_index = lax.axis_index("freq")
    seg_local = strain.shape[0]
    step_time = B // freq_count
    highest = lax.Precision.HIGHEST
    first_cos, first_sin = cos_sin_table(
        jnp.arange(A, dtype=jnp.int32), jnp.arange(A, dtype=jnp.int32), A
    )
    first_table = jnp.concatenate([first_cos, -first_sin], axis=0)
    time_ids = freq_index * step_time + jnp.arange(step_time, dtype=jnp.int32)
    twist_cos, twist_sin = cos_sin_table(jnp.arange(A, dtype=jnp.int32), time_ids, LEN)
    slab_blocks = strain.reshape(seg_local, A // freq_count, B)
    both_parts = jnp.einsum(
        "kn,snb->skb",
        first_table,
        lax.all_to_all(slab_blocks, "freq", split_axis=2, concat_axis=1, tiled=True),
        precision=highest,
    )
    half_rows = first_table.shape[0] // 2
    real_part = both_parts[:, :half_rows]
    imag_part = both_parts[:, half_rows:]
    second_cos, second_sin = cos_sin_table(
        jnp.arange(B, dtype=jnp.int32), jnp.arange(NB, dtype=jnp.int32), B
    )
    rotation = jnp.concatenate(
        [
            jnp.concatenate([second_cos, -second_sin], axis=1),
            jnp.concatenate([second_sin, second_cos], axis=1),
        ],
        axis=0,
    )
    amplitude = jnp.sqrt(LEN * psd)
    real_in = lax.all_to_all(
        real_part * twist_cos + imag_part * twist_sin,
        "freq",
        split_axis=1,
        concat_axis=2,
        tiled=True,
    )
    imag_in = lax.all_to_all(
        imag_part * twist_cos - real_part * twist_sin,
        "freq",
        split_axis=1,
        concat_axis=2,
        tiled=True,
    )
    joined = jnp.concatenate([real_in, imag_in], axis=2)
    both_out = jnp.einsum("spc,cm->smp", joined, rotation, precision=highest)
    both_out = both_out.reshape(joined.shape[0], 2, NB, joined.shape[1])
    whitened = (both_out / amplitude).astype(jnp.bfloat16)
    local_data = lax.all_to_all(whitened, "freq", split_axis=2, concat_axis=3, tiled=True)
    first_block = freq_index * (NB // freq_count)
    seg_piece = lax.all_gather(local_data, "tmpl", axis=0, tiled=True)
    partial_sums = intersect(seg_piece, templates, cutoffs, lags, first_block)
    return lax.psum_scatter(partial_sums, "freq", scatter_dimension=0, tiled=True)


def solution(mesh):
    placed = (P("tmpl", "freq"), P(None, "freq"), P("tmpl", None, "freq", None), P("tmpl"), P())
    return jax.shard_map(
        on_device, mesh=mesh, in_specs=placed, out_specs=P("freq", None, "tmpl"), check_vma=False
    )
```

time: 710 us -> 387 us (0.55)
  other arithmetic: 272 us -> 40.9 us
  matrix products: 66.3 us -> 11.3 us
  local copies, waits for them, and re-layouts: 116 us -> 75.8 us
  blocking collectives: 22.1 us -> 0 us
  Pallas kernels: 0 us -> 18.7 us
  loops' own time: 11.2 us -> 0 us
  starting transfers between devices: 26.1 us -> 36.8 us
  waiting for transfers between devices: 172 us -> 182 us
    another operation x16 -> x0, other arithmetic: 140 us -> none  [one_span(): jnp.stack([real_rows, imag_rows], axis=1)]
    dot_general x16 -> x0, matrix products: 55 us -> none  [multiply(): lax.dot_general(lhs_rows, tmpl_cols, (((1,), (1,)), ((), ())), preferred_...]
    neg x8 -> x0, other arithmetic: 38.4 us -> none  [one_span(): imag_rows = jnp.stack([imag_q, -real_q], axis=2)]
    convert_element_type x24 -> x0, other arithmetic: 29.8 us -> none  [the longest x8 22.3 us: one_span(): imag_q = (data_real * lag_sin + data_imag * lag_cos).astype(jnp.bfloat16)]
    while x8 -> x0, local copies, waits for them, and re-layouts: 25.3 us -> none
    add x8 -> x1, other arithmetic: 23.8 us -> 0.01 us  [intersect(): block_ids = first_block + jnp.arange(blocks_here, dtype=jnp.int32)]
    all_to_all x1 -> x0, blocking collectives: 22.1 us -> none  [on_device(): lax.all_to_all(whitened, 'freq', split_axis=2, concat_axis=3, tiled=True)]
    pallas_call x0 -> x1, Pallas kernels: none -> 18.7 us  [intersect(): pl.pallas_call(intersect_kernel, out_shape=jax.ShapeDtypeStruct((seg_coun...]
  transfers between devices with their start and end apart: 5 -> 6, of which waited for: 4 -> 5; matrix products, arithmetic and copies ran while one was open for 8% -> 15% of each run, Pallas kernels for 0% -> 0%
where the time goes in v1:
time: 387 us; the launch traced here: 379 us
  waiting for transfers between devices  182 us (47%)
  local copies, waits for them, and re-layouts  75.8 us (20%)
  other arithmetic  40.9 us (11%)
  starting transfers between devices  36.8 us (10%)
  Pallas kernels  18.7 us (5%)
  between operations  13.9 us (4%)
  matrix products  11.3 us (3%)
    reduce_scatter x1, waiting for transfers between devices, on_device(): lax.psum_scatter(partial_sums, 'freq', scatter_dimension=0, tiled=True)  137 us
    unnamed x15, local copies, waits for them, and re-layouts  27.1 us
    pallas_call x1, Pallas kernels, intersect(): pl.pallas_call(intersect_kernel, out_shape=jax.ShapeDtypeStruct((seg_coun...  18.7 us
    all_to_all x1, starting transfers between devices, on_device(): lax.all_to_all(slab_blocks, 'freq', split_axis=2, concat_axis=1, tiled=True)  13.6 us
    all_to_all x1, waiting for transfers between devices, on_device(): lax.all_to_all(slab_blocks, 'freq', split_axis=2, concat_axis=1, tiled=True)  12.8 us
    all_to_all x1, waiting for transfers between devices, on_device(): lax.all_to_all(whitened, 'freq', split_axis=2, concat_axis=3, tiled=True)  11.9 us
    all_to_all x2, local copies, waits for them, and re-layouts, on_device(): lax.all_to_all(imag_part * twist_cos - real_part * twist_sin, 'freq', spl...  11.3 us
    all_to_all x2, local copies, waits for them, and re-layouts, on_device(): lax.all_to_all(real_part * twist_cos + imag_part * twist_sin, 'freq', spl...  11.3 us
  transfers between devices with their start and end apart: 6, of which 5 were waited for; matrix products, arithmetic and copies ran while one was open for 15% of the time, Pallas kernels for 0%

profile of v1, /device:TPU:1, one launch (start us, length us, event | category | flops | bytes accessed | tf_op | source)
XLA Modules:
  0.0 379.0 jit_solution(5599903289922193966)
XLA Ops:
  6.5 1.3 copy.119
  7.9 2.7 copy.92
  10.6 4.2 %reshape.225 = f32[64,1,2048]{2,1,0:T(1,128)} reshape(f32[1024,8,16]{2,1,0:T(8,128)} %bitcast.55) | data formatting | bytes 1048576
  14.8 13.6 %all-to-all-start = ((f32[64,1,2048]{2,1,0:T(1,128)}), f32[64,1,2048]{2,1,0:T(1,128)S(1)}, u32[]{:S(2)}, u32[]{:S(2)}) async-start(f32[64,1,2048]{2,1,0:T(1,128)} %reshape.225), calls=%async_computation | async-start | bytes 1048576 | tf_op jit(solution)/shard_map/all_to_all | solution.py:111
  28.5 4.1 %sine_negate_fusion = (f32[512,512]{1,0:T(8,128)S(1)}, f32[512,512]{1,0:T(8,128)S(1)}) fusion(), kind=kLoop, calls=%fused_computation.34 | loop fusion | flops 3932160 | bytes 2097152 | tf_op jit(solution)/shard_map/neg | solution.py:104
  32.6 0.2 fusion.48
  32.8 12.8 %all-to-all-done = f32[64,1,2048]{2,1,0:T(1,128)S(1)} async-done(((f32[64,1,2048]{2,1,0:T(1,128)}), f32[64,1,2048]{2,1,0:T(1,128)S(1)}, u32[]{:S(2)}, u32[]{:S(2)}) %all-to-all-start) | async-done | bytes 524320 | tf_op jit(solution)/shard_map/all_to_all | solution.py:111
  45.7 0.5 broadcast.322
  46.2 1.9 reduce
  48.1 2.8 reshape.226
  50.8 6.0 %copy.94 = f32[16,64,8,16]{3,2,1,0:T(8,128)} copy(f32[16,64,8,16]{0,2,3,1:T(8,128)} %bitcast.58) | data formatting | bytes 1048576 | tf_op jit(solution)/shard_map/all_to_all | solution.py:111
  56.8 2.8 copy.95
  59.6 2.0 fusion.11
  61.6 0.2 multiply_add_fusion
  61.8 3.6 copy.96
  65.4 4.2 %reshape.229 = f32[64,1,2048]{2,1,0:T(1,128)} reshape(f32[512,16,16]{2,1,0:T(8,128)} %bitcast.56) | data formatting | bytes 1048576
  69.6 6.3 %all-to-all-start.1 = ((f32[64,1,2048]{2,1,0:T(1,128)}), f32[64,1,2048]{2,1,0:T(1,128)S(1)}, u32[]{:S(2)}, u32[]{:S(2)}) async-start(f32[64,1,2048]{2,1,0:T(1,128)} %reshape.229), calls=%async_computation.1 | async-start | bytes 1048576 | tf_op jit(solution)/shard_map/all_to_all | solution.py:128
  75.9 3.6 copy.99
  79.6 0.0 copy-start
  79.6 4.2 %reshape.227 = f32[64,1,2048]{2,1,0:T(1,128)} reshape(f32[512,16,16]{2,1,0:T(8,128)} %bitcast.57) | data formatting | bytes 1048576
  83.8 9.5 %all-to-all-done.1 = f32[64,1,2048]{2,1,0:T(1,128)S(1)} async-done(((f32[64,1,2048]{2,1,0:T(1,128)}), f32[64,1,2048]{2,1,0:T(1,128)S(1)}, u32[]{:S(2)}, u32[]{:S(2)}) %all-to-all-start.1) | async-done | bytes 524320 | tf_op jit(solution)/shard_map/all_to_all | solution.py:128
  93.3 6.5 %all-to-all-start.2 = ((f32[64,1,2048]{2,1,0:T(1,128)}), f32[64,1,2048]{2,1,0:T(1,128)}, u32[]{:S(2)}, u32[]{:S(2)}) async-start(f32[64,1,2048]{2,1,0:T(1,128)} %reshape.227), calls=%async_computation.2 | async-start | bytes 1048576 | tf_op jit(solution)/shard_map/all_to_all | solution.py:135
  99.7 0.0 copy-done
  99.8 9.0 %fusion.27 = (f32[1024,512]{1,0:T(8,128)S(1)}, f32[1024,512]{1,0:T(8,128)}) fusion(), kind=kLoop, calls=%fused_computation.37 | loop fusion | flops 7340032 | bytes 4194304 | tf_op jit(solution)/shard_map/sin | solution.py:22
  108.8 8.6 %fusion.30 = f32[1024,512]{1,0:T(8,128)} fusion(), kind=kLoop, calls=%fused_computation.40 | loop fusion | flops 7864320 | bytes 2097152 | tf_op jit(solution)/shard_map/neg | solution.py:122
  117.3 1.9 reduce.2
  119.2 2.8 reshape.230
  122.0 6.6 %copy.113 = f32[16,8,64,16]{3,2,0,1:T(8,128)} copy(f32[16,8,64,16]{3,0,1,2:T(8,128)} %bitcast.60) | data formatting | bytes 1048576 | tf_op jit(solution)/shard_map/all_to_all | solution.py:128
  128.6 4.7 %reshape.223 = f32[16,8,1024]{2,0,1:T(8,128)S(1)} reshape(f32[16,8,64,16]{3,2,0,1:T(8,128)} %copy.113) | data formatting | bytes 1048576 | tf_op jit(solution)/shard_map/all_to_all | solution.py:128
  133.3 0.0 all-to-all-done.2
  133.3 2.9 reduce.1
  136.3 3.0 reshape.228
  139.2 6.6 %copy.115 = f32[16,8,64,16]{3,2,0,1:T(8,128)} copy(f32[16,8,64,16]{3,0,1,2:T(8,128)} %bitcast.61) | data formatting | bytes 1048576 | tf_op jit(solution)/shard_map/all_to_all | solution.py:135
  145.8 4.7 %reshape.224 = f32[16,8,1024]{2,0,1:T(8,128)S(1)} reshape(f32[16,8,64,16]{3,2,0,1:T(8,128)} %copy.115) | data formatting | bytes 1048576 | tf_op jit(solution)/shard_map/all_to_all | solution.py:135
  150.5 9.2 %fusion.18 = f32[16,1024,8]{1,0,2:T(8,128)S(1)} fusion(f32[1024,512]{1,0:T(8,128)} %get-tuple-element.14, f32[1024,512]{1,0:T(8,128)S(1)} %get-tuple-element.13, f32[1024,512]{1,0:T(8,128)} %fusion.30, f32[16,8,1024]{2,0,1:T(8,128)S(1)} %reshape.224, f32[16,8,1024]{2,0,1:T(8,128)S(1)} %reshape.223), kind=kOutput, calls=%fused_computation.27 | convolution fusion | flops 3227779072 | bytes 7864320 | tf_op jit(solution)/shard_map/spc,cm->smp/dot_general | solution.py:143
  159.8 0.3 copy.104
  160.1 2.1 copy.105
  162.2 3.0 reshape.231
  165.2 10.3 %all-to-all-start.3 = ((bf16[64,2,1024]{2,1,0:T(2,128)(2,1)}), bf16[64,2,1024]{2,1,0:T(2,128)(2,1)S(1)}, u32[]{:S(2)}, u32[]{:S(2)}) async-start(bf16[64,2,1024]{2,1,0:T(2,128)(2,1)} %reshape.231), calls=%async_computation.3 | async-start | bytes 524288 | tf_op jit(solution)/shard_map/all_to_all | solution.py:146
  175.5 0.0 all-gather.2.cloned.1.call-start
  175.5 11.9 %all-to-all-done.3 = bf16[64,2,1024]{2,1,0:T(2,128)(2,1)S(1)} async-done(((bf16[64,2,1024]{2,1,0:T(2,128)(2,1)}), bf16[64,2,1024]{2,1,0:T(2,128)(2,1)S(1)}, u32[]{:S(2)}, u32[]{:S(2)}) %all-to-all-start.3) | async-done | bytes 262176 | tf_op jit(solution)/shard_map/all_to_all | solution.py:146
  187.5 1.7 reshape.232
  189.2 1.9 copy.124
  191.0 0.0 copy-start.1
  191.0 0.0 copy-start.2
  191.0 2.5 copy.108
  193.6 0.0 all-gather.2.cloned.1.call-update
  193.6 0.0 reduce-scatter.2.cloned.1.call-start
  193.7 0.0 copy-done.1
  193.7 0.1 fusion.49
  193.8 0.1 add_select_fusion.5
  193.9 1.1 fusion.36
  195.0 0.8 maximum_bitcast_fusion.4.ph_ref
  195.8 0.0 copy-done.2
  195.8 0.1 broadcast_compare_fusion
  195.9 9.9 %fusion.7.tm_ref = bf16[8,2,256,512]{3,2,1,0:T(8,128)(2,1)} fusion(bf16[256,2,8,512]{3,2,1,0:T(8,128)(2,1)} %param.7, pred[256,8]{0,1:T(8,128)(4,1)S(1)} %broadcast_compare_fusion), kind=kLoop, calls=%fused_computation.9 | loop fusion | flops 2097152 | bytes 8390656 | tf_op jit(solution)/shard_map/transpose | solution.py:74
  205.8 10.4 %all-gather.2.cloned.1.call-done = bf16[64,2,8,512]{3,0,1,2:T(8,128)(2,1)} async-done(((bf16[16,2,8,512]{3,0,1,2:T(8,128)(2,1)}), bf16[64,2,8,512]{3,0,1,2:T(8,128)(2,1)}) %all-gather.2.cloned.1.call-update) | async-done | bytes 1048592 | tf_op jit(solution)/shard_map/all_gather | solution.py:148
  216.3 18.7 %shard_map.55 = f32[64,32,256]{2,1,0:T(8,128)} custom-call(f32[8,2,16,512]{3,2,1,0:T(8,128)} %maximum_bitcast_fusion.4.ph_ref, bf16[8,2,64,512]{3,2,1,0:T(8,128)(2,1)} %bitcast.70, bf16[8,2,256,512]{3,2,1,0:T(8,128)(2,1)} %fusion.7.tm_ref), custom_call_target="tpu_custom_call" | custom-call | flops 8589934592 | bytes 7864320 | tf_op jit(solution)/shard_map/pallas_call | solution.py:79
  234.9 0.0 reduce-scatter.2.cloned.1.call-update
  234.9 136.9 %reduce-scatter.2.cloned.1.call-done = f32[1,32,256]{2,1,0:T(8,128)} async-done(((f32[64,32,256]{2,1,0:T(8,128)}), f32[1,32,256]{2,1,0:T(8,128)}) %reduce-scatter.2.cloned.1.call-update) | async-done | bytes 32784 | tf_op jit(solution)/shard_map/reduce_scatter | solution.py:150
  (4 shorter events, 0.1 us)
Async XLA Ops:
  14.8 30.8 %all-to-all-start = ((f32[64,1,2048]{2,1,0:T(1,128)}), f32[64,1,2048]{2,1,0:T(1,128)S(1)}, u32[]{:S(2)}, u32[]{:S(2)}) async-start(f32[64,1,2048]{2,1,0:T(1,128)} %reshape.225), calls=%async_computation | async-start | bytes 1048576 | tf_op jit(solution)/shard_map/all_to_all | solution.py:111
  69.6 23.6 %all-to-all-start.1 = ((f32[64,1,2048]{2,1,0:T(1,128)}), f32[64,1,2048]{2,1,0:T(1,128)S(1)}, u32[]{:S(2)}, u32[]{:S(2)}) async-start(f32[64,1,2048]{2,1,0:T(1,128)} %reshape.229), calls=%async_computation.1 | async-start | bytes 1048576 | tf_op jit(solution)/shard_map/all_to_all | solution.py:128
  79.6 20.2 %copy-start = (f32[512,8]{0,1:T(8,128)S(1)}, f32[512,8]{0,1:T(8,128)}, u32[]{:S(2)}) copy-start(f32[512,8]{0,1:T(8,128)} %param.6) | copy-start | bytes 49156
  93.3 40.1 %all-to-all-start.2 = ((f32[64,1,2048]{2,1,0:T(1,128)}), f32[64,1,2048]{2,1,0:T(1,128)}, u32[]{:S(2)}, u32[]{:S(2)}) async-start(f32[64,1,2048]{2,1,0:T(1,128)} %reshape.227), calls=%async_computation.2 | async-start | bytes 1048576 | tf_op jit(solution)/shard_map/all_to_all | solution.py:135
  165.2 22.3 %all-to-all-start.3 = ((bf16[64,2,1024]{2,1,0:T(2,128)(2,1)}), bf16[64,2,1024]{2,1,0:T(2,128)(2,1)S(1)}, u32[]{:S(2)}, u32[]{:S(2)}) async-start(bf16[64,2,1024]{2,1,0:T(2,128)(2,1)} %reshape.231), calls=%async_computation.3 | async-start | bytes 524288 | tf_op jit(solution)/shard_map/all_to_all | solution.py:146
  175.5 40.8 %all-gather.2.cloned.1.call-start = ((), (), s32[]{:S(2)}) async-start(), calls=%async_computation.5 | async-start | bytes 1310720 | tf_op jit(solution)/shard_map/all_gather | solution.py:148
  191.0 2.6 copy-start.1
  191.0 4.8 %copy-start.2 = (s32[256]{0:T(256)S(1)}, s32[256]{0:T(256)}, u32[]{:S(2)}) copy-start(s32[256]{0:T(256)} %param.8) | copy-start | bytes 3076
  193.6 178.3 %reduce-scatter.2.cloned.1.call-start = ((), (), s32[]{:S(2)}) async-start(), calls=%async_computation.6 | async-start | bytes 2129920 | tf_op jit(solution)/shard_map/reduce_scatter | solution.py:150
Sparse Core Ops, SparseCore 0:
  193.7 22.4 all-gather.1
  235.1 136.7 reduce-scatter.1

commit v2 on v1

--- a/solution.py
+++ b/solution.py
@@ -5,7 +5,7 @@
 from jax import lax
 from jax.experimental import pallas as pl
 from jax.experimental.pallas import tpu as pltpu
-from jax.sharding import PartitionSpec as P
+from jax.sharding import Mesh, PartitionSpec as P
 
 A = 512
 B = 1024
@@ -14,6 +14,7 @@
 
 
 two_pi = 2.0 * math.pi
+FREQ = ("fx", "fz", "fc")
 
 
 def cos_sin_table(row_ids, col_ids, modulus):
@@ -93,8 +94,8 @@
 
 
 def on_device(strain, psd, templates, cutoffs, lags):
-    freq_count = lax.axis_size("freq")
-    freq_index = lax.axis_index("freq")
+    freq_count = lax.axis_size(FREQ)
+    freq_index = lax.axis_index(FREQ)
     seg_local = strain.shape[0]
     step_time = B // freq_count
     highest = lax.Precision.HIGHEST
@@ -108,7 +109,7 @@
     both_parts = jnp.einsum(
         "kn,snb->skb",
         first_table,
-        lax.all_to_all(slab_blocks, "freq", split_axis=2, concat_axis=1, tiled=True),
+        lax.all_to_all(slab_blocks, FREQ, split_axis=2, concat_axis=1, tiled=True),
         precision=highest,
     )
     half_rows = first_table.shape[0] // 2
@@ -127,14 +128,14 @@
     amplitude = jnp.sqrt(LEN * psd)
     real_in = lax.all_to_all(
         real_part * twist_cos + imag_part * twist_sin,
-        "freq",
+        FREQ,
         split_axis=1,
         concat_axis=2,
         tiled=True,
     )
     imag_in = lax.all_to_all(
         imag_part * twist_cos - real_part * twist_sin,
-        "freq",
+        FREQ,
         split_axis=1,
         concat_axis=2,
         tiled=True,
@@ -143,15 +144,24 @@
     both_out = jnp.einsum("spc,cm->smp", joined, rotation, precision=highest)
     both_out = both_out.reshape(joined.shape[0], 2, NB, joined.shape[1])
     whitened = (both_out / amplitude).astype(jnp.bfloat16)
-    local_data = lax.all_to_all(whitened, "freq", split_axis=2, concat_axis=3, tiled=True)
+    local_data = lax.all_to_all(whitened, FREQ, split_axis=2, concat_axis=3, tiled=True)
     first_block = freq_index * (NB // freq_count)
     seg_piece = lax.all_gather(local_data, "tmpl", axis=0, tiled=True)
-    partial_sums = intersect(seg_piece, templates, cutoffs, lags, first_block)
-    return lax.psum_scatter(partial_sums, "freq", scatter_dimension=0, tiled=True)
+    x_size, z_size, c_size = (lax.axis_size(name) for name in FREQ)
+    seg_order = seg_piece.reshape((x_size, z_size, c_size) + seg_piece.shape[1:])
+    seg_order = seg_order.transpose(2, 1, 0, 3, 4, 5).reshape(seg_piece.shape)
+    partial_sums = intersect(seg_order, templates, cutoffs, lags, first_block)
+    for name in ("fc", "fz", "fx"):
+        partial_sums = lax.psum_scatter(partial_sums, name, scatter_dimension=0, tiled=True)
+    return partial_sums
 
 
 def solution(mesh):
-    placed = (P("tmpl", "freq"), P(None, "freq"), P("tmpl", None, "freq", None), P("tmpl"), P())
+    tmpl_size, freq_size = mesh.devices.shape
+    split = Mesh(
+        mesh.devices.reshape(tmpl_size, 4, freq_size // 8, 2), ("tmpl",) + FREQ
+    )
+    placed = (P("tmpl", FREQ), P(None, FREQ), P("tmpl", None, FREQ, None), P("tmpl"), P())
     return jax.shard_map(
-        on_device, mesh=mesh, in_specs=placed, out_specs=P("freq", None, "tmpl"), check_vma=False
+        on_device, mesh=split, in_specs=placed, out_specs=P(FREQ, None, "tmpl"), check_vma=False
     )

time: 387 us -> 331 us (0.86)
  waiting for transfers between devices: 182 us -> 126 us
    reduce_scatter x1 -> x3, waiting for transfers between devices: 137 us -> 80.9 us  [on_device(): lax.psum_scatter(partial_sums, name, scatter_dimension=0, tiled=True)]
  transfers between devices with their start and end apart: 6 -> 8, of which waited for: 5 -> 7; matrix products, arithmetic and copies ran while one was open for 15% -> 18% of each run, Pallas kernels for 0% -> 0%
where the time goes in v2:
time: 331 us; the launch traced here: 326 us
  waiting for transfers between devices  126 us (38%)
  local copies, waits for them, and re-layouts  79.1 us (24%)
  other arithmetic  40.9 us (12%)
  starting transfers between devices  36.9 us (11%)
  Pallas kernels  18.7 us (6%)
  between operations  13.8 us (4%)
  matrix products  11.3 us (3%)
    reduce_scatter x3, waiting for transfers between devices, on_device(): lax.psum_scatter(partial_sums, name, scatter_dimension=0, tiled=True)  80.9 us
    unnamed x15, local copies, waits for them, and re-layouts  27.1 us
    pallas_call x1, Pallas kernels, intersect(): pl.pallas_call(intersect_kernel, out_shape=jax.ShapeDtypeStruct((seg_coun...  18.7 us
    all_to_all x1, starting transfers between devices, on_device(): lax.all_to_all(slab_blocks, FREQ, split_axis=2, concat_axis=1, tiled=True)  13.6 us
    all_to_all x1, waiting for transfers between devices, on_device(): lax.all_to_all(slab_blocks, FREQ, split_axis=2, concat_axis=1, tiled=True)  12.8 us
    all_to_all x1, waiting for transfers between devices, on_device(): lax.all_to_all(whitened, FREQ, split_axis=2, concat_axis=3, tiled=True)  11.9 us
    all_to_all x2, local copies, waits for them, and re-layouts, on_device(): lax.all_to_all(imag_part * twist_cos - real_part * twist_sin, FREQ, split...  11.3 us
    all_to_all x2, local copies, waits for them, and re-layouts, on_device(): lax.all_to_all(real_part * twist_cos + imag_part * twist_sin, FREQ, split...  11.3 us
  transfers between devices with their start and end apart: 8, of which 7 were waited for; matrix products, arithmetic and copies ran while one was open for 18% of the time, Pallas kernels for 0%

profile of v2, /device:TPU:1, one launch (start us, length us, event | category | flops | bytes accessed | tf_op | source)
XLA Modules:
  0.0 326.2 jit_solution(13912406685278721780)
XLA Ops:
  6.5 1.3 copy.125
  7.9 2.7 copy.97
  10.6 4.2 %reshape.233 = f32[64,1,2048]{2,1,0:T(1,128)} reshape(f32[1024,8,16]{2,1,0:T(8,128)} %bitcast.60) | data formatting | bytes 1048576
  14.8 13.6 %all-to-all-start = ((f32[64,1,2048]{2,1,0:T(1,128)}), f32[64,1,2048]{2,1,0:T(1,128)S(1)}, u32[]{:S(2)}, u32[]{:S(2)}) async-start(f32[64,1,2048]{2,1,0:T(1,128)} %reshape.233), calls=%async_computation | async-start | bytes 1048576 | tf_op jit(solution)/shard_map/all_to_all | solution.py:112
  28.5 4.1 %sine_negate_fusion = (f32[512,512]{1,0:T(8,128)S(1)}, f32[512,512]{1,0:T(8,128)S(1)}) fusion(), kind=kLoop, calls=%fused_computation.34 | loop fusion | flops 3932160 | bytes 2097152 | tf_op jit(solution)/shard_map/neg | solution.py:105
  32.6 0.2 fusion.48
  32.8 12.8 %all-to-all-done = f32[64,1,2048]{2,1,0:T(1,128)S(1)} async-done(((f32[64,1,2048]{2,1,0:T(1,128)}), f32[64,1,2048]{2,1,0:T(1,128)S(1)}, u32[]{:S(2)}, u32[]{:S(2)}) %all-to-all-start) | async-done | bytes 524320 | tf_op jit(solution)/shard_map/all_to_all | solution.py:112
  45.7 0.5 broadcast.322
  46.2 1.9 reduce
  48.1 2.8 reshape.234
  50.8 6.0 %copy.99 = f32[16,64,8,16]{3,2,1,0:T(8,128)} copy(f32[16,64,8,16]{0,2,3,1:T(8,128)} %bitcast.63) | data formatting | bytes 1048576 | tf_op jit(solution)/shard_map/all_to_all | solution.py:112
  56.8 2.8 copy.100
  59.6 2.0 fusion.11
  61.6 0.2 multiply_add_fusion
  61.8 3.6 %copy.101 = f32[16,512,16]{2,0,1:T(8,128)} copy(f32[16,512,16]{1,2,0:T(8,128)S(1)} %get-tuple-element.5) | data formatting | bytes 1048576 | tf_op jit(solution)/shard_map/add | solution.py:130
  65.4 4.2 %reshape.237 = f32[64,1,2048]{2,1,0:T(1,128)} reshape(f32[512,16,16]{2,1,0:T(8,128)} %bitcast.61) | data formatting | bytes 1048576
  69.6 6.3 %all-to-all-start.1 = ((f32[64,1,2048]{2,1,0:T(1,128)}), f32[64,1,2048]{2,1,0:T(1,128)S(1)}, u32[]{:S(2)}, u32[]{:S(2)}) async-start(f32[64,1,2048]{2,1,0:T(1,128)} %reshape.237), calls=%async_computation.1 | async-start | bytes 1048576 | tf_op jit(solution)/shard_map/all_to_all | solution.py:129
  75.9 3.6 %copy.104 = f32[16,512,16]{2,0,1:T(8,128)} copy(f32[16,512,16]{1,2,0:T(8,128)S(1)} %get-tuple-element.6) | data formatting | bytes 1048576 | tf_op jit(solution)/shard_map/sub | solution.py:137
  79.6 4.2 %reshape.235 = f32[64,1,2048]{2,1,0:T(1,128)} reshape(f32[512,16,16]{2,1,0:T(8,128)} %bitcast.62) | data formatting | bytes 1048576
  83.8 9.5 %all-to-all-done.1 = f32[64,1,2048]{2,1,0:T(1,128)S(1)} async-done(((f32[64,1,2048]{2,1,0:T(1,128)}), f32[64,1,2048]{2,1,0:T(1,128)S(1)}, u32[]{:S(2)}, u32[]{:S(2)}) %all-to-all-start.1) | async-done | bytes 524320 | tf_op jit(solution)/shard_map/all_to_all | solution.py:129
  93.3 6.5 %all-to-all-start.2 = ((f32[64,1,2048]{2,1,0:T(1,128)}), f32[64,1,2048]{2,1,0:T(1,128)}, u32[]{:S(2)}, u32[]{:S(2)}) async-start(f32[64,1,2048]{2,1,0:T(1,128)} %reshape.235), calls=%async_computation.2 | async-start | bytes 1048576 | tf_op jit(solution)/shard_map/all_to_all | solution.py:136
  99.7 0.0 copy-done
  99.8 9.0 %fusion.27 = (f32[1024,512]{1,0:T(8,128)S(1)}, f32[1024,512]{1,0:T(8,128)}) fusion(), kind=kLoop, calls=%fused_computation.37 | loop fusion | flops 7340032 | bytes 4194304 | tf_op jit(solution)/shard_map/sin | solution.py:23
  108.8 8.6 %fusion.30 = f32[1024,512]{1,0:T(8,128)} fusion(), kind=kLoop, calls=%fused_computation.40 | loop fusion | flops 7864320 | bytes 2097152 | tf_op jit(solution)/shard_map/neg | solution.py:123
  117.4 1.9 reduce.2
  119.2 2.8 reshape.238
  122.0 6.6 %copy.119 = f32[16,8,64,16]{3,2,0,1:T(8,128)} copy(f32[16,8,64,16]{3,0,1,2:T(8,128)} %bitcast.65) | data formatting | bytes 1048576 | tf_op jit(solution)/shard_map/all_to_all | solution.py:129
  128.6 4.7 %reshape.231 = f32[16,8,1024]{2,0,1:T(8,128)S(1)} reshape(f32[16,8,64,16]{3,2,0,1:T(8,128)} %copy.119) | data formatting | bytes 1048576 | tf_op jit(solution)/shard_map/all_to_all | solution.py:129
  133.3 0.0 all-to-all-done.2
  133.3 2.9 reduce.1
  136.3 3.0 reshape.236
  139.2 6.6 %copy.121 = f32[16,8,64,16]{3,2,0,1:T(8,128)} copy(f32[16,8,64,16]{3,0,1,2:T(8,128)} %bitcast.66) | data formatting | bytes 1048576 | tf_op jit(solution)/shard_map/all_to_all | solution.py:136
  145.8 4.7 %reshape.232 = f32[16,8,1024]{2,0,1:T(8,128)S(1)} reshape(f32[16,8,64,16]{3,2,0,1:T(8,128)} %copy.121) | data formatting | bytes 1048576 | tf_op jit(solution)/shard_map/all_to_all | solution.py:136
  150.5 9.2 %fusion.18 = f32[16,1024,8]{1,0,2:T(8,128)S(1)} fusion(f32[1024,512]{1,0:T(8,128)} %get-tuple-element.14, f32[1024,512]{1,0:T(8,128)S(1)} %get-tuple-element.13, f32[1024,512]{1,0:T(8,128)} %fusion.30, f32[16,8,1024]{2,0,1:T(8,128)S(1)} %reshape.232, f32[16,8,1024]{2,0,1:T(8,128)S(1)} %reshape.231), kind=kOutput, calls=%fused_computation.27 | convolution fusion | flops 3227779072 | bytes 7864320 | tf_op jit(solution)/shard_map/spc,cm->smp/dot_general | solution.py:144
  159.8 0.3 copy.109
  160.1 2.1 copy.110
  162.2 3.0 reshape.239
  165.2 10.3 %all-to-all-start.3 = ((bf16[64,2,1024]{2,1,0:T(2,128)(2,1)}), bf16[64,2,1024]{2,1,0:T(2,128)(2,1)S(1)}, u32[]{:S(2)}, u32[]{:S(2)}) async-start(bf16[64,2,1024]{2,1,0:T(2,128)(2,1)} %reshape.239), calls=%async_computation.3 | async-start | bytes 524288 | tf_op jit(solution)/shard_map/all_to_all | solution.py:147
  175.5 0.0 all-gather.2.cloned.1.call-start
  175.5 11.9 %all-to-all-done.3 = bf16[64,2,1024]{2,1,0:T(2,128)(2,1)S(1)} async-done(((bf16[64,2,1024]{2,1,0:T(2,128)(2,1)}), bf16[64,2,1024]{2,1,0:T(2,128)(2,1)S(1)}, u32[]{:S(2)}, u32[]{:S(2)}) %all-to-all-start.3) | async-done | bytes 262176 | tf_op jit(solution)/shard_map/all_to_all | solution.py:147
  187.5 1.7 reshape.240
  189.2 1.9 copy.130
  191.0 2.6 copy.113
  193.7 0.0 all-gather.2.cloned.1.call-update
  193.7 0.0 reduce-scatter.4.cloned.1.call-start
  193.8 0.1 fusion.49
  193.9 0.1 add_select_fusion.5
  193.9 1.1 fusion.36
  195.1 0.8 maximum_bitcast_fusion.4.ph_ref
  195.9 0.0 copy-done.2
  195.9 0.1 broadcast_compare_fusion
  196.0 9.9 %fusion.7.tm_ref = bf16[8,2,256,512]{3,2,1,0:T(8,128)(2,1)} fusion(bf16[256,2,8,512]{3,2,1,0:T(8,128)(2,1)} %param.7, pred[256,8]{0,1:T(8,128)(4,1)S(1)} %broadcast_compare_fusion), kind=kLoop, calls=%fused_computation.9 | loop fusion | flops 2097152 | bytes 8390656 | tf_op jit(solution)/shard_map/transpose | solution.py:75
  205.9 10.4 %all-gather.2.cloned.1.call-done = bf16[64,2,8,512]{3,2,1,0:T(8,128)(2,1)} async-done(((bf16[16,2,8,512]{3,2,1,0:T(8,128)(2,1)}), bf16[64,2,8,512]{3,2,1,0:T(8,128)(2,1)}) %all-gather.2.cloned.1.call-update) | async-done | bytes 1048592 | tf_op jit(solution)/shard_map/all_gather | solution.py:149
  216.3 2.0 copy.114
  218.4 1.1 reshape.227
  219.5 18.7 %shard_map.55 = f32[64,32,256]{2,1,0:T(8,128)} custom-call(f32[8,2,16,512]{3,2,1,0:T(8,128)} %maximum_bitcast_fusion.4.ph_ref, bf16[8,2,64,512]{3,2,1,0:T(8,128)(2,1)} %bitcast.75, bf16[8,2,256,512]{3,2,1,0:T(8,128)(2,1)} %fusion.7.tm_ref), custom_call_target="tpu_custom_call" | custom-call | flops 8589934592 | bytes 7864320 | tf_op jit(solution)/shard_map/pallas_call | solution.py:80
  238.2 0.0 reduce-scatter.4.cloned.1.call-update
  238.2 0.0 reduce-scatter.6.cloned.1.call-start
  238.3 16.9 %reduce-scatter.4.cloned.1.call-done = f32[32,32,256]{2,1,0:T(8,128)} async-done(((f32[64,32,256]{2,1,0:T(8,128)}), f32[32,32,256]{2,1,0:T(8,128)}) %reduce-scatter.4.cloned.1.call-update) | async-done | bytes 1048592 | tf_op jit(solution)/shard_map/reduce_scatter | solution.py:155
  255.1 0.0 reduce-scatter.6.cloned.1.call-update
  255.2 0.0 reduce-scatter.8.cloned.1.call-start
  255.2 37.1 %reduce-scatter.6.cloned.1.call-done = f32[4,32,256]{2,1,0:T(8,128)} async-done(((f32[32,32,256]{2,1,0:T(8,128)}), f32[4,32,256]{2,1,0:T(8,128)}) %reduce-scatter.6.cloned.1.call-update) | async-done | bytes 131088 | tf_op jit(solution)/shard_map/reduce_scatter | solution.py:155
  292.3 0.0 reduce-scatter.8.cloned.1.call-update
  292.4 26.8 %reduce-scatter.8.cloned.1.call-done = f32[1,32,256]{2,1,0:T(8,128)} async-done(((f32[4,32,256]{2,1,0:T(8,128)}), f32[1,32,256]{2,1,0:T(8,128)}) %reduce-scatter.8.cloned.1.call-update) | async-done | bytes 32784 | tf_op jit(solution)/shard_map/reduce_scatter | solution.py:155
  (8 shorter events, 0.1 us)
Async XLA Ops:
  14.8 30.8 %all-to-all-start = ((f32[64,1,2048]{2,1,0:T(1,128)}), f32[64,1,2048]{2,1,0:T(1,128)S(1)}, u32[]{:S(2)}, u32[]{:S(2)}) async-start(f32[64,1,2048]{2,1,0:T(1,128)} %reshape.233), calls=%async_computation | async-start | bytes 1048576 | tf_op jit(solution)/shard_map/all_to_all | solution.py:112
  69.6 23.6 %all-to-all-start.1 = ((f32[64,1,2048]{2,1,0:T(1,128)}), f32[64,1,2048]{2,1,0:T(1,128)S(1)}, u32[]{:S(2)}, u32[]{:S(2)}) async-start(f32[64,1,2048]{2,1,0:T(1,128)} %reshape.237), calls=%async_computation.1 | async-start | bytes 1048576 | tf_op jit(solution)/shard_map/all_to_all | solution.py:129
  79.6 20.2 %copy-start = (f32[512,8]{0,1:T(8,128)S(1)}, f32[512,8]{0,1:T(8,128)}, u32[]{:S(2)}) copy-start(f32[512,8]{0,1:T(8,128)} %param.6) | copy-start | bytes 49156
  93.3 40.1 %all-to-all-start.2 = ((f32[64,1,2048]{2,1,0:T(1,128)}), f32[64,1,2048]{2,1,0:T(1,128)}, u32[]{:S(2)}, u32[]{:S(2)}) async-start(f32[64,1,2048]{2,1,0:T(1,128)} %reshape.235), calls=%async_computation.2 | async-start | bytes 1048576 | tf_op jit(solution)/shard_map/all_to_all | solution.py:136
  165.2 22.3 %all-to-all-start.3 = ((bf16[64,2,1024]{2,1,0:T(2,128)(2,1)}), bf16[64,2,1024]{2,1,0:T(2,128)(2,1)S(1)}, u32[]{:S(2)}, u32[]{:S(2)}) async-start(bf16[64,2,1024]{2,1,0:T(2,128)(2,1)} %reshape.239), calls=%async_computation.3 | async-start | bytes 524288 | tf_op jit(solution)/shard_map/all_to_all | solution.py:147
  175.5 40.9 %all-gather.2.cloned.1.call-start = ((), (), s32[]{:S(2)}) async-start(), calls=%async_computation.7 | async-start | bytes 1310720 | tf_op jit(solution)/shard_map/all_gather | solution.py:149
  191.0 2.7 copy-start.1
  191.0 4.9 %copy-start.2 = (s32[256]{0:T(256)S(1)}, s32[256]{0:T(256)}, u32[]{:S(2)}) copy-start(s32[256]{0:T(256)} %param.8) | copy-start | bytes 3076
  193.7 61.4 %reduce-scatter.4.cloned.1.call-start = ((), (), s32[]{:S(2)}) async-start(), calls=%async_computation.8 | async-start | bytes 3145728 | tf_op jit(solution)/shard_map/reduce_scatter | solution.py:155
  238.2 54.1 %reduce-scatter.6.cloned.1.call-start = ((), (), s32[]{:S(2)}) async-start(), calls=%async_computation.9 | async-start | bytes 1179648 | tf_op jit(solution)/shard_map/reduce_scatter | solution.py:155
  255.2 64.1 %reduce-scatter.8.cloned.1.call-start = ((), (), s32[]{:S(2)}) async-start(), calls=%async_computation.10 | async-start | bytes 163840 | tf_op jit(solution)/shard_map/reduce_scatter | solution.py:155
Sparse Core Ops, SparseCore 0:
  193.8 22.4 all-gather.1
  238.3 16.7 reduce-scatter.3
  257.8 34.4 reduce-scatter.5
  294.9 24.3 reduce-scatter.7

commit v3 on v2

--- a/solution.py
+++ b/solution.py
@@ -126,21 +126,12 @@
         axis=0,
     )
     amplitude = jnp.sqrt(LEN * psd)
-    real_in = lax.all_to_all(
-        real_part * twist_cos + imag_part * twist_sin,
-        FREQ,
-        split_axis=1,
-        concat_axis=2,
-        tiled=True,
+    twisted = jnp.stack(
+        [real_part * twist_cos + imag_part * twist_sin, imag_part * twist_cos - real_part * twist_sin],
+        axis=2,
     )
-    imag_in = lax.all_to_all(
-        imag_part * twist_cos - real_part * twist_sin,
-        FREQ,
-        split_axis=1,
-        concat_axis=2,
-        tiled=True,
-    )
-    joined = jnp.concatenate([real_in, imag_in], axis=2)
+    joined = lax.all_to_all(twisted, FREQ, split_axis=1, concat_axis=3, tiled=True)
+    joined = joined.reshape(joined.shape[0], joined.shape[1], -1)
     both_out = jnp.einsum("spc,cm->smp", joined, rotation, precision=highest)
     both_out = both_out.reshape(joined.shape[0], 2, NB, joined.shape[1])
     whitened = (both_out / amplitude).astype(jnp.bfloat16)
@@ -151,7 +142,7 @@
     seg_order = seg_piece.reshape((x_size, z_size, c_size) + seg_piece.shape[1:])
     seg_order = seg_order.transpose(2, 1, 0, 3, 4, 5).reshape(seg_piece.shape)
     partial_sums = intersect(seg_order, templates, cutoffs, lags, first_block)
-    for name in ("fc", "fz", "fx"):
+    for name in ("fc", ("fz", "fx")):
         partial_sums = lax.psum_scatter(partial_sums, name, scatter_dimension=0, tiled=True)
     return partial_sums
 

time: 331 us -> 468 us (1.41)
  waiting for transfers between devices: 126 us -> 277 us
  starting transfers between devices: 36.9 us -> 26.4 us
  local copies, waits for them, and re-layouts: 79.1 us -> 73.7 us
    reduce_scatter x3 -> x2, waiting for transfers between devices: 80.9 us -> 231 us  [on_device(): lax.psum_scatter(partial_sums, name, scatter_dimension=0, tiled=True)]
    all_to_all x4 -> x0, local copies, waits for them, and re-layouts: 22.6 us -> none  [the longest x2 11.3 us: on_device(): lax.all_to_all(imag_part * twist_cos - real_part * twist_sin, FREQ, split...]
    reshape x0 -> x2, local copies, waits for them, and re-layouts: none -> 19.5 us  [on_device(): joined = joined.reshape(joined.shape[0], joined.shape[1], -1)]
    another operation x0 -> x1, local copies, waits for them, and re-layouts: none -> 7.47 us  [on_device(): jnp.stack([real_part * twist_cos + imag_part * twist_sin, imag_part * twi...]
    all_to_all x2 -> x1, starting transfers between devices: 12.8 us -> 6.42 us  [on_device(): lax.all_to_all(twisted, FREQ, split_axis=1, concat_axis=3, tiled=True)]
    all_to_all x2 -> x1, waiting for transfers between devices: 9.48 us -> 10.9 us  [on_device(): lax.all_to_all(twisted, FREQ, split_axis=1, concat_axis=3, tiled=True)]
  transfers between devices with their start and end apart: 8 -> 6, of which waited for: 7 -> 6; matrix products, arithmetic and copies ran while one was open for 18% -> 7% of each run, Pallas kernels for 0% -> 0%
where the time goes in v3:
time: 468 us; the launch traced here: 460 us
  waiting for transfers between devices  277 us (59%)
  local copies, waits for them, and re-layouts  73.7 us (16%)
  other arithmetic  39.7 us (8%)
  starting transfers between devices  26.4 us (6%)
  Pallas kernels  18.7 us (4%)
  between operations  13.6 us (3%)
  matrix products  11.2 us (2%)
    reduce_scatter x2, waiting for transfers between devices, on_device(): lax.psum_scatter(partial_sums, name, scatter_dimension=0, tiled=True)  231 us
    unnamed x15, local copies, waits for them, and re-layouts  24.6 us
    reshape x2, local copies, waits for them, and re-layouts, on_device(): joined = joined.reshape(joined.shape[0], joined.shape[1], -1)  19.5 us
    pallas_call x1, Pallas kernels, intersect(): pl.pallas_call(intersect_kernel, out_shape=jax.ShapeDtypeStruct((seg_coun...  18.7 us
    all_to_all x1, starting transfers between devices, on_device(): lax.all_to_all(slab_blocks, FREQ, split_axis=2, concat_axis=1, tiled=True)  13.6 us
    all_to_all x1, waiting for transfers between devices, on_device(): lax.all_to_all(slab_blocks, FREQ, split_axis=2, concat_axis=1, tiled=True)  12.8 us
    all_to_all x1, waiting for transfers between devices, on_device(): lax.all_to_all(whitened, FREQ, split_axis=2, concat_axis=3, tiled=True)  11.9 us
    all_to_all x1, waiting for transfers between devices, on_device(): lax.all_to_all(twisted, FREQ, split_axis=1, concat_axis=3, tiled=True)  10.9 us
  transfers between devices with their start and end apart: 6, of which 6 were waited for; matrix products, arithmetic and copies ran while one was open for 7% of the time, Pallas kernels for 0%

profile of v3, /device:TPU:1, one launch (start us, length us, event | category | flops | bytes accessed | tf_op | source)
XLA Modules:
  0.0 460.1 jit_solution(11155158366169786821)
XLA Ops:
  6.5 1.3 copy.98
  7.9 2.7 copy.77
  10.6 4.2 reshape.237
  14.8 13.6 %all-to-all-start = ((f32[64,1,2048]{2,1,0:T(1,128)}), f32[64,1,2048]{2,1,0:T(1,128)S(1)}, u32[]{:S(2)}, u32[]{:S(2)}) async-start(f32[64,1,2048]{2,1,0:T(1,128)} %reshape.237), calls=%async_computation | async-start | bytes 1048576 | tf_op jit(solution)/shard_map/all_to_all | solution.py:112
  28.5 4.1 sine_negate_fusion
  32.6 0.2 fusion.45
  32.8 12.8 %all-to-all-done = f32[64,1,2048]{2,1,0:T(1,128)S(1)} async-done(((f32[64,1,2048]{2,1,0:T(1,128)}), f32[64,1,2048]{2,1,0:T(1,128)S(1)}, u32[]{:S(2)}, u32[]{:S(2)}) %all-to-all-start) | async-done | bytes 524320 | tf_op jit(solution)/shard_map/all_to_all | solution.py:112
  45.6 0.5 broadcast.322
  46.1 1.9 reduce
  48.0 2.8 reshape.238
  50.8 6.0 %copy.79 = f32[16,64,8,16]{3,2,1,0:T(8,128)} copy(f32[16,64,8,16]{0,2,3,1:T(8,128)} %bitcast.59) | data formatting | bytes 1048576 | tf_op jit(solution)/shard_map/all_to_all | solution.py:112
  56.8 2.8 copy.80
  59.6 2.0 fusion.11
  61.6 0.2 add_bitcast_fusion
  61.8 0.1 pad_maximum_fusion
  61.9 7.5 %copy.81 = f32[16,512,2,16]{3,0,2,1:T(8,128)} copy(f32[16,512,2,16]{1,3,0,2:T(8,128)S(1)} %pad_maximum_fusion) | data formatting | bytes 2097152 | tf_op jit(solution)/shard_map/stack | solution.py:129
  69.3 7.1 %reshape.239 = f32[64,1,4096]{2,1,0:T(1,128)} reshape(f32[512,2,16,16]{3,2,1,0:T(8,128)} %bitcast.56) | data formatting | bytes 2097152
  76.4 0.0 copy-start.1
  76.4 6.4 %all-to-all-start.1 = ((f32[64,1,4096]{2,1,0:T(1,128)}), f32[64,1,4096]{2,1,0:T(1,128)S(1)}, u32[]{:S(2)}, u32[]{:S(2)}) async-start(f32[64,1,4096]{2,1,0:T(1,128)} %reshape.239), calls=%async_computation.1 | async-start | bytes 2097152 | tf_op jit(solution)/shard_map/all_to_all | solution.py:133
  82.8 0.0 copy-done.1
  82.9 9.1 %fusion.24 = (f32[1024,512]{1,0:T(8,128)}, f32[1024,512]{1,0:T(8,128)}) fusion(), kind=kLoop, calls=%fused_computation.35 | loop fusion | flops 7340032 | bytes 4194304 | tf_op jit(solution)/shard_map/sin | solution.py:23
  92.0 8.5 %fusion.27 = f32[1024,512]{1,0:T(8,128)} fusion(), kind=kLoop, calls=%fused_computation.38 | loop fusion | flops 7864320 | bytes 2097152 | tf_op jit(solution)/shard_map/neg | solution.py:123
  100.5 10.9 %all-to-all-done.1 = f32[64,1,4096]{2,1,0:T(1,128)S(1)} async-done(((f32[64,1,4096]{2,1,0:T(1,128)}), f32[64,1,4096]{2,1,0:T(1,128)S(1)}, u32[]{:S(2)}, u32[]{:S(2)}) %all-to-all-start.1) | async-done | bytes 1048608 | tf_op jit(solution)/shard_map/all_to_all | solution.py:133
  111.4 3.3 reduce.1
  114.7 4.8 %reshape.240 = f32[512,2,16,16]{3,2,1,0:T(8,128)} reshape(f32[64,4096]{1,0:T(8,128)S(1)} %reduce.1) | data formatting | bytes 2097152
  119.5 11.3 %copy.95 = f32[16,8,2,64,16]{4,3,2,0,1:T(8,128)} copy(f32[16,8,2,64,16]{4,0,2,1,3:T(8,128)} %bitcast.57) | data formatting | bytes 2097152 | tf_op jit(solution)/shard_map/reshape | solution.py:134
  130.8 0.0 copy-start
  130.8 8.2 %reshape.236 = f32[16,8,2048]{2,0,1:T(8,128)S(1)} reshape(f32[16,8,2,64,16]{4,3,2,0,1:T(8,128)} %copy.95) | data formatting | bytes 2097152 | tf_op jit(solution)/shard_map/reshape | solution.py:134
  139.0 0.0 copy-done
  139.0 9.2 %fusion.18 = f32[16,1024,8]{1,0,2:T(8,128)S(1)} fusion(f32[16,8,2048]{2,0,1:T(8,128)S(1)} %reshape.236, f32[1024,512]{1,0:T(8,128)} %get-tuple-element.14, f32[1024,512]{1,0:T(8,128)S(1)} %copy-done, f32[1024,512]{1,0:T(8,128)} %fusion.27), kind=kOutput, calls=%fused_computation.27 | convolution fusion | flops 3227516928 | bytes 7864320 | tf_op jit(solution)/shard_map/spc,cm->smp/dot_general | solution.py:135
  148.2 0.3 copy.85
  148.6 2.1 copy.86
  150.7 2.9 reshape.241
  153.6 6.2 %all-to-all-start.2 = ((bf16[64,2,1024]{2,1,0:T(2,128)(2,1)}), bf16[64,2,1024]{2,1,0:T(2,128)(2,1)S(1)}, u32[]{:S(2)}, u32[]{:S(2)}) async-start(bf16[64,2,1024]{2,1,0:T(2,128)(2,1)} %reshape.241), calls=%async_computation.2 | async-start | bytes 524288 | tf_op jit(solution)/shard_map/all_to_all | solution.py:138
  159.8 0.0 all-gather.2.cloned.1.call-start
  159.9 11.9 %all-to-all-done.2 = bf16[64,2,1024]{2,1,0:T(2,128)(2,1)S(1)} async-done(((bf16[64,2,1024]{2,1,0:T(2,128)(2,1)}), bf16[64,2,1024]{2,1,0:T(2,128)(2,1)S(1)}, u32[]{:S(2)}, u32[]{:S(2)}) %all-to-all-start.2) | async-done | bytes 262176 | tf_op jit(solution)/shard_map/all_to_all | solution.py:138
  171.8 1.4 reshape.242
  173.2 1.9 copy.103
  175.1 0.0 copy-start.2
  175.1 0.0 copy-start.3
  175.1 2.6 copy.89
  177.7 0.0 all-gather.2.cloned.1.call-update
  177.8 0.0 reduce-scatter.3.cloned.1.call-start
  177.8 0.0 copy-done.2
  177.8 0.1 fusion.46
  177.9 0.1 add_select_fusion.5
  178.0 1.1 fusion.33
  179.1 0.8 maximum_bitcast_fusion.4.ph_ref
  180.0 0.0 copy-done.3
  180.0 0.1 broadcast_compare_fusion
  180.0 10.2 %fusion.7.tm_ref = bf16[8,2,256,512]{3,2,1,0:T(8,128)(2,1)} fusion(bf16[256,2,8,512]{3,2,1,0:T(8,128)(2,1)} %param.7, pred[256,8]{0,1:T(8,128)(4,1)S(1)} %broadcast_compare_fusion), kind=kLoop, calls=%fused_computation.9 | loop fusion | flops 2097152 | bytes 8390656 | tf_op jit(solution)/shard_map/transpose | solution.py:75
  190.2 10.2 %all-gather.2.cloned.1.call-done = bf16[64,2,8,512]{3,2,1,0:T(8,128)(2,1)} async-done(((bf16[16,2,8,512]{3,2,1,0:T(8,128)(2,1)}), bf16[64,2,8,512]{3,2,1,0:T(8,128)(2,1)}) %all-gather.2.cloned.1.call-update) | async-done | bytes 1048592 | tf_op jit(solution)/shard_map/all_gather | solution.py:140
  200.4 2.0 copy.90
  202.4 1.1 reshape.232
  203.6 18.7 %shard_map.55 = f32[64,32,256]{2,1,0:T(8,128)} custom-call(f32[8,2,16,512]{3,2,1,0:T(8,128)} %maximum_bitcast_fusion.4.ph_ref, bf16[8,2,64,512]{3,2,1,0:T(8,128)(2,1)} %bitcast.69, bf16[8,2,256,512]{3,2,1,0:T(8,128)(2,1)} %fusion.7.tm_ref), custom_call_target="tpu_custom_call" | custom-call | flops 8589934592 | bytes 7864320 | tf_op jit(solution)/shard_map/pallas_call | solution.py:80
  222.2 0.0 reduce-scatter.3.cloned.1.call-update
  222.3 0.0 reduce-scatter.5.cloned.1.call-start
  222.3 16.9 %reduce-scatter.3.cloned.1.call-done = f32[32,32,256]{2,1,0:T(8,128)} async-done(((f32[64,32,256]{2,1,0:T(8,128)}), f32[32,32,256]{2,1,0:T(8,128)}) %reduce-scatter.3.cloned.1.call-update) | async-done | bytes 1048592 | tf_op jit(solution)/shard_map/reduce_scatter | solution.py:146
  239.2 0.0 reduce-scatter.5.cloned.1.call-update
  239.2 214.1 %reduce-scatter.5.cloned.1.call-done = f32[1,32,256]{2,1,0:T(8,128)} async-done(((f32[32,32,256]{2,1,0:T(8,128)}), f32[1,32,256]{2,1,0:T(8,128)}) %reduce-scatter.5.cloned.1.call-update) | async-done | bytes 32784 | tf_op jit(solution)/shard_map/reduce_scatter | solution.py:146
  (4 shorter events, 0.1 us)
Async XLA Ops:
  14.8 30.8 %all-to-all-start = ((f32[64,1,2048]{2,1,0:T(1,128)}), f32[64,1,2048]{2,1,0:T(1,128)S(1)}, u32[]{:S(2)}, u32[]{:S(2)}) async-start(f32[64,1,2048]{2,1,0:T(1,128)} %reshape.237), calls=%async_computation | async-start | bytes 1048576 | tf_op jit(solution)/shard_map/all_to_all | solution.py:112
  76.4 6.4 %copy-start.1 = (f32[512,8]{0,1:T(8,128)S(1)}, f32[512,8]{0,1:T(8,128)}, u32[]{:S(2)}) copy-start(f32[512,8]{0,1:T(8,128)} %param.6) | copy-start | bytes 49156
  76.4 35.0 %all-to-all-start.1 = ((f32[64,1,4096]{2,1,0:T(1,128)}), f32[64,1,4096]{2,1,0:T(1,128)S(1)}, u32[]{:S(2)}, u32[]{:S(2)}) async-start(f32[64,1,4096]{2,1,0:T(1,128)} %reshape.239), calls=%async_computation.1 | async-start | bytes 2097152 | tf_op jit(solution)/shard_map/all_to_all | solution.py:133
  130.8 8.2 %copy-start = (f32[1024,512]{1,0:T(8,128)S(1)}, f32[1024,512]{1,0:T(8,128)}, u32[]{:S(2)}) copy-start(f32[1024,512]{1,0:T(8,128)} %get-tuple-element.13) | copy-start | bytes 6291460
  153.6 18.2 %all-to-all-start.2 = ((bf16[64,2,1024]{2,1,0:T(2,128)(2,1)}), bf16[64,2,1024]{2,1,0:T(2,128)(2,1)S(1)}, u32[]{:S(2)}, u32[]{:S(2)}) async-start(bf16[64,2,1024]{2,1,0:T(2,128)(2,1)} %reshape.241), calls=%async_computation.2 | async-start | bytes 524288 | tf_op jit(solution)/shard_map/all_to_all | solution.py:138
  159.8 40.6 %all-gather.2.cloned.1.call-start = ((), (), s32[]{:S(2)}) async-start(), calls=%async_computation.5 | async-start | bytes 1310720 | tf_op jit(solution)/shard_map/all_gather | solution.py:140
  175.1 2.7 copy-start.2
  175.1 4.8 %copy-start.3 = (s32[256]{0:T(256)S(1)}, s32[256]{0:T(256)}, u32[]{:S(2)}) copy-start(s32[256]{0:T(256)} %param.8) | copy-start | bytes 3076
  177.8 61.4 %reduce-scatter.3.cloned.1.call-start = ((), (), s32[]{:S(2)}) async-start(), calls=%async_computation.6 | async-start | bytes 3145728 | tf_op jit(solution)/shard_map/reduce_scatter | solution.py:146
  222.3 231.0 %reduce-scatter.5.cloned.1.call-start = ((), (), s32[]{:S(2)}) async-start(), calls=%async_computation.7 | async-start | bytes 1081344 | tf_op jit(solution)/shard_map/reduce_scatter | solution.py:146
Sparse Core Ops, SparseCore 0:
  177.9 22.4 all-gather.1
  222.4 16.7 reduce-scatter.2
  243.5 209.7 reduce-scatter.4

commit v4 on v3

--- a/solution.py
+++ b/solution.py
@@ -1,3 +1,4 @@
+import functools
 import math
 
 import jax
@@ -93,6 +94,55 @@
     )(phases, data, masked)
 
 
+def scatter_kernel(axis, size, x_ref, o_ref, recv_ref, send_sem, recv_sem):
+    me = lax.axis_index(axis)
+    piece = o_ref.shape[0]
+    mesh_ids = pl.DeviceIdType.MESH
+    barrier = pltpu.get_barrier_semaphore()
+    for k in range(1, size):
+        peer = lax.rem(me + k, size)
+        pl.semaphore_signal(barrier, inc=1, device_id={axis: peer}, device_id_type=mesh_ids)
+    pl.semaphore_wait(barrier, size - 1)
+    copies = []
+    for k in range(1, size):
+        peer = lax.rem(me + k, size)
+        copy = pltpu.make_async_remote_copy(
+            src_ref=x_ref.at[pl.ds(peer * piece, piece)],
+            dst_ref=recv_ref.at[k],
+            send_sem=send_sem.at[k],
+            recv_sem=recv_sem.at[k],
+            device_id={axis: peer},
+            device_id_type=mesh_ids,
+        )
+        copy.start()
+        copies.append(copy)
+    for copy in copies:
+        copy.wait()
+    total = x_ref[pl.ds(me * piece, piece)]
+    for k in range(1, size):
+        total = total + recv_ref[k]
+    o_ref[...] = total
+
+
+def scatter_sum(parts, axis, collective_id):
+    size = lax.axis_size(axis)
+    piece = parts.shape[0] // size
+    out_shape = (piece,) + parts.shape[1:]
+    vmem = pltpu.VMEM
+    return pl.pallas_call(
+        functools.partial(scatter_kernel, axis, size),
+        out_shape=jax.ShapeDtypeStruct(out_shape, parts.dtype),
+        in_specs=[pl.BlockSpec(memory_space=vmem)],
+        out_specs=pl.BlockSpec(memory_space=vmem),
+        scratch_shapes=[
+            vmem((size,) + out_shape, parts.dtype),
+            pltpu.SemaphoreType.DMA((size,)),
+            pltpu.SemaphoreType.DMA((size,)),
+        ],
+        compiler_params=pltpu.CompilerParams(collective_id=collective_id, has_side_effects=True),
+    )(parts)
+
+
 def on_device(strain, psd, templates, cutoffs, lags):
     freq_count = lax.axis_size(FREQ)
     freq_index = lax.axis_index(FREQ)
@@ -142,8 +192,8 @@
     seg_order = seg_piece.reshape((x_size, z_size, c_size) + seg_piece.shape[1:])
     seg_order = seg_order.transpose(2, 1, 0, 3, 4, 5).reshape(seg_piece.shape)
     partial_sums = intersect(seg_order, templates, cutoffs, lags, first_block)
-    for name in ("fc", ("fz", "fx")):
-        partial_sums = lax.psum_scatter(partial_sums, name, scatter_dimension=0, tiled=True)
+    for collective_id, name in enumerate(("fc", "fz", "fx")):
+        partial_sums = scatter_sum(partial_sums, name, collective_id + 1)
     return partial_sums
 
 

time: 468 us -> 279 us (0.60)
  waiting for transfers between devices: 277 us -> 46.2 us
  Pallas kernels: 18.7 us -> 63.5 us
    reduce_scatter x2 -> x0, waiting for transfers between devices: 231 us -> none  [on_device(): lax.psum_scatter(partial_sums, name, scatter_dimension=0, tiled=True)]
    pallas_call x0 -> x3, Pallas kernels: none -> 44.8 us  [scatter_sum(): pl.pallas_call(functools.partial(scatter_kernel, axis, size), out_shape=j...]
    unnamed x15 -> x16, local copies, waits for them, and re-layouts: 24.6 us -> 26.2 us
  transfers between devices with their start and end apart: 6 -> 4, of which waited for: 6 -> 4; matrix products, arithmetic and copies ran while one was open for 7% -> 12% of each run, Pallas kernels for 0% -> 0%
where the time goes in v4:
time: 279 us; the launch traced here: 276 us
  local copies, waits for them, and re-layouts  75.3 us (27%)
  Pallas kernels  63.5 us (23%)
  waiting for transfers between devices  46.2 us (17%)
  other arithmetic  39.5 us (14%)
  starting transfers between devices  26.2 us (9%)
  between operations  13.9 us (5%)
  matrix products  11.2 us (4%)
    pallas_call x3, Pallas kernels, scatter_sum(): pl.pallas_call(functools.partial(scatter_kernel, axis, size), out_shape=j...  44.8 us
    unnamed x16, local copies, waits for them, and re-layouts  26.2 us
    reshape x2, local copies, waits for them, and re-layouts, on_device(): joined = joined.reshape(joined.shape[0], joined.shape[1], -1)  19.5 us
    pallas_call x1, Pallas kernels, intersect(): pl.pallas_call(intersect_kernel, out_shape=jax.ShapeDtypeStruct((seg_coun...  18.7 us
    all_to_all x1, starting transfers between devices, on_device(): lax.all_to_all(slab_blocks, FREQ, split_axis=2, concat_axis=1, tiled=True)  13.6 us
    all_to_all x1, waiting for transfers between devices, on_device(): lax.all_to_all(slab_blocks, FREQ, split_axis=2, concat_axis=1, tiled=True)  12.8 us
    all_to_all x1, waiting for transfers between devices, on_device(): lax.all_to_all(whitened, FREQ, split_axis=2, concat_axis=3, tiled=True)  11.9 us
    all_to_all x1, waiting for transfers between devices, on_device(): lax.all_to_all(twisted, FREQ, split_axis=1, concat_axis=3, tiled=True)  10.9 us
  transfers between devices with their start and end apart: 4, of which 4 were waited for; matrix products, arithmetic and copies ran while one was open for 12% of the time, Pallas kernels for 0%

profile of v4, /device:TPU:1, one launch (start us, length us, event | category | flops | bytes accessed | tf_op | source)
XLA Modules:
  0.0 275.8 jit_solution(9023503277796216617)
XLA Ops:
  6.5 1.3 copy.98
  7.9 2.7 copy.77
  10.6 4.2 %reshape.237 = f32[64,1,2048]{2,1,0:T(1,128)} reshape(f32[1024,8,16]{2,1,0:T(8,128)} %bitcast.58) | data formatting | bytes 1048576
  14.8 13.6 %all-to-all-start = ((f32[64,1,2048]{2,1,0:T(1,128)}), f32[64,1,2048]{2,1,0:T(1,128)S(1)}, u32[]{:S(2)}, u32[]{:S(2)}) async-start(f32[64,1,2048]{2,1,0:T(1,128)} %reshape.237), calls=%async_computation | async-start | bytes 1048576 | tf_op jit(solution)/shard_map/all_to_all | solution.py:162
  28.4 4.1 %sine_negate_fusion = (f32[512,512]{1,0:T(8,128)S(1)}, f32[512,512]{1,0:T(8,128)S(1)}) fusion(), kind=kLoop, calls=%fused_computation.32 | loop fusion | flops 3932160 | bytes 2097152 | tf_op jit(solution)/shard_map/neg | solution.py:155
  32.5 0.2 fusion.45
  32.7 12.8 %all-to-all-done = f32[64,1,2048]{2,1,0:T(1,128)S(1)} async-done(((f32[64,1,2048]{2,1,0:T(1,128)}), f32[64,1,2048]{2,1,0:T(1,128)S(1)}, u32[]{:S(2)}, u32[]{:S(2)}) %all-to-all-start) | async-done | bytes 524320 | tf_op jit(solution)/shard_map/all_to_all | solution.py:162
  45.6 0.5 broadcast.322
  46.1 1.9 reduce
  48.0 2.8 %reshape.238 = f32[1024,8,16]{2,1,0:T(8,128)} reshape(f32[64,2048]{1,0:T(8,128)S(1)} %reduce) | data formatting | bytes 1048576
  50.8 6.0 %copy.79 = f32[16,64,8,16]{3,2,1,0:T(8,128)} copy(f32[16,64,8,16]{0,2,3,1:T(8,128)} %bitcast.59) | data formatting | bytes 1048576 | tf_op jit(solution)/shard_map/all_to_all | solution.py:162
  56.7 2.8 %copy.80 = f32[16,512,16]{1,2,0:T(8,128)S(1)} copy(f32[16,512,16]{2,1,0:T(8,128)} %bitcast.60) | data formatting | bytes 1048576 | tf_op jit(solution)/shard_map/all_to_all | solution.py:162
  59.5 2.0 fusion.11
  61.6 0.2 add_bitcast_fusion
  61.7 0.1 pad_maximum_fusion
  61.8 7.5 %copy.81 = f32[16,512,2,16]{3,0,2,1:T(8,128)} copy(f32[16,512,2,16]{1,3,0,2:T(8,128)S(1)} %pad_maximum_fusion) | data formatting | bytes 2097152 | tf_op jit(solution)/shard_map/stack | solution.py:179
  69.3 7.1 %reshape.239 = f32[64,1,4096]{2,1,0:T(1,128)} reshape(f32[512,2,16,16]{3,2,1,0:T(8,128)} %bitcast.56) | data formatting | bytes 2097152
  76.3 0.0 copy-start.1
  76.3 6.4 %all-to-all-start.1 = ((f32[64,1,4096]{2,1,0:T(1,128)}), f32[64,1,4096]{2,1,0:T(1,128)S(1)}, u32[]{:S(2)}, u32[]{:S(2)}) async-start(f32[64,1,4096]{2,1,0:T(1,128)} %reshape.239), calls=%async_computation.1 | async-start | bytes 2097152 | tf_op jit(solution)/shard_map/all_to_all | solution.py:183
  82.8 0.0 copy-done.1
  82.8 9.1 %fusion.24 = (f32[1024,512]{1,0:T(8,128)}, f32[1024,512]{1,0:T(8,128)}) fusion(), kind=kLoop, calls=%fused_computation.35 | loop fusion | flops 7340032 | bytes 4194304 | tf_op jit(solution)/shard_map/sin | solution.py:24
  91.9 8.5 %fusion.27 = f32[1024,512]{1,0:T(8,128)} fusion(), kind=kLoop, calls=%fused_computation.38 | loop fusion | flops 7864320 | bytes 2097152 | tf_op jit(solution)/shard_map/neg | solution.py:173
  100.4 10.9 %all-to-all-done.1 = f32[64,1,4096]{2,1,0:T(1,128)S(1)} async-done(((f32[64,1,4096]{2,1,0:T(1,128)}), f32[64,1,4096]{2,1,0:T(1,128)S(1)}, u32[]{:S(2)}, u32[]{:S(2)}) %all-to-all-start.1) | async-done | bytes 1048608 | tf_op jit(solution)/shard_map/all_to_all | solution.py:183
  111.3 3.3 %reduce.1 = f32[64,4096]{1,0:T(8,128)S(1)} reduce(f32[64,1,4096]{2,1,0:T(1,128)S(1)} %all-to-all-done.1, f32[]{:T(128)} %broadcast.322), dimensions={1}, to_apply=%all_to_all.41.reduce_sub_computation | reduce | bytes 2097156 | tf_op jit(solution)/shard_map/all_to_all | solution.py:183
  114.6 4.8 %reshape.240 = f32[512,2,16,16]{3,2,1,0:T(8,128)} reshape(f32[64,4096]{1,0:T(8,128)S(1)} %reduce.1) | data formatting | bytes 2097152
  119.4 11.3 %copy.95 = f32[16,8,2,64,16]{4,3,2,0,1:T(8,128)} copy(f32[16,8,2,64,16]{4,0,2,1,3:T(8,128)} %bitcast.57) | data formatting | bytes 2097152 | tf_op jit(solution)/shard_map/reshape | solution.py:184
  130.8 0.0 copy-start
  130.8 8.2 %reshape.236 = f32[16,8,2048]{2,0,1:T(8,128)S(1)} reshape(f32[16,8,2,64,16]{4,3,2,0,1:T(8,128)} %copy.95) | data formatting | bytes 2097152 | tf_op jit(solution)/shard_map/reshape | solution.py:184
  139.0 0.0 copy-done
  139.0 9.2 %fusion.18 = f32[16,1024,8]{1,0,2:T(8,128)S(1)} fusion(f32[16,8,2048]{2,0,1:T(8,128)S(1)} %reshape.236, f32[1024,512]{1,0:T(8,128)} %get-tuple-element.14, f32[1024,512]{1,0:T(8,128)S(1)} %copy-done, f32[1024,512]{1,0:T(8,128)} %fusion.27), kind=kOutput, calls=%fused_computation.27 | convolution fusion | flops 3227516928 | bytes 7864320 | tf_op jit(solution)/shard_map/spc,cm->smp/dot_general | solution.py:185
  148.2 0.3 copy.85
  148.5 2.1 copy.86
  150.6 2.9 %reshape.241 = bf16[64,2,1024]{2,1,0:T(2,128)(2,1)} reshape(bf16[512,2,8,16]{3,2,1,0:T(8,128)(2,1)S(1)} %bitcast.61) | data formatting | bytes 524288
  153.5 6.2 %all-to-all-start.2 = ((bf16[64,2,1024]{2,1,0:T(2,128)(2,1)}), bf16[64,2,1024]{2,1,0:T(2,128)(2,1)S(1)}, u32[]{:S(2)}, u32[]{:S(2)}) async-start(bf16[64,2,1024]{2,1,0:T(2,128)(2,1)} %reshape.241), calls=%async_computation.2 | async-start | bytes 524288 | tf_op jit(solution)/shard_map/all_to_all | solution.py:188
  159.7 0.0 all-gather.2.cloned.1.call-start
  159.8 11.9 %all-to-all-done.2 = bf16[64,2,1024]{2,1,0:T(2,128)(2,1)S(1)} async-done(((bf16[64,2,1024]{2,1,0:T(2,128)(2,1)}), bf16[64,2,1024]{2,1,0:T(2,128)(2,1)S(1)}, u32[]{:S(2)}, u32[]{:S(2)}) %all-to-all-start.2) | async-done | bytes 262176 | tf_op jit(solution)/shard_map/all_to_all | solution.py:188
  171.7 1.7 reshape.242
  173.4 1.9 copy.103
  175.3 0.0 copy-start.2
  175.3 0.0 copy-start.3
  175.3 2.6 copy.89
  177.9 0.0 all-gather.2.cloned.1.call-update
  178.0 0.0 copy-done.2
  178.0 0.1 fusion.46
  178.1 0.1 add_select_fusion.5
  178.1 1.1 fusion.33
  179.2 0.8 maximum_bitcast_fusion.4.ph_ref
  180.1 0.0 copy-done.3
  180.1 0.1 broadcast_compare_fusion
  180.2 9.9 %fusion.7.tm_ref = bf16[8,2,256,512]{3,2,1,0:T(8,128)(2,1)} fusion(bf16[256,2,8,512]{3,2,1,0:T(8,128)(2,1)} %param.7, pred[256,8]{0,1:T(8,128)(4,1)S(1)} %broadcast_compare_fusion), kind=kLoop, calls=%fused_computation.9 | loop fusion | flops 2097152 | bytes 8390656 | tf_op jit(solution)/shard_map/transpose | solution.py:76
  190.1 10.5 %all-gather.2.cloned.1.call-done = bf16[64,2,8,512]{3,2,1,0:T(8,128)(2,1)} async-done(((bf16[16,2,8,512]{3,2,1,0:T(8,128)(2,1)}), bf16[64,2,8,512]{3,2,1,0:T(8,128)(2,1)}) %all-gather.2.cloned.1.call-update) | async-done | bytes 1048592 | tf_op jit(solution)/shard_map/all_gather | solution.py:190
  200.6 2.0 copy.90
  202.6 1.1 reshape.232
  203.8 18.7 %shard_map.55.x_ref = f32[64,32,256]{2,1,0:T(8,128)} custom-call(f32[8,2,16,512]{3,2,1,0:T(8,128)} %maximum_bitcast_fusion.4.ph_ref, bf16[8,2,64,512]{3,2,1,0:T(8,128)(2,1)} %bitcast.69, bf16[8,2,256,512]{3,2,1,0:T(8,128)(2,1)} %fusion.7.tm_ref), custom_call_target="tpu_custom_call" | custom-call | flops 8589934592 | bytes 7864320 | tf_op jit(solution)/shard_map/pallas_call | solution.py:81
  222.4 6.6 %shard_map.56.x_ref = f32[32,32,256]{2,1,0:T(8,128)} custom-call(f32[64,32,256]{2,1,0:T(8,128)} %shard_map.55.x_ref), custom_call_target="tpu_custom_call" | custom-call | tf_op jit(solution)/shard_map/pallas_call | solution.py:132
  229.0 31.3 %shard_map.57.x_ref = f32[4,32,256]{2,1,0:T(8,128)} custom-call(f32[32,32,256]{2,1,0:T(8,128)} %shard_map.56.x_ref), custom_call_target="tpu_custom_call" | custom-call | tf_op jit(solution)/shard_map/pallas_call | solution.py:132
  260.3 7.0 %shard_map.58 = f32[1,32,256]{2,1,0:T(8,128)} custom-call(f32[4,32,256]{2,1,0:T(8,128)} %shard_map.57.x_ref), custom_call_target="tpu_custom_call" | custom-call | tf_op jit(solution)/shard_map/pallas_call | solution.py:132
  267.3 1.4 copy.105
  (4 shorter events, 0.1 us)
Async XLA Ops:
  14.8 30.8 %all-to-all-start = ((f32[64,1,2048]{2,1,0:T(1,128)}), f32[64,1,2048]{2,1,0:T(1,128)S(1)}, u32[]{:S(2)}, u32[]{:S(2)}) async-start(f32[64,1,2048]{2,1,0:T(1,128)} %reshape.237), calls=%async_computation | async-start | bytes 1048576 | tf_op jit(solution)/shard_map/all_to_all | solution.py:162
  76.3 6.4 %copy-start.1 = (f32[512,8]{0,1:T(8,128)S(1)}, f32[512,8]{0,1:T(8,128)}, u32[]{:S(2)}) copy-start(f32[512,8]{0,1:T(8,128)} %param.6) | copy-start | bytes 49156
  76.3 35.0 %all-to-all-start.1 = ((f32[64,1,4096]{2,1,0:T(1,128)}), f32[64,1,4096]{2,1,0:T(1,128)S(1)}, u32[]{:S(2)}, u32[]{:S(2)}) async-start(f32[64,1,4096]{2,1,0:T(1,128)} %reshape.239), calls=%async_computation.1 | async-start | bytes 2097152 | tf_op jit(solution)/shard_map/all_to_all | solution.py:183
  130.8 8.2 %copy-start = (f32[1024,512]{1,0:T(8,128)S(1)}, f32[1024,512]{1,0:T(8,128)}, u32[]{:S(2)}) copy-start(f32[1024,512]{1,0:T(8,128)} %get-tuple-element.13) | copy-start | bytes 6291460
  153.5 18.2 %all-to-all-start.2 = ((bf16[64,2,1024]{2,1,0:T(2,128)(2,1)}), bf16[64,2,1024]{2,1,0:T(2,128)(2,1)S(1)}, u32[]{:S(2)}, u32[]{:S(2)}) async-start(bf16[64,2,1024]{2,1,0:T(2,128)(2,1)} %reshape.241), calls=%async_computation.2 | async-start | bytes 524288 | tf_op jit(solution)/shard_map/all_to_all | solution.py:188
  159.7 40.9 %all-gather.2.cloned.1.call-start = ((), (), s32[]{:S(2)}) async-start(), calls=%async_computation.3 | async-start | bytes 1310720 | tf_op jit(solution)/shard_map/all_gather | solution.py:190
  175.3 2.7 copy-start.2
  175.3 4.8 %copy-start.3 = (s32[256]{0:T(256)S(1)}, s32[256]{0:T(256)}, u32[]{:S(2)}) copy-start(s32[256]{0:T(256)} %param.8) | copy-start | bytes 3076
Sparse Core Ops, SparseCore 0:
  178.1 22.4 all-gather.1

commit v5 on v4

--- a/solution.py
+++ b/solution.py
@@ -61,8 +61,8 @@
     out_ref[:, lag_total:, :] += imag_sum.reshape(seg_count, lag_total, width)
 
 
-def intersect(seg_piece, templates, cutoffs, lags, first_block):
-    seg_count, _, blocks_here, width = seg_piece.shape
+def intersect(data, templates, cutoffs, lags, first_block):
+    blocks_here, _, seg_count, width = data.shape
     tmpl_local = templates.shape[0]
     lag_total = lags.shape[0]
     block_ids = first_block + jnp.arange(blocks_here, dtype=jnp.int32)
@@ -74,7 +74,6 @@
     phases = jnp.stack([jnp.cos(phase_angle), jnp.sin(phase_angle)], axis=0).transpose(2, 0, 1, 3)
     keep = block_ids[None, None, :, None] < cutoffs[:, None, None, None]
     masked = jnp.where(keep, templates, jnp.zeros_like(templates)).transpose(2, 1, 0, 3)
-    data = seg_piece.transpose(2, 1, 0, 3)
     rows = seg_count * lag_total
     flops = 2 * 2 * (2 * rows) * width * tmpl_local * blocks_here
     moved = masked.size * 2 + data.size * 2 + phases.size * 4 + seg_count * 2 * lag_total * tmpl_local * 4
@@ -143,55 +142,61 @@
     )(parts)
 
 
-def on_device(strain, psd, templates, cutoffs, lags):
+def spectrum_blocks(strain, psd):
     freq_count = lax.axis_size(FREQ)
     freq_index = lax.axis_index(FREQ)
     seg_local = strain.shape[0]
-    step_time = B // freq_count
+    rows_here = A // freq_count
+    cols_here = B // freq_count
     highest = lax.Precision.HIGHEST
     first_cos, first_sin = cos_sin_table(
         jnp.arange(A, dtype=jnp.int32), jnp.arange(A, dtype=jnp.int32), A
     )
     first_table = jnp.concatenate([first_cos, -first_sin], axis=0)
-    time_ids = freq_index * step_time + jnp.arange(step_time, dtype=jnp.int32)
+    sent = strain.reshape(seg_local, rows_here, freq_count, cols_here).transpose(2, 1, 3, 0)
+    sent = sent.reshape(freq_count, rows_here, cols_here * seg_local)
+    slab = lax.all_to_all(sent, FREQ, 0, 0, tiled=True).reshape(A, cols_here * seg_local)
+    both_parts = jnp.dot(first_table, slab, precision=highest)
+    real_part = both_parts[:A]
+    imag_part = both_parts[A:]
+    time_ids = freq_index * cols_here + jnp.arange(cols_here, dtype=jnp.int32)
     twist_cos, twist_sin = cos_sin_table(jnp.arange(A, dtype=jnp.int32), time_ids, LEN)
-    slab_blocks = strain.reshape(seg_local, A // freq_count, B)
-    both_parts = jnp.einsum(
-        "kn,snb->skb",
-        first_table,
-        lax.all_to_all(slab_blocks, FREQ, split_axis=2, concat_axis=1, tiled=True),
-        precision=highest,
-    )
-    half_rows = first_table.shape[0] // 2
-    real_part = both_parts[:, :half_rows]
-    imag_part = both_parts[:, half_rows:]
+    twist_cos = jnp.repeat(twist_cos, seg_local, axis=1)
+    twist_sin = jnp.repeat(twist_sin, seg_local, axis=1)
+    twisted = jnp.stack(
+        [real_part * twist_cos + imag_part * twist_sin, imag_part * twist_cos - real_part * twist_sin]
+    )
+    p_here = A // freq_count
+    twisted = twisted.reshape(2, freq_count, p_here, cols_here, seg_local).transpose(1, 3, 0, 2, 4)
+    twisted = twisted.reshape(freq_count, cols_here, 2 * p_here * seg_local)
+    columns = lax.all_to_all(twisted, FREQ, 0, 0, tiled=True).reshape(B, 2 * p_here * seg_local)
     second_cos, second_sin = cos_sin_table(
-        jnp.arange(B, dtype=jnp.int32), jnp.arange(NB, dtype=jnp.int32), B
-    )
-    rotation = jnp.concatenate(
-        [
-            jnp.concatenate([second_cos, -second_sin], axis=1),
-            jnp.concatenate([second_sin, second_cos], axis=1),
-        ],
-        axis=0,
-    )
-    amplitude = jnp.sqrt(LEN * psd)
-    twisted = jnp.stack(
-        [real_part * twist_cos + imag_part * twist_sin, imag_part * twist_cos - real_part * twist_sin],
-        axis=2,
-    )
-    joined = lax.all_to_all(twisted, FREQ, split_axis=1, concat_axis=3, tiled=True)
-    joined = joined.reshape(joined.shape[0], joined.shape[1], -1)
-    both_out = jnp.einsum("spc,cm->smp", joined, rotation, precision=highest)
-    both_out = both_out.reshape(joined.shape[0], 2, NB, joined.shape[1])
-    whitened = (both_out / amplitude).astype(jnp.bfloat16)
-    local_data = lax.all_to_all(whitened, FREQ, split_axis=2, concat_axis=3, tiled=True)
-    first_block = freq_index * (NB // freq_count)
-    seg_piece = lax.all_gather(local_data, "tmpl", axis=0, tiled=True)
+        jnp.arange(NB, dtype=jnp.int32), jnp.arange(B, dtype=jnp.int32), B
+    )
+    with_cos = jnp.dot(second_cos, columns, precision=highest).reshape(NB, 2, p_here, seg_local)
+    with_sin = jnp.dot(second_sin, columns, precision=highest).reshape(NB, 2, p_here, seg_local)
+    amplitude = jnp.sqrt(LEN * psd)[:, :, None]
+    real_out = (with_cos[:, 0] + with_sin[:, 1]) / amplitude
+    imag_out = (with_cos[:, 1] - with_sin[:, 0]) / amplitude
+    whitened = jnp.stack([real_out, imag_out], axis=1).astype(jnp.bfloat16)
+    j_here = NB // freq_count
+    whitened = whitened.reshape(freq_count, j_here, 2, p_here, seg_local)
+    return lax.all_to_all(whitened, FREQ, 0, 0, tiled=True)
+
+
+def on_device(strain, psd, templates, cutoffs, lags):
+    freq_index = lax.axis_index(FREQ)
+    received = spectrum_blocks(strain, psd)
+    freq_count, j_here, _, p_here, seg_local = received.shape
+    gathered = lax.all_gather(received, "tmpl", axis=0)
+    tmpl_count = gathered.shape[0]
     x_size, z_size, c_size = (lax.axis_size(name) for name in FREQ)
-    seg_order = seg_piece.reshape((x_size, z_size, c_size) + seg_piece.shape[1:])
-    seg_order = seg_order.transpose(2, 1, 0, 3, 4, 5).reshape(seg_piece.shape)
-    partial_sums = intersect(seg_order, templates, cutoffs, lags, first_block)
+    data = gathered.transpose(2, 3, 0, 5, 1, 4).reshape(
+        j_here, 2, x_size, z_size, c_size, freq_count * p_here
+    )
+    data = data.transpose(0, 1, 4, 3, 2, 5).reshape(j_here, 2, tmpl_count * seg_local, -1)
+    first_block = freq_index * j_here
+    partial_sums = intersect(data, templates, cutoffs, lags, first_block)
     for collective_id, name in enumerate(("fc", "fz", "fx")):
         partial_sums = scatter_sum(partial_sums, name, collective_id + 1)
     return partial_sums

time: 279 us -> 358 us (1.28)
  waiting for transfers between devices: 46.2 us -> 122 us
  other arithmetic: 39.5 us -> 18.8 us
  local copies, waits for them, and re-layouts: 75.3 us -> 89.5 us
  matrix products: 11.2 us -> 21.9 us
    all_gather x1, waiting for transfers between devices: 10.5 us -> 70 us  [on_device(): gathered = lax.all_gather(received, 'tmpl', axis=0)]
    all_gather x0 -> x1, local copies, waits for them, and re-layouts: none -> 28.4 us  [on_device(): gathered = lax.all_gather(received, 'tmpl', axis=0)]
    unnamed x16 -> x11, local copies, waits for them, and re-layouts: 26.2 us -> 6.55 us
    all_to_all x3, waiting for transfers between devices: 35.7 us -> 51.9 us  [the longest x1 28.4 us: spectrum_blocks(): lax.all_to_all(twisted, FREQ, 0, 0, tiled=True)]
    dot_general x1 -> x3, matrix products: 9.19 us -> 21.9 us  [the longest x1 10.1 us: spectrum_blocks(): jnp.dot(second_sin, columns, precision=highest)]
    all_to_all x5 -> x1, local copies, waits for them, and re-layouts: 13.8 us -> 1.73 us  [spectrum_blocks(): return lax.all_to_all(whitened, FREQ, 0, 0, tiled=True)]
    reshape x4 -> x7, local copies, waits for them, and re-layouts: 23.4 us -> 33.5 us  [the longest x1 24.5 us: on_device(): gathered.transpose(2, 3, 0, 5, 1, 4)]
    sin x1 -> x0, other arithmetic: 9.11 us -> none  [cos_sin_table(): return (jnp.cos(phase_angle), jnp.sin(phase_angle))]
  transfers between devices with their start and end apart: 4 -> 4, of which waited for: 4 -> 4; matrix products, arithmetic and copies ran while one was open for 12% -> 5% of each run, Pallas kernels for 0% -> 0%
where the time goes in v5:
time: 358 us; the launch traced here: 355 us
  waiting for transfers between devices  122 us (34%)
  local copies, waits for them, and re-layouts  89.5 us (25%)
  Pallas kernels  62.6 us (17%)
  starting transfers between devices  26.4 us (7%)
  matrix products  21.9 us (6%)
  other arithmetic  18.8 us (5%)
  between operations  13.9 us (4%)
    all_gather x1, waiting for transfers between devices, on_device(): gathered = lax.all_gather(received, 'tmpl', axis=0)  70 us
    pallas_call x3, Pallas kernels, scatter_sum(): pl.pallas_call(functools.partial(scatter_kernel, axis, size), out_shape=j...  43.9 us
    all_to_all x1, waiting for transfers between devices, spectrum_blocks(): lax.all_to_all(twisted, FREQ, 0, 0, tiled=True)  28.4 us
    all_gather x1, local copies, waits for them, and re-layouts, on_device(): gathered = lax.all_gather(received, 'tmpl', axis=0)  28.4 us
    reshape x1, local copies, waits for them, and re-layouts, on_device(): gathered.transpose(2, 3, 0, 5, 1, 4)  24.5 us
    pallas_call x1, Pallas kernels, intersect(): pl.pallas_call(intersect_kernel, out_shape=jax.ShapeDtypeStruct((seg_coun...  18.7 us
    all_to_all x1, starting transfers between devices, spectrum_blocks(): lax.all_to_all(sent, FREQ, 0, 0, tiled=True)  13.6 us
    another operation x4, local copies, waits for them, and re-layouts, spectrum_blocks(): jnp.stack([real_part * twist_cos + imag_part * twist_sin, imag_part * twi...  12.5 us
  transfers between devices with their start and end apart: 4, of which 4 were waited for; matrix products, arithmetic and copies ran while one was open for 5% of the time, Pallas kernels for 0%

profile of v5, /device:TPU:1, one launch (start us, length us, event | category | flops | bytes accessed | tf_op | source)
XLA Modules:
  0.0 355.0 jit_solution(12889159479339870095)
XLA Ops:
  6.5 3.7 %reshape.200 = f32[16,8,64,16]{3,2,1,0:T(8,128)} reshape(f32[16,8192]{1,0:T(8,128)} %param.5) | data formatting | bytes 1048576 | tf_op jit(solution)/shard_map/reshape | solution.py:156
  10.3 2.9 copy.73
  13.1 1.2 copy.74
  14.3 13.6 %all-to-all-start = ((f32[64,8,256]{2,1,0:T(8,128)}), f32[64,8,256]{2,1,0:T(8,128)S(1)}, u32[]{:S(2)}, u32[]{:S(2)}) async-start(f32[64,8,256]{2,1,0:T(8,128)} %copy.74), calls=%async_computation | async-start | bytes 1048576 | tf_op jit(solution)/shard_map/all_to_all | solution.py:158
  27.9 0.2 fusion.47
  28.1 0.1 broadcast_in_dim.11
  28.1 0.2 copy.75
  28.4 0.1 broadcast_in_dim.12
  28.4 1.0 copy.76
  29.4 4.1 %sine_negate_fusion = (f32[512,512]{1,0:T(8,128)S(1)}, f32[512,512]{1,0:T(8,128)S(1)}) fusion(), kind=kLoop, calls=%fused_computation.29 | loop fusion | flops 3932160 | bytes 2097152 | tf_op jit(solution)/shard_map/neg | solution.py:155
  33.5 11.5 %all-to-all-done = f32[64,8,256]{2,1,0:T(8,128)S(1)} async-done(((f32[64,8,256]{2,1,0:T(8,128)}), f32[64,8,256]{2,1,0:T(8,128)S(1)}, u32[]{:S(2)}, u32[]{:S(2)}) %all-to-all-start) | async-done | bytes 524320 | tf_op jit(solution)/shard_map/all_to_all | solution.py:158
  45.0 0.0 copy-start
  45.0 1.8 fusion.4
  46.9 0.0 copy-done
  46.9 0.1 multiply_add_fusion
  47.0 2.6 stack.24
  49.7 3.6 %copy.79 = f32[1,64,8,16,16]{1,4,3,2,0:T(8,128)S(1)} copy(f32[1,64,8,16,16]{4,3,2,1,0:T(8,128)} %stack.24) | data formatting | bytes 1048576 | tf_op jit(solution)/shard_map/stack | solution.py:166
  53.3 2.6 stack.25
  55.9 3.6 %copy.80 = f32[1,64,8,16,16]{1,4,3,2,0:T(8,128)S(1)} copy(f32[1,64,8,16,16]{4,3,2,1,0:T(8,128)} %stack.25) | data formatting | bytes 1048576 | tf_op jit(solution)/shard_map/stack | solution.py:166
  59.6 0.2 maximum_bitcast_fusion
  59.7 0.2 copy.81
  60.0 0.0 copy-start.1
  60.0 1.8 copy.82
  61.8 6.6 %all-to-all-start.1 = ((f32[64,16,256]{2,1,0:T(8,128)}), f32[64,16,256]{2,1,0:T(8,128)S(1)}, u32[]{:S(2)}, u32[]{:S(2)}) async-start(f32[64,16,256]{2,1,0:T(8,128)} %copy.82), calls=%async_computation.1 | async-start | bytes 2097152 | tf_op jit(solution)/shard_map/all_to_all | solution.py:172
  68.3 0.0 copy-done.1
  68.3 28.4 %all-to-all-done.1 = f32[64,16,256]{2,1,0:T(8,128)S(1)} async-done(((f32[64,16,256]{2,1,0:T(8,128)}), f32[64,16,256]{2,1,0:T(8,128)S(1)}, u32[]{:S(2)}, u32[]{:S(2)}) %all-to-all-start.1) | async-done | bytes 1048608 | tf_op jit(solution)/shard_map/all_to_all | solution.py:172
  96.7 0.3 copy.83
  97.1 10.0 %fusion.10 = f32[512,2,8,16]{0,3,2,1:T(8,128)S(1)} fusion(f32[2,8,16,1024]{3,2,1,0:T(8,128)S(1)} %bitcast.54), kind=kOutput, calls=%fused_computation.16 | convolution fusion | flops 1617952768 | bytes 1572864 | tf_op jit(solution)/shard_map/dot_general | solution.py:176
  107.1 10.1 %fusion.8 = f32[512,2,8,16]{0,3,2,1:T(8,128)S(1)} fusion(f32[2,8,16,1024]{3,2,1,0:T(8,128)S(1)} %bitcast.55), kind=kOutput, calls=%fused_computation.14 | convolution fusion | flops 1617952768 | bytes 1572864 | tf_op jit(solution)/shard_map/dot_general | solution.py:177
  117.2 0.1 fusion.33
  117.4 0.8 copy.84
  118.1 1.7 copy.85
  119.8 2.0 copy_bitcast_fusion
  121.8 2.9 reshape.212
  124.7 6.2 %all-to-all-start.2 = ((bf16[64,2,1024]{2,1,0:T(2,128)(2,1)}), bf16[64,2,1024]{2,1,0:T(2,128)(2,1)S(1)}, u32[]{:S(2)}, u32[]{:S(2)}) async-start(bf16[64,2,1024]{2,1,0:T(2,128)(2,1)} %reshape.212), calls=%async_computation.2 | async-start | bytes 524288 | tf_op jit(solution)/shard_map/all_to_all | solution.py:184
  130.9 0.0 all-gather.3.cloned.1.call-start
  131.0 12.0 %all-to-all-done.2 = bf16[64,2,1024]{2,1,0:T(2,128)(2,1)S(1)} async-done(((bf16[64,2,1024]{2,1,0:T(2,128)(2,1)}), bf16[64,2,1024]{2,1,0:T(2,128)(2,1)S(1)}, u32[]{:S(2)}, u32[]{:S(2)}) %all-to-all-start.2) | async-done | bytes 262176 | tf_op jit(solution)/shard_map/all_to_all | solution.py:184
  142.9 1.6 reshape.213
  144.6 1.7 copy.87
  146.3 0.0 copy-start.2
  146.3 0.0 copy-start.3
  146.3 0.0 all-gather.3.cloned.1.call-update
  146.4 0.6 copy-done.2
  147.0 0.1 fusion.48
  147.0 0.1 add_select_fusion.5
  147.1 1.1 fusion.35
  148.2 0.9 maximum_bitcast_fusion.1.ph_ref
  149.1 0.0 copy-done.3
  149.1 0.1 broadcast_compare_fusion
  149.2 9.9 %fusion.tm_ref = bf16[8,2,256,512]{3,2,1,0:T(8,128)(2,1)} fusion(bf16[256,2,8,512]{3,2,1,0:T(8,128)(2,1)} %param.7, pred[256,8]{0,1:T(8,128)(4,1)S(1)} %broadcast_compare_fusion), kind=kLoop, calls=%fused_computation.1 | loop fusion | flops 2097152 | bytes 8390656 | tf_op jit(solution)/shard_map/transpose | solution.py:76
  159.1 70.0 %all-gather.3.cloned.1.call-done = bf16[256,8,2,8,16]{4,3,2,1,0:T(8,128)(2,1)} async-done(((bf16[64,8,2,8,16]{4,3,2,1,0:T(8,128)(2,1)}), bf16[256,8,2,8,16]{4,3,2,1,0:T(8,128)(2,1)}) %all-gather.3.cloned.1.call-update) | async-done | bytes 1048592 | tf_op jit(solution)/shard_map/all_gather | solution.py:191
  229.0 28.4 %copy.88 = bf16[4,64,8,2,8,16]{4,1,2,5,0,3:T(8,128)(2,1)} copy(bf16[4,64,8,2,8,16]{5,4,3,2,1,0:T(8,128)(2,1)} %bitcast.44) | data formatting | bytes 2097152 | tf_op jit(solution)/shard_map/all_gather | solution.py:191
  257.4 24.5 %reshape.207 = bf16[8,2,4,8,2,512]{5,0,4,3,2,1:T(8,128)(2,1)S(1)} reshape(bf16[8,2,4,16,64,8]{5,4,0,3,2,1:T(8,128)(2,1)} %bitcast.42) | data formatting | bytes 2097152 | tf_op jit(solution)/shard_map/reshape | solution.py:194
  282.0 0.8 copy.89
  282.8 1.1 reshape.208.dat_ref
  283.9 18.7 %shard_map.55.x_ref = f32[64,32,256]{2,1,0:T(8,128)} custom-call(f32[8,2,16,512]{3,2,1,0:T(8,128)} %maximum_bitcast_fusion.1.ph_ref, bf16[8,2,64,512]{3,2,1,0:T(8,128)(2,1)} %reshape.208.dat_ref, bf16[8,2,256,512]{3,2,1,0:T(8,128)(2,1)} %fusion.tm_ref), custom_call_target="tpu_custom_call" | custom-call | flops 8589934592 | bytes 7864320 | tf_op jit(solution)/shard_map/pallas_call | solution.py:80
  302.6 5.7 %shard_map.56.x_ref = f32[32,32,256]{2,1,0:T(8,128)} custom-call(f32[64,32,256]{2,1,0:T(8,128)} %shard_map.55.x_ref), custom_call_target="tpu_custom_call" | custom-call | tf_op jit(solution)/shard_map/pallas_call | solution.py:131
  308.2 31.3 %shard_map.57.x_ref = f32[4,32,256]{2,1,0:T(8,128)} custom-call(f32[32,32,256]{2,1,0:T(8,128)} %shard_map.56.x_ref), custom_call_target="tpu_custom_call" | custom-call | tf_op jit(solution)/shard_map/pallas_call | solution.py:131
  339.5 7.0 %shard_map.58 = f32[1,32,256]{2,1,0:T(8,128)} custom-call(f32[4,32,256]{2,1,0:T(8,128)} %shard_map.57.x_ref), custom_call_target="tpu_custom_call" | custom-call | tf_op jit(solution)/shard_map/pallas_call | solution.py:131
  346.5 1.4 copy.98
  (3 shorter events, 0.0 us)
Async XLA Ops:
  14.3 30.8 %all-to-all-start = ((f32[64,8,256]{2,1,0:T(8,128)}), f32[64,8,256]{2,1,0:T(8,128)S(1)}, u32[]{:S(2)}, u32[]{:S(2)}) async-start(f32[64,8,256]{2,1,0:T(8,128)} %copy.74), calls=%async_computation | async-start | bytes 1048576 | tf_op jit(solution)/shard_map/all_to_all | solution.py:158
  45.0 1.8 copy-start
  60.0 8.4 %copy-start.1 = (f32[512,8]{0,1:T(8,128)S(1)}, f32[512,8]{0,1:T(8,128)}, u32[]{:S(2)}) copy-start(f32[512,8]{0,1:T(8,128)} %param.6) | copy-start | bytes 49156
  61.8 35.0 %all-to-all-start.1 = ((f32[64,16,256]{2,1,0:T(8,128)}), f32[64,16,256]{2,1,0:T(8,128)S(1)}, u32[]{:S(2)}, u32[]{:S(2)}) async-start(f32[64,16,256]{2,1,0:T(8,128)} %copy.82), calls=%async_computation.1 | async-start | bytes 2097152 | tf_op jit(solution)/shard_map/all_to_all | solution.py:172
  124.7 18.2 %all-to-all-start.2 = ((bf16[64,2,1024]{2,1,0:T(2,128)(2,1)}), bf16[64,2,1024]{2,1,0:T(2,128)(2,1)S(1)}, u32[]{:S(2)}, u32[]{:S(2)}) async-start(bf16[64,2,1024]{2,1,0:T(2,128)(2,1)} %reshape.212), calls=%async_computation.2 | async-start | bytes 524288 | tf_op jit(solution)/shard_map/all_to_all | solution.py:184
  130.9 98.1 %all-gather.3.cloned.1.call-start = ((), (), s32[]{:S(2)}) async-start(), calls=%async_computation.3 | async-start | bytes 10485760 | tf_op jit(solution)/shard_map/all_gather | solution.py:191
  146.3 0.7 copy-start.2
  146.3 2.8 copy-start.3
Sparse Core Ops, SparseCore 0:
  146.5 82.5 all-gather.2

commit v6 on v5

--- a/solution.py
+++ b/solution.py
@@ -178,23 +178,19 @@
     amplitude = jnp.sqrt(LEN * psd)[:, :, None]
     real_out = (with_cos[:, 0] + with_sin[:, 1]) / amplitude
     imag_out = (with_cos[:, 1] - with_sin[:, 0]) / amplitude
-    whitened = jnp.stack([real_out, imag_out], axis=1).astype(jnp.bfloat16)
-    j_here = NB // freq_count
-    whitened = whitened.reshape(freq_count, j_here, 2, p_here, seg_local)
-    return lax.all_to_all(whitened, FREQ, 0, 0, tiled=True)
+    whitened = jnp.stack([real_out, imag_out], axis=1).transpose(3, 1, 0, 2).astype(jnp.bfloat16)
+    return lax.all_to_all(whitened, FREQ, split_axis=2, concat_axis=3, tiled=True)
 
 
 def on_device(strain, psd, templates, cutoffs, lags):
     freq_index = lax.axis_index(FREQ)
-    received = spectrum_blocks(strain, psd)
-    freq_count, j_here, _, p_here, seg_local = received.shape
-    gathered = lax.all_gather(received, "tmpl", axis=0)
-    tmpl_count = gathered.shape[0]
+    local_data = spectrum_blocks(strain, psd)
+    seg_piece = lax.all_gather(local_data, "tmpl", axis=0, tiled=True)
     x_size, z_size, c_size = (lax.axis_size(name) for name in FREQ)
-    data = gathered.transpose(2, 3, 0, 5, 1, 4).reshape(
-        j_here, 2, x_size, z_size, c_size, freq_count * p_here
-    )
-    data = data.transpose(0, 1, 4, 3, 2, 5).reshape(j_here, 2, tmpl_count * seg_local, -1)
+    seg_order = seg_piece.reshape((x_size, z_size, c_size) + seg_piece.shape[1:])
+    seg_order = seg_order.transpose(2, 1, 0, 3, 4, 5).reshape(seg_piece.shape)
+    data = seg_order.transpose(2, 1, 0, 3)
+    j_here = data.shape[0]
     first_block = freq_index * j_here
     partial_sums = intersect(data, templates, cutoffs, lags, first_block)
     for collective_id, name in enumerate(("fc", "fz", "fx")):

time: 358 us -> 247 us (0.69)
  waiting for transfers between devices: 122 us -> 62.5 us
  local copies, waits for them, and re-layouts: 89.5 us -> 39.5 us
    all_gather x1, waiting for transfers between devices: 70 us -> 10.6 us  [on_device(): seg_piece = lax.all_gather(local_data, 'tmpl', axis=0, tiled=True)]
    all_gather x1 -> x0, local copies, waits for them, and re-layouts: 28.4 us -> none  [on_device(): gathered = lax.all_gather(received, 'tmpl', axis=0)]
    reshape x2 -> x1, local copies, waits for them, and re-layouts: 25.6 us -> 1.14 us  [on_device(): seg_order = seg_order.transpose(2, 1, 0, 3, 4, 5).reshape(seg_piece.shape)]
  transfers between devices with their start and end apart: 4 -> 4, of which waited for: 4 -> 4; matrix products, arithmetic and copies ran while one was open for 5% -> 7% of each run, Pallas kernels for 0% -> 0%
where the time goes in v6:
time: 247 us; the launch traced here: 245 us
  Pallas kernels  63.5 us (26%)
  waiting for transfers between devices  62.5 us (25%)
  local copies, waits for them, and re-layouts  39.5 us (16%)
  starting transfers between devices  26.4 us (11%)
  matrix products  21.9 us (9%)
  other arithmetic  16.8 us (7%)
  between operations  13.9 us (6%)
    pallas_call x3, Pallas kernels, scatter_sum(): pl.pallas_call(functools.partial(scatter_kernel, axis, size), out_shape=j...  44.8 us
    all_to_all x1, waiting for transfers between devices, spectrum_blocks(): lax.all_to_all(twisted, FREQ, 0, 0, tiled=True)  28.4 us
    pallas_call x1, Pallas kernels, intersect(): pl.pallas_call(intersect_kernel, out_shape=jax.ShapeDtypeStruct((seg_coun...  18.7 us
    all_to_all x1, starting transfers between devices, spectrum_blocks(): lax.all_to_all(sent, FREQ, 0, 0, tiled=True)  13.6 us
    another operation x4, local copies, waits for them, and re-layouts, spectrum_blocks(): jnp.stack([real_part * twist_cos + imag_part * twist_sin, imag_part * twi...  12.5 us
    all_to_all x1, waiting for transfers between devices, spectrum_blocks(): lax.all_to_all(whitened, FREQ, split_axis=2, concat_axis=3, tiled=True)  12 us
    all_to_all x1, waiting for transfers between devices, spectrum_blocks(): lax.all_to_all(sent, FREQ, 0, 0, tiled=True)  11.5 us
    all_gather x1, waiting for transfers between devices, on_device(): seg_piece = lax.all_gather(local_data, 'tmpl', axis=0, tiled=True)  10.6 us
  transfers between devices with their start and end apart: 4, of which 4 were waited for; matrix products, arithmetic and copies ran while one was open for 7% of the time, Pallas kernels for 0%

profile of v6, /device:TPU:1, one launch (start us, length us, event | category | flops | bytes accessed | tf_op | source)
XLA Modules:
  0.0 244.5 jit_solution(7690752190306775383)
XLA Ops:
  6.5 3.7 %reshape.195 = f32[16,8,64,16]{3,2,1,0:T(8,128)} reshape(f32[16,8192]{1,0:T(8,128)} %param.5) | data formatting | bytes 1048576 | tf_op jit(solution)/shard_map/reshape | solution.py:156
  10.3 2.9 %copy.34 = f32[64,8,16,16]{0,3,2,1:T(8,128)S(1)} copy(f32[64,8,16,16]{2,0,1,3:T(8,128)} %bitcast.46) | data formatting | bytes 1048576 | tf_op jit(solution)/shard_map/transpose | solution.py:156
  13.1 1.2 copy.35
  14.3 13.6 %all-to-all-start = ((f32[64,8,256]{2,1,0:T(8,128)}), f32[64,8,256]{2,1,0:T(8,128)S(1)}, u32[]{:S(2)}, u32[]{:S(2)}) async-start(f32[64,8,256]{2,1,0:T(8,128)} %copy.35), calls=%async_computation | async-start | bytes 1048576 | tf_op jit(solution)/shard_map/all_to_all | solution.py:158
  27.9 0.2 fusion.47
  28.1 0.1 broadcast_in_dim.11
  28.1 0.2 copy.36
  28.4 0.1 broadcast_in_dim.12
  28.4 1.0 copy.37
  29.4 4.1 %sine_negate_fusion = (f32[512,512]{1,0:T(8,128)S(1)}, f32[512,512]{1,0:T(8,128)S(1)}) fusion(), kind=kLoop, calls=%fused_computation.29 | loop fusion | flops 3932160 | bytes 2097152 | tf_op jit(solution)/shard_map/neg | solution.py:155
  33.5 11.5 %all-to-all-done = f32[64,8,256]{2,1,0:T(8,128)S(1)} async-done(((f32[64,8,256]{2,1,0:T(8,128)}), f32[64,8,256]{2,1,0:T(8,128)S(1)}, u32[]{:S(2)}, u32[]{:S(2)}) %all-to-all-start) | async-done | bytes 524320 | tf_op jit(solution)/shard_map/all_to_all | solution.py:158
  45.0 0.0 copy-start
  45.0 1.8 fusion.4
  46.9 0.0 copy-done
  46.9 0.1 multiply_add_fusion
  47.0 2.6 %stack.21 = f32[1,64,8,16,16]{4,3,2,1,0:T(8,128)} reshape(f32[512,256]{1,0:T(8,128)S(1)} %get-tuple-element.5) | data formatting | bytes 1048576 | tf_op jit(solution)/shard_map/stack | solution.py:166
  49.7 3.6 %copy.40 = f32[1,64,8,16,16]{1,4,3,2,0:T(8,128)S(1)} copy(f32[1,64,8,16,16]{4,3,2,1,0:T(8,128)} %stack.21) | data formatting | bytes 1048576 | tf_op jit(solution)/shard_map/stack | solution.py:166
  53.3 2.6 %stack.22 = f32[1,64,8,16,16]{4,3,2,1,0:T(8,128)} reshape(f32[512,256]{1,0:T(8,128)S(1)} %get-tuple-element.6) | data formatting | bytes 1048576 | tf_op jit(solution)/shard_map/stack | solution.py:166
  55.9 3.6 %copy.41 = f32[1,64,8,16,16]{1,4,3,2,0:T(8,128)S(1)} copy(f32[1,64,8,16,16]{4,3,2,1,0:T(8,128)} %stack.22) | data formatting | bytes 1048576 | tf_op jit(solution)/shard_map/stack | solution.py:166
  59.6 0.2 maximum_bitcast_fusion
  59.7 0.2 copy.42
  60.0 0.0 copy-start.1
  60.0 1.8 copy.43
  61.8 6.6 %all-to-all-start.1 = ((f32[64,16,256]{2,1,0:T(8,128)}), f32[64,16,256]{2,1,0:T(8,128)S(1)}, u32[]{:S(2)}, u32[]{:S(2)}) async-start(f32[64,16,256]{2,1,0:T(8,128)} %copy.43), calls=%async_computation.1 | async-start | bytes 2097152 | tf_op jit(solution)/shard_map/all_to_all | solution.py:172
  68.3 0.0 copy-done.1
  68.3 28.4 %all-to-all-done.1 = f32[64,16,256]{2,1,0:T(8,128)S(1)} async-done(((f32[64,16,256]{2,1,0:T(8,128)}), f32[64,16,256]{2,1,0:T(8,128)S(1)}, u32[]{:S(2)}, u32[]{:S(2)}) %all-to-all-start.1) | async-done | bytes 1048608 | tf_op jit(solution)/shard_map/all_to_all | solution.py:172
  96.7 0.3 copy.44
  97.1 10.0 %fusion.10 = f32[512,2,8,16]{0,3,2,1:T(8,128)S(1)} fusion(f32[2,8,16,1024]{3,2,1,0:T(8,128)S(1)} %bitcast.57), kind=kOutput, calls=%fused_computation.15 | convolution fusion | flops 1617952768 | bytes 1572864 | tf_op jit(solution)/shard_map/dot_general | solution.py:176
  107.1 10.1 %fusion.8 = f32[512,2,8,16]{0,3,2,1:T(8,128)S(1)} fusion(f32[2,8,16,1024]{3,2,1,0:T(8,128)S(1)} %bitcast.58), kind=kOutput, calls=%fused_computation.13 | convolution fusion | flops 1617952768 | bytes 1572864 | tf_op jit(solution)/shard_map/dot_general | solution.py:177
  117.2 0.1 fusion.33
  117.4 2.0 copy.45
  119.4 3.1 %reshape.206 = bf16[64,2,1024]{2,1,0:T(2,128)(2,1)} reshape(bf16[512,2,8,16]{3,2,1,0:T(8,128)(2,1)S(1)} %bitcast.47) | data formatting | bytes 524288
  122.5 6.2 %all-to-all-start.2 = ((bf16[64,2,1024]{2,1,0:T(2,128)(2,1)}), bf16[64,2,1024]{2,1,0:T(2,128)(2,1)S(1)}, u32[]{:S(2)}, u32[]{:S(2)}) async-start(bf16[64,2,1024]{2,1,0:T(2,128)(2,1)} %reshape.206), calls=%async_computation.2 | async-start | bytes 524288 | tf_op jit(solution)/shard_map/all_to_all | solution.py:182
  128.7 0.0 all-gather.2.cloned.1.call-start
  128.7 12.0 %all-to-all-done.2 = bf16[64,2,1024]{2,1,0:T(2,128)(2,1)S(1)} async-done(((bf16[64,2,1024]{2,1,0:T(2,128)(2,1)}), bf16[64,2,1024]{2,1,0:T(2,128)(2,1)S(1)}, u32[]{:S(2)}, u32[]{:S(2)}) %all-to-all-start.2) | async-done | bytes 262176 | tf_op jit(solution)/shard_map/all_to_all | solution.py:182
  140.7 1.4 reshape.207
  142.1 1.9 copy.58
  144.0 0.0 copy-start.2
  144.0 0.0 copy-start.3
  144.0 2.6 %copy.48 = bf16[16,2,8,512]{3,2,1,0:T(8,128)(2,1)} copy(bf16[16,2,8,512]{0,3,2,1:T(8,128)(2,1)} %bitcast.50) | data formatting | bytes 524288 | tf_op jit(solution)/shard_map/all_to_all | solution.py:182
  146.7 0.0 all-gather.2.cloned.1.call-update
  146.7 0.0 copy-done.2
  146.7 0.1 fusion.48
  146.8 0.1 add_select_fusion.5
  146.9 1.1 fusion.35
  148.0 0.8 maximum_bitcast_fusion.1.ph_ref
  148.8 0.0 copy-done.3
  148.8 0.1 broadcast_compare_fusion
  148.9 9.9 %fusion.tm_ref = bf16[8,2,256,512]{3,2,1,0:T(8,128)(2,1)} fusion(bf16[256,2,8,512]{3,2,1,0:T(8,128)(2,1)} %param.7, pred[256,8]{0,1:T(8,128)(4,1)S(1)} %broadcast_compare_fusion), kind=kLoop, calls=%fused_computation.1 | loop fusion | flops 2097152 | bytes 8390656 | tf_op jit(solution)/shard_map/transpose | solution.py:76
  158.8 10.6 %all-gather.2.cloned.1.call-done = bf16[64,2,8,512]{3,2,1,0:T(8,128)(2,1)} async-done(((bf16[16,2,8,512]{3,2,1,0:T(8,128)(2,1)}), bf16[64,2,8,512]{3,2,1,0:T(8,128)(2,1)}) %all-gather.2.cloned.1.call-update) | async-done | bytes 1048592 | tf_op jit(solution)/shard_map/all_gather | solution.py:188
  169.3 2.0 copy.49
  171.4 1.1 reshape.203
  172.5 18.7 %shard_map.55.x_ref = f32[64,32,256]{2,1,0:T(8,128)} custom-call(f32[8,2,16,512]{3,2,1,0:T(8,128)} %maximum_bitcast_fusion.1.ph_ref, bf16[8,2,64,512]{3,2,1,0:T(8,128)(2,1)} %bitcast.56, bf16[8,2,256,512]{3,2,1,0:T(8,128)(2,1)} %fusion.tm_ref), custom_call_target="tpu_custom_call" | custom-call | flops 8589934592 | bytes 7864320 | tf_op jit(solution)/shard_map/pallas_call | solution.py:80
  191.2 6.6 %shard_map.56.x_ref = f32[32,32,256]{2,1,0:T(8,128)} custom-call(f32[64,32,256]{2,1,0:T(8,128)} %shard_map.55.x_ref), custom_call_target="tpu_custom_call" | custom-call | tf_op jit(solution)/shard_map/pallas_call | solution.py:131
  197.8 31.3 %shard_map.57.x_ref = f32[4,32,256]{2,1,0:T(8,128)} custom-call(f32[32,32,256]{2,1,0:T(8,128)} %shard_map.56.x_ref), custom_call_target="tpu_custom_call" | custom-call | tf_op jit(solution)/shard_map/pallas_call | solution.py:131
  229.1 7.0 %shard_map.58 = f32[1,32,256]{2,1,0:T(8,128)} custom-call(f32[4,32,256]{2,1,0:T(8,128)} %shard_map.57.x_ref), custom_call_target="tpu_custom_call" | custom-call | tf_op jit(solution)/shard_map/pallas_call | solution.py:131
  236.1 1.4 copy.60
  (4 shorter events, 0.0 us)
Async XLA Ops:
  14.3 30.8 %all-to-all-start = ((f32[64,8,256]{2,1,0:T(8,128)}), f32[64,8,256]{2,1,0:T(8,128)S(1)}, u32[]{:S(2)}, u32[]{:S(2)}) async-start(f32[64,8,256]{2,1,0:T(8,128)} %copy.35), calls=%async_computation | async-start | bytes 1048576 | tf_op jit(solution)/shard_map/all_to_all | solution.py:158
  45.0 1.8 copy-start
  60.0 8.4 %copy-start.1 = (f32[512,8]{0,1:T(8,128)S(1)}, f32[512,8]{0,1:T(8,128)}, u32[]{:S(2)}) copy-start(f32[512,8]{0,1:T(8,128)} %param.6) | copy-start | bytes 49156
  61.8 35.0 %all-to-all-start.1 = ((f32[64,16,256]{2,1,0:T(8,128)}), f32[64,16,256]{2,1,0:T(8,128)S(1)}, u32[]{:S(2)}, u32[]{:S(2)}) async-start(f32[64,16,256]{2,1,0:T(8,128)} %copy.43), calls=%async_computation.1 | async-start | bytes 2097152 | tf_op jit(solution)/shard_map/all_to_all | solution.py:172
  122.5 18.2 %all-to-all-start.2 = ((bf16[64,2,1024]{2,1,0:T(2,128)(2,1)}), bf16[64,2,1024]{2,1,0:T(2,128)(2,1)S(1)}, u32[]{:S(2)}, u32[]{:S(2)}) async-start(bf16[64,2,1024]{2,1,0:T(2,128)(2,1)} %reshape.206), calls=%async_computation.2 | async-start | bytes 524288 | tf_op jit(solution)/shard_map/all_to_all | solution.py:182
  128.7 40.6 %all-gather.2.cloned.1.call-start = ((), (), s32[]{:S(2)}) async-start(), calls=%async_computation.3 | async-start | bytes 1310720 | tf_op jit(solution)/shard_map/all_gather | solution.py:188
  144.0 2.7 %copy-start.2 = (s32[16]{0:T(128)S(1)}, s32[16]{0:T(128)}, u32[]{:S(2)}) copy-start(s32[16]{0:T(128)} %param.9) | copy-start | bytes 196
  144.0 4.8 %copy-start.3 = (s32[256]{0:T(256)S(1)}, s32[256]{0:T(256)}, u32[]{:S(2)}) copy-start(s32[256]{0:T(256)} %param.8) | copy-start | bytes 3076
Sparse Core Ops, SparseCore 0:
  146.8 22.4 all-gather.1

commit v7 on v6

--- a/solution.py
+++ b/solution.py
@@ -170,9 +170,16 @@
     twisted = twisted.reshape(2, freq_count, p_here, cols_here, seg_local).transpose(1, 3, 0, 2, 4)
     twisted = twisted.reshape(freq_count, cols_here, 2 * p_here * seg_local)
     columns = lax.all_to_all(twisted, FREQ, 0, 0, tiled=True).reshape(B, 2 * p_here * seg_local)
-    second_cos, second_sin = cos_sin_table(
-        jnp.arange(NB, dtype=jnp.int32), jnp.arange(B, dtype=jnp.int32), B
-    )
+    split = 32
+    j_ids = jnp.arange(NB, dtype=jnp.int32)
+    high_cos, high_sin = cos_sin_table(j_ids, split * jnp.arange(B // split, dtype=jnp.int32), B)
+    low_cos, low_sin = cos_sin_table(j_ids, jnp.arange(split, dtype=jnp.int32), B)
+    second_cos = (
+        high_cos[:, :, None] * low_cos[:, None, :] - high_sin[:, :, None] * low_sin[:, None, :]
+    ).reshape(NB, B)
+    second_sin = (
+        high_sin[:, :, None] * low_cos[:, None, :] + high_cos[:, :, None] * low_sin[:, None, :]
+    ).reshape(NB, B)
     with_cos = jnp.dot(second_cos, columns, precision=highest).reshape(NB, 2, p_here, seg_local)
     with_sin = jnp.dot(second_sin, columns, precision=highest).reshape(NB, 2, p_here, seg_local)
     amplitude = jnp.sqrt(LEN * psd)[:, :, None]

time: 247 us -> 231 us (0.935)
  matrix products: 21.9 us -> 7.78 us
  waiting for transfers between devices: 62.5 us -> 59.8 us
  other arithmetic: 16.8 us -> 19.4 us
    dot_general x1, matrix products: 10.1 us -> 2.04 us  [spectrum_blocks(): jnp.dot(second_sin, columns, precision=highest)]
    dot_general x1, matrix products: 10 us -> 3.93 us  [spectrum_blocks(): jnp.dot(second_cos, columns, precision=highest)]
    unnamed x11 -> x13, local copies, waits for them, and re-layouts: 5.95 us -> 5.75 us
  transfers between devices with their start and end apart: 4 -> 4, of which waited for: 4 -> 4; matrix products, arithmetic and copies ran while one was open for 7% -> 9% of each run, Pallas kernels for 0% -> 0%
where the time goes in v7:
time: 231 us; the launch traced here: 230 us
  Pallas kernels  63.5 us (27%)
  waiting for transfers between devices  59.8 us (26%)
  local copies, waits for them, and re-layouts  40.2 us (17%)
  starting transfers between devices  25.8 us (11%)
  other arithmetic  19.4 us (8%)
  between operations  13.7 us (6%)
  matrix products  7.78 us (3%)
    pallas_call x3, Pallas kernels, scatter_sum(): pl.pallas_call(functools.partial(scatter_kernel, axis, size), out_shape=j...  44.8 us
    all_to_all x1, waiting for transfers between devices, spectrum_blocks(): lax.all_to_all(twisted, FREQ, 0, 0, tiled=True)  25.9 us
    pallas_call x1, Pallas kernels, intersect(): pl.pallas_call(intersect_kernel, out_shape=jax.ShapeDtypeStruct((seg_coun...  18.7 us
    all_to_all x1, starting transfers between devices, spectrum_blocks(): lax.all_to_all(sent, FREQ, 0, 0, tiled=True)  13 us
    another operation x4, local copies, waits for them, and re-layouts, spectrum_blocks(): jnp.stack([real_part * twist_cos + imag_part * twist_sin, imag_part * twi...  12.5 us
    all_to_all x1, waiting for transfers between devices, spectrum_blocks(): lax.all_to_all(whitened, FREQ, split_axis=2, concat_axis=3, tiled=True)  11.7 us
    all_to_all x1, waiting for transfers between devices, spectrum_blocks(): lax.all_to_all(sent, FREQ, 0, 0, tiled=True)  11.6 us
    all_gather x1, waiting for transfers between devices, on_device(): seg_piece = lax.all_gather(local_data, 'tmpl', axis=0, tiled=True)  10.5 us
  transfers between devices with their start and end apart: 4, of which 4 were waited for; matrix products, arithmetic and copies ran while one was open for 9% of the time, Pallas kernels for 0%

profile of v7, /device:TPU:1, one launch (start us, length us, event | category | flops | bytes accessed | tf_op | source)
XLA Modules:
  0.0 230.2 jit_solution(4023655525021187125)
XLA Ops:
  6.5 3.7 %reshape.326 = f32[16,8,64,16]{3,2,1,0:T(8,128)} reshape(f32[16,8192]{1,0:T(8,128)} %param.5) | data formatting | bytes 1048576 | tf_op jit(solution)/shard_map/reshape | solution.py:156
  10.2 2.9 %copy.38 = f32[64,8,16,16]{0,3,2,1:T(8,128)S(1)} copy(f32[64,8,16,16]{2,0,1,3:T(8,128)} %bitcast.44) | data formatting | bytes 1048576 | tf_op jit(solution)/shard_map/transpose | solution.py:156
  13.1 1.1 copy.39
  14.2 13.0 %all-to-all-start = ((f32[64,8,256]{2,1,0:T(8,128)}), f32[64,8,256]{2,1,0:T(8,128)S(1)}, u32[]{:S(2)}, u32[]{:S(2)}) async-start(f32[64,8,256]{2,1,0:T(8,128)} %copy.39), calls=%async_computation | async-start | bytes 1048576 | tf_op jit(solution)/shard_map/all_to_all | solution.py:158
  27.3 0.2 fusion.49
  27.5 0.1 broadcast_in_dim.11
  27.5 0.2 copy.40
  27.7 0.1 broadcast_in_dim.12
  27.8 1.0 copy.41
  28.8 4.1 %sine_negate_fusion = (f32[512,512]{1,0:T(8,128)S(1)}, f32[512,512]{1,0:T(8,128)S(1)}) fusion(), kind=kLoop, calls=%fused_computation.16 | loop fusion | flops 3932160 | bytes 2097152 | tf_op jit(solution)/shard_map/neg | solution.py:155
  32.9 11.6 %all-to-all-done = f32[64,8,256]{2,1,0:T(8,128)S(1)} async-done(((f32[64,8,256]{2,1,0:T(8,128)}), f32[64,8,256]{2,1,0:T(8,128)S(1)}, u32[]{:S(2)}, u32[]{:S(2)}) %all-to-all-start) | async-done | bytes 524320 | tf_op jit(solution)/shard_map/all_to_all | solution.py:158
  44.6 0.0 copy-start
  44.6 1.8 fusion.1
  46.4 0.0 copy-done
  46.4 0.1 multiply_add_fusion.1
  46.5 2.6 %stack.21 = f32[1,64,8,16,16]{4,3,2,1,0:T(8,128)} reshape(f32[512,256]{1,0:T(8,128)S(1)} %get-tuple-element.5) | data formatting | bytes 1048576 | tf_op jit(solution)/shard_map/stack | solution.py:166
  49.2 3.6 %copy.44 = f32[1,64,8,16,16]{1,4,3,2,0:T(8,128)S(1)} copy(f32[1,64,8,16,16]{4,3,2,1,0:T(8,128)} %stack.21) | data formatting | bytes 1048576 | tf_op jit(solution)/shard_map/stack | solution.py:166
  52.8 2.6 %stack.22 = f32[1,64,8,16,16]{4,3,2,1,0:T(8,128)} reshape(f32[512,256]{1,0:T(8,128)S(1)} %get-tuple-element.6) | data formatting | bytes 1048576 | tf_op jit(solution)/shard_map/stack | solution.py:166
  55.4 3.6 %copy.45 = f32[1,64,8,16,16]{1,4,3,2,0:T(8,128)S(1)} copy(f32[1,64,8,16,16]{4,3,2,1,0:T(8,128)} %stack.22) | data formatting | bytes 1048576 | tf_op jit(solution)/shard_map/stack | solution.py:166
  59.0 0.2 maximum_bitcast_fusion
  59.2 0.2 copy.46
  59.4 0.0 copy-start.2
  59.5 1.8 copy.47
  61.2 6.3 %all-to-all-start.1 = ((f32[64,16,256]{2,1,0:T(8,128)}), f32[64,16,256]{2,1,0:T(8,128)S(1)}, u32[]{:S(2)}, u32[]{:S(2)}) async-start(f32[64,16,256]{2,1,0:T(8,128)} %copy.47), calls=%async_computation.1 | async-start | bytes 2097152 | tf_op jit(solution)/shard_map/all_to_all | solution.py:172
  67.5 0.3 fusion.40
  67.8 0.0 copy-done.2
  67.8 0.3 fusion.43
  68.2 1.9 multiply_subtract_fusion
  70.1 25.9 %all-to-all-done.1 = f32[64,16,256]{2,1,0:T(8,128)S(1)} async-done(((f32[64,16,256]{2,1,0:T(8,128)}), f32[64,16,256]{2,1,0:T(8,128)S(1)}, u32[]{:S(2)}, u32[]{:S(2)}) %all-to-all-start.1) | async-done | bytes 1048608 | tf_op jit(solution)/shard_map/all_to_all | solution.py:172
  96.1 1.3 copy.48
  97.4 0.0 copy-start.1
  97.4 3.9 %fusion.53 = f32[512,2,8,16]{0,3,2,1:T(8,128)S(1)} fusion(f32[512,1024,1,1]{0,1,3,2:T(8,128)} %bitcast.52, f32[2,8,16,1024]{3,2,1,0:T(8,128)} %bitcast.56), kind=kOutput, calls=%fused_computation.95 | convolution fusion | flops 1610612736 | bytes 3670016 | tf_op jit(solution)/shard_map/dot_general | solution.py:183
  101.3 0.0 copy-done.1
  101.3 2.0 fusion.54
  103.4 0.1 fusion.19
  103.5 2.0 copy.51
  105.5 2.9 %reshape.337 = bf16[64,2,1024]{2,1,0:T(2,128)(2,1)} reshape(bf16[512,2,8,16]{3,2,1,0:T(8,128)(2,1)S(1)} %bitcast.45) | data formatting | bytes 524288
  108.4 6.2 %all-to-all-start.2 = ((bf16[64,2,1024]{2,1,0:T(2,128)(2,1)}), bf16[64,2,1024]{2,1,0:T(2,128)(2,1)S(1)}, u32[]{:S(2)}, u32[]{:S(2)}) async-start(bf16[64,2,1024]{2,1,0:T(2,128)(2,1)} %reshape.337), calls=%async_computation.2 | async-start | bytes 524288 | tf_op jit(solution)/shard_map/all_to_all | solution.py:189
  114.6 0.3 all-gather.2.cloned.1.call-start
  114.9 11.7 %all-to-all-done.2 = bf16[64,2,1024]{2,1,0:T(2,128)(2,1)S(1)} async-done(((bf16[64,2,1024]{2,1,0:T(2,128)(2,1)}), bf16[64,2,1024]{2,1,0:T(2,128)(2,1)S(1)}, u32[]{:S(2)}, u32[]{:S(2)}) %all-to-all-start.2) | async-done | bytes 262176 | tf_op jit(solution)/shard_map/all_to_all | solution.py:189
  126.6 1.4 reshape.338
  128.1 1.9 copy.66
  129.9 0.0 copy-start.3
  129.9 0.0 copy-start.4
  129.9 2.6 %copy.54 = bf16[16,2,8,512]{3,2,1,0:T(8,128)(2,1)} copy(bf16[16,2,8,512]{0,3,2,1:T(8,128)(2,1)} %bitcast.48) | data formatting | bytes 524288 | tf_op jit(solution)/shard_map/all_to_all | solution.py:189
  132.6 0.0 all-gather.2.cloned.1.call-update
  132.6 0.0 copy-done.3
  132.6 0.1 fusion.50
  132.7 0.1 add_select_fusion.6
  132.8 1.1 fusion.21
  133.9 0.9 maximum_bitcast_fusion.1.ph_ref
  134.8 0.0 copy-done.4
  134.8 0.1 broadcast_compare_fusion
  134.8 9.9 %fusion.tm_ref = bf16[8,2,256,512]{3,2,1,0:T(8,128)(2,1)} fusion(bf16[256,2,8,512]{3,2,1,0:T(8,128)(2,1)} %param.7, pred[256,8]{0,1:T(8,128)(4,1)S(1)} %broadcast_compare_fusion), kind=kLoop, calls=%fused_computation.1 | loop fusion | flops 2097152 | bytes 8390656 | tf_op jit(solution)/shard_map/transpose | solution.py:76
  144.7 10.5 %all-gather.2.cloned.1.call-done = bf16[64,2,8,512]{3,2,1,0:T(8,128)(2,1)} async-done(((bf16[16,2,8,512]{3,2,1,0:T(8,128)(2,1)}), bf16[64,2,8,512]{3,2,1,0:T(8,128)(2,1)}) %all-gather.2.cloned.1.call-update) | async-done | bytes 1048592 | tf_op jit(solution)/shard_map/all_gather | solution.py:195
  155.3 2.0 copy.55
  157.3 1.1 reshape.334
  158.4 18.7 %shard_map.55.x_ref = f32[64,32,256]{2,1,0:T(8,128)} custom-call(f32[8,2,16,512]{3,2,1,0:T(8,128)} %maximum_bitcast_fusion.1.ph_ref, bf16[8,2,64,512]{3,2,1,0:T(8,128)(2,1)} %bitcast.58, bf16[8,2,256,512]{3,2,1,0:T(8,128)(2,1)} %fusion.tm_ref), custom_call_target="tpu_custom_call" | custom-call | flops 8589934592 | bytes 7864320 | tf_op jit(solution)/shard_map/pallas_call | solution.py:80
  177.1 6.6 %shard_map.56.x_ref = f32[32,32,256]{2,1,0:T(8,128)} custom-call(f32[64,32,256]{2,1,0:T(8,128)} %shard_map.55.x_ref), custom_call_target="tpu_custom_call" | custom-call | tf_op jit(solution)/shard_map/pallas_call | solution.py:131
  183.7 31.3 %shard_map.57.x_ref = f32[4,32,256]{2,1,0:T(8,128)} custom-call(f32[32,32,256]{2,1,0:T(8,128)} %shard_map.56.x_ref), custom_call_target="tpu_custom_call" | custom-call | tf_op jit(solution)/shard_map/pallas_call | solution.py:131
  215.0 7.0 %shard_map.58 = f32[1,32,256]{2,1,0:T(8,128)} custom-call(f32[4,32,256]{2,1,0:T(8,128)} %shard_map.57.x_ref), custom_call_target="tpu_custom_call" | custom-call | tf_op jit(solution)/shard_map/pallas_call | solution.py:131
  222.0 1.4 copy.68
  (5 shorter events, 0.1 us)
Async XLA Ops:
  14.2 30.3 %all-to-all-start = ((f32[64,8,256]{2,1,0:T(8,128)}), f32[64,8,256]{2,1,0:T(8,128)S(1)}, u32[]{:S(2)}, u32[]{:S(2)}) async-start(f32[64,8,256]{2,1,0:T(8,128)} %copy.39), calls=%async_computation | async-start | bytes 1048576 | tf_op jit(solution)/shard_map/all_to_all | solution.py:158
  44.6 1.8 copy-start
  59.4 8.4 %copy-start.2 = (f32[512,8]{0,1:T(8,128)S(1)}, f32[512,8]{0,1:T(8,128)}, u32[]{:S(2)}) copy-start(f32[512,8]{0,1:T(8,128)} %param.6) | copy-start | bytes 49156
  61.2 34.8 %all-to-all-start.1 = ((f32[64,16,256]{2,1,0:T(8,128)}), f32[64,16,256]{2,1,0:T(8,128)S(1)}, u32[]{:S(2)}, u32[]{:S(2)}) async-start(f32[64,16,256]{2,1,0:T(8,128)} %copy.47), calls=%async_computation.1 | async-start | bytes 2097152 | tf_op jit(solution)/shard_map/all_to_all | solution.py:172
  97.4 3.9 %copy-start.1 = (f32[256,1024]{1,0:T(8,128)S(1)}, f32[256,1024]{1,0:T(8,128)}, u32[]{:S(2)}) copy-start(f32[256,1024]{1,0:T(8,128)} %copy.48) | copy-start | bytes 3145732
  108.4 18.2 %all-to-all-start.2 = ((bf16[64,2,1024]{2,1,0:T(2,128)(2,1)}), bf16[64,2,1024]{2,1,0:T(2,128)(2,1)S(1)}, u32[]{:S(2)}, u32[]{:S(2)}) async-start(bf16[64,2,1024]{2,1,0:T(2,128)(2,1)} %reshape.337), calls=%async_computation.2 | async-start | bytes 524288 | tf_op jit(solution)/shard_map/all_to_all | solution.py:189
  114.6 40.6 %all-gather.2.cloned.1.call-start = ((), (), s32[]{:S(2)}) async-start(), calls=%async_computation.3 | async-start | bytes 1310720 | tf_op jit(solution)/shard_map/all_gather | solution.py:195
  129.9 2.7 %copy-start.3 = (s32[16]{0:T(128)S(1)}, s32[16]{0:T(128)}, u32[]{:S(2)}) copy-start(s32[16]{0:T(128)} %param.9) | copy-start | bytes 196
  129.9 4.8 %copy-start.4 = (s32[256]{0:T(256)S(1)}, s32[256]{0:T(256)}, u32[]{:S(2)}) copy-start(s32[256]{0:T(256)} %param.8) | copy-start | bytes 3076
Sparse Core Ops, SparseCore 0:
  132.7 22.4 all-gather.1

commit v8 on v7

--- a/solution.py
+++ b/solution.py
@@ -195,12 +195,12 @@
     seg_piece = lax.all_gather(local_data, "tmpl", axis=0, tiled=True)
     x_size, z_size, c_size = (lax.axis_size(name) for name in FREQ)
     seg_order = seg_piece.reshape((x_size, z_size, c_size) + seg_piece.shape[1:])
-    seg_order = seg_order.transpose(2, 1, 0, 3, 4, 5).reshape(seg_piece.shape)
+    seg_order = seg_order.transpose(2, 0, 1, 3, 4, 5).reshape(seg_piece.shape)
     data = seg_order.transpose(2, 1, 0, 3)
     j_here = data.shape[0]
     first_block = freq_index * j_here
     partial_sums = intersect(data, templates, cutoffs, lags, first_block)
-    for collective_id, name in enumerate(("fc", "fz", "fx")):
+    for collective_id, name in enumerate(("fc", "fx", "fz")):
         partial_sums = scatter_sum(partial_sums, name, collective_id + 1)
     return partial_sums
 

time: 231 us -> 223 us (0.965)
  Pallas kernels: 63.5 us -> 55.7 us
    pallas_call x3, Pallas kernels: 44.8 us -> 37 us  [scatter_sum(): pl.pallas_call(functools.partial(scatter_kernel, axis, size), out_shape=j...]
where the time goes in v8:
time: 223 us; the launch traced here: 222 us
  waiting for transfers between devices  59.8 us (27%)
  Pallas kernels  55.7 us (25%)
  local copies, waits for them, and re-layouts  39.8 us (18%)
  starting transfers between devices  25.8 us (12%)
  other arithmetic  19.4 us (9%)
  between operations  13.7 us (6%)
  matrix products  7.78 us (3%)
    pallas_call x3, Pallas kernels, scatter_sum(): pl.pallas_call(functools.partial(scatter_kernel, axis, size), out_shape=j...  37 us
    all_to_all x1, waiting for transfers between devices, spectrum_blocks(): lax.all_to_all(twisted, FREQ, 0, 0, tiled=True)  25.9 us
    pallas_call x1, Pallas kernels, intersect(): pl.pallas_call(intersect_kernel, out_shape=jax.ShapeDtypeStruct((seg_coun...  18.7 us
    all_to_all x1, starting transfers between devices, spectrum_blocks(): lax.all_to_all(sent, FREQ, 0, 0, tiled=True)  13 us
    another operation x4, local copies, waits for them, and re-layouts, spectrum_blocks(): jnp.stack([real_part * twist_cos + imag_part * twist_sin, imag_part * twi...  12.5 us
    all_to_all x1, waiting for transfers between devices, spectrum_blocks(): lax.all_to_all(whitened, FREQ, split_axis=2, concat_axis=3, tiled=True)  11.7 us
    all_to_all x1, waiting for transfers between devices, spectrum_blocks(): lax.all_to_all(sent, FREQ, 0, 0, tiled=True)  11.6 us
    all_gather x1, waiting for transfers between devices, on_device(): seg_piece = lax.all_gather(local_data, 'tmpl', axis=0, tiled=True)  10.5 us
  transfers between devices with their start and end apart: 4, of which 4 were waited for; matrix products, arithmetic and copies ran while one was open for 9% of the time, Pallas kernels for 0%

profile of v8, /device:TPU:1, one launch (start us, length us, event | category | flops | bytes accessed | tf_op | source)
XLA Modules:
  0.0 222.0 jit_solution(11098947825459895621)
XLA Ops:
  6.5 3.7 %reshape.326 = f32[16,8,64,16]{3,2,1,0:T(8,128)} reshape(f32[16,8192]{1,0:T(8,128)} %param.5) | data formatting | bytes 1048576 | tf_op jit(solution)/shard_map/reshape | solution.py:156
  10.2 2.9 %copy.38 = f32[64,8,16,16]{0,3,2,1:T(8,128)S(1)} copy(f32[64,8,16,16]{2,0,1,3:T(8,128)} %bitcast.44) | data formatting | bytes 1048576 | tf_op jit(solution)/shard_map/transpose | solution.py:156
  13.1 1.1 copy.39
  14.2 13.0 %all-to-all-start = ((f32[64,8,256]{2,1,0:T(8,128)}), f32[64,8,256]{2,1,0:T(8,128)S(1)}, u32[]{:S(2)}, u32[]{:S(2)}) async-start(f32[64,8,256]{2,1,0:T(8,128)} %copy.39), calls=%async_computation | async-start | bytes 1048576 | tf_op jit(solution)/shard_map/all_to_all | solution.py:158
  27.3 0.2 fusion.49
  27.5 0.1 broadcast_in_dim.11
  27.5 0.2 copy.40
  27.7 0.1 broadcast_in_dim.12
  27.8 1.0 copy.41
  28.8 4.1 %sine_negate_fusion = (f32[512,512]{1,0:T(8,128)S(1)}, f32[512,512]{1,0:T(8,128)S(1)}) fusion(), kind=kLoop, calls=%fused_computation.16 | loop fusion | flops 3932160 | bytes 2097152 | tf_op jit(solution)/shard_map/neg | solution.py:155
  32.9 11.6 %all-to-all-done = f32[64,8,256]{2,1,0:T(8,128)S(1)} async-done(((f32[64,8,256]{2,1,0:T(8,128)}), f32[64,8,256]{2,1,0:T(8,128)S(1)}, u32[]{:S(2)}, u32[]{:S(2)}) %all-to-all-start) | async-done | bytes 524320 | tf_op jit(solution)/shard_map/all_to_all | solution.py:158
  44.6 0.0 copy-start
  44.6 1.8 fusion.1
  46.4 0.0 copy-done
  46.4 0.1 multiply_add_fusion.1
  46.5 2.6 %stack.21 = f32[1,64,8,16,16]{4,3,2,1,0:T(8,128)} reshape(f32[512,256]{1,0:T(8,128)S(1)} %get-tuple-element.5) | data formatting | bytes 1048576 | tf_op jit(solution)/shard_map/stack | solution.py:166
  49.2 3.6 %copy.44 = f32[1,64,8,16,16]{1,4,3,2,0:T(8,128)S(1)} copy(f32[1,64,8,16,16]{4,3,2,1,0:T(8,128)} %stack.21) | data formatting | bytes 1048576 | tf_op jit(solution)/shard_map/stack | solution.py:166
  52.8 2.6 %stack.22 = f32[1,64,8,16,16]{4,3,2,1,0:T(8,128)} reshape(f32[512,256]{1,0:T(8,128)S(1)} %get-tuple-element.6) | data formatting | bytes 1048576 | tf_op jit(solution)/shard_map/stack | solution.py:166
  55.4 3.6 %copy.45 = f32[1,64,8,16,16]{1,4,3,2,0:T(8,128)S(1)} copy(f32[1,64,8,16,16]{4,3,2,1,0:T(8,128)} %stack.22) | data formatting | bytes 1048576 | tf_op jit(solution)/shard_map/stack | solution.py:166
  59.0 0.2 maximum_bitcast_fusion
  59.2 0.2 copy.46
  59.4 0.0 copy-start.2
  59.5 1.8 copy.47
  61.2 6.3 %all-to-all-start.1 = ((f32[64,16,256]{2,1,0:T(8,128)}), f32[64,16,256]{2,1,0:T(8,128)S(1)}, u32[]{:S(2)}, u32[]{:S(2)}) async-start(f32[64,16,256]{2,1,0:T(8,128)} %copy.47), calls=%async_computation.1 | async-start | bytes 2097152 | tf_op jit(solution)/shard_map/all_to_all | solution.py:172
  67.5 0.3 fusion.40
  67.8 0.0 copy-done.2
  67.8 0.3 fusion.43
  68.2 1.9 multiply_subtract_fusion
  70.1 25.9 %all-to-all-done.1 = f32[64,16,256]{2,1,0:T(8,128)S(1)} async-done(((f32[64,16,256]{2,1,0:T(8,128)}), f32[64,16,256]{2,1,0:T(8,128)S(1)}, u32[]{:S(2)}, u32[]{:S(2)}) %all-to-all-start.1) | async-done | bytes 1048608 | tf_op jit(solution)/shard_map/all_to_all | solution.py:172
  96.1 1.3 copy.48
  97.4 0.0 copy-start.1
  97.4 3.9 %fusion.53 = f32[512,2,8,16]{0,3,2,1:T(8,128)S(1)} fusion(f32[512,1024,1,1]{0,1,3,2:T(8,128)} %bitcast.52, f32[2,8,16,1024]{3,2,1,0:T(8,128)} %bitcast.56), kind=kOutput, calls=%fused_computation.95 | convolution fusion | flops 1610612736 | bytes 3670016 | tf_op jit(solution)/shard_map/dot_general | solution.py:183
  101.3 0.0 copy-done.1
  101.3 2.0 fusion.54
  103.4 0.1 fusion.19
  103.5 2.0 copy.51
  105.5 2.9 %reshape.337 = bf16[64,2,1024]{2,1,0:T(2,128)(2,1)} reshape(bf16[512,2,8,16]{3,2,1,0:T(8,128)(2,1)S(1)} %bitcast.45) | data formatting | bytes 524288
  108.4 6.2 %all-to-all-start.2 = ((bf16[64,2,1024]{2,1,0:T(2,128)(2,1)}), bf16[64,2,1024]{2,1,0:T(2,128)(2,1)S(1)}, u32[]{:S(2)}, u32[]{:S(2)}) async-start(bf16[64,2,1024]{2,1,0:T(2,128)(2,1)} %reshape.337), calls=%async_computation.2 | async-start | bytes 524288 | tf_op jit(solution)/shard_map/all_to_all | solution.py:189
  114.6 0.3 all-gather.2.cloned.1.call-start
  114.9 11.7 %all-to-all-done.2 = bf16[64,2,1024]{2,1,0:T(2,128)(2,1)S(1)} async-done(((bf16[64,2,1024]{2,1,0:T(2,128)(2,1)}), bf16[64,2,1024]{2,1,0:T(2,128)(2,1)S(1)}, u32[]{:S(2)}, u32[]{:S(2)}) %all-to-all-start.2) | async-done | bytes 262176 | tf_op jit(solution)/shard_map/all_to_all | solution.py:189
  126.6 1.4 reshape.338
  128.1 1.9 copy.66
  129.9 0.0 copy-start.3
  129.9 0.0 copy-start.4
  129.9 2.6 %copy.54 = bf16[16,2,8,512]{3,2,1,0:T(8,128)(2,1)} copy(bf16[16,2,8,512]{0,3,2,1:T(8,128)(2,1)} %bitcast.48) | data formatting | bytes 524288 | tf_op jit(solution)/shard_map/all_to_all | solution.py:189
  132.6 0.0 all-gather.2.cloned.1.call-update
  132.6 0.0 copy-done.3
  132.6 0.1 fusion.50
  132.7 0.1 add_select_fusion.6
  132.8 1.1 fusion.21
  133.9 0.9 maximum_bitcast_fusion.1.ph_ref
  134.8 0.0 copy-done.4
  134.8 0.1 broadcast_compare_fusion
  134.8 9.9 %fusion.tm_ref = bf16[8,2,256,512]{3,2,1,0:T(8,128)(2,1)} fusion(bf16[256,2,8,512]{3,2,1,0:T(8,128)(2,1)} %param.7, pred[256,8]{0,1:T(8,128)(4,1)S(1)} %broadcast_compare_fusion), kind=kLoop, calls=%fused_computation.1 | loop fusion | flops 2097152 | bytes 8390656 | tf_op jit(solution)/shard_map/transpose | solution.py:76
  144.7 10.5 %all-gather.2.cloned.1.call-done = bf16[64,2,8,512]{3,2,1,0:T(8,128)(2,1)} async-done(((bf16[16,2,8,512]{3,2,1,0:T(8,128)(2,1)}), bf16[64,2,8,512]{3,2,1,0:T(8,128)(2,1)}) %all-gather.2.cloned.1.call-update) | async-done | bytes 1048592 | tf_op jit(solution)/shard_map/all_gather | solution.py:195
  155.3 2.8 %copy.55 = bf16[2,4,8,2,8,512]{5,2,1,0,3,4:T(8,128)(2,1)} copy(bf16[2,4,8,2,8,512]{5,4,3,0,2,1:T(8,128)(2,1)} %bitcast.55) | data formatting | bytes 2097152 | tf_op jit(solution)/shard_map/transpose | solution.py:198
  158.0 18.7 %shard_map.55.x_ref = f32[64,32,256]{2,1,0:T(8,128)} custom-call(f32[8,2,16,512]{3,2,1,0:T(8,128)} %maximum_bitcast_fusion.1.ph_ref, bf16[8,2,64,512]{3,2,1,0:T(8,128)(2,1)} %bitcast.58, bf16[8,2,256,512]{3,2,1,0:T(8,128)(2,1)} %fusion.tm_ref), custom_call_target="tpu_custom_call" | custom-call | flops 8589934592 | bytes 7864320 | tf_op jit(solution)/shard_map/pallas_call | solution.py:80
  176.7 6.6 %shard_map.56.x_ref = f32[32,32,256]{2,1,0:T(8,128)} custom-call(f32[64,32,256]{2,1,0:T(8,128)} %shard_map.55.x_ref), custom_call_target="tpu_custom_call" | custom-call | tf_op jit(solution)/shard_map/pallas_call | solution.py:131
  183.3 17.5 %shard_map.57.x_ref = f32[8,32,256]{2,1,0:T(8,128)} custom-call(f32[32,32,256]{2,1,0:T(8,128)} %shard_map.56.x_ref), custom_call_target="tpu_custom_call" | custom-call | tf_op jit(solution)/shard_map/pallas_call | solution.py:131
  200.8 13.0 %shard_map.58 = f32[1,32,256]{2,1,0:T(8,128)} custom-call(f32[8,32,256]{2,1,0:T(8,128)} %shard_map.57.x_ref), custom_call_target="tpu_custom_call" | custom-call | tf_op jit(solution)/shard_map/pallas_call | solution.py:131
  213.8 1.4 copy.68
  (5 shorter events, 0.1 us)
Async XLA Ops:
  14.2 30.3 %all-to-all-start = ((f32[64,8,256]{2,1,0:T(8,128)}), f32[64,8,256]{2,1,0:T(8,128)S(1)}, u32[]{:S(2)}, u32[]{:S(2)}) async-start(f32[64,8,256]{2,1,0:T(8,128)} %copy.39), calls=%async_computation | async-start | bytes 1048576 | tf_op jit(solution)/shard_map/all_to_all | solution.py:158
  44.6 1.8 copy-start
  59.4 8.4 %copy-start.2 = (f32[512,8]{0,1:T(8,128)S(1)}, f32[512,8]{0,1:T(8,128)}, u32[]{:S(2)}) copy-start(f32[512,8]{0,1:T(8,128)} %param.6) | copy-start | bytes 49156
  61.2 34.8 %all-to-all-start.1 = ((f32[64,16,256]{2,1,0:T(8,128)}), f32[64,16,256]{2,1,0:T(8,128)S(1)}, u32[]{:S(2)}, u32[]{:S(2)}) async-start(f32[64,16,256]{2,1,0:T(8,128)} %copy.47), calls=%async_computation.1 | async-start | bytes 2097152 | tf_op jit(solution)/shard_map/all_to_all | solution.py:172
  97.4 3.9 %copy-start.1 = (f32[256,1024]{1,0:T(8,128)S(1)}, f32[256,1024]{1,0:T(8,128)}, u32[]{:S(2)}) copy-start(f32[256,1024]{1,0:T(8,128)} %copy.48) | copy-start | bytes 3145732
  108.4 18.2 %all-to-all-start.2 = ((bf16[64,2,1024]{2,1,0:T(2,128)(2,1)}), bf16[64,2,1024]{2,1,0:T(2,128)(2,1)S(1)}, u32[]{:S(2)}, u32[]{:S(2)}) async-start(bf16[64,2,1024]{2,1,0:T(2,128)(2,1)} %reshape.337), calls=%async_computation.2 | async-start | bytes 524288 | tf_op jit(solution)/shard_map/all_to_all | solution.py:189
  114.6 40.6 %all-gather.2.cloned.1.call-start = ((), (), s32[]{:S(2)}) async-start(), calls=%async_computation.3 | async-start | bytes 1310720 | tf_op jit(solution)/shard_map/all_gather | solution.py:195
  129.9 2.7 %copy-start.3 = (s32[16]{0:T(128)S(1)}, s32[16]{0:T(128)}, u32[]{:S(2)}) copy-start(s32[16]{0:T(128)} %param.9) | copy-start | bytes 196
  129.9 4.8 %copy-start.4 = (s32[256]{0:T(256)S(1)}, s32[256]{0:T(256)}, u32[]{:S(2)}) copy-start(s32[256]{0:T(256)} %param.8) | copy-start | bytes 3076
Sparse Core Ops, SparseCore 0:
  132.7 22.4 all-gather.1

commit v9 on v8

--- a/solution.py
+++ b/solution.py
@@ -142,6 +142,45 @@
     )(parts)
 
 
+def gather_kernel(axis, size, x_ref, o_ref, send_sem, recv_sem):
+    me = lax.axis_index(axis)
+    mesh_ids = pl.DeviceIdType.MESH
+    barrier = pltpu.get_barrier_semaphore()
+    for k in range(1, size):
+        peer = lax.rem(me + k, size)
+        pl.semaphore_signal(barrier, inc=1, device_id={axis: peer}, device_id_type=mesh_ids)
+    pl.semaphore_wait(barrier, size - 1)
+    copies = []
+    for k in range(1, size):
+        peer = lax.rem(me + k, size)
+        copy = pltpu.make_async_remote_copy(
+            src_ref=x_ref,
+            dst_ref=o_ref.at[me],
+            send_sem=send_sem.at[k],
+            recv_sem=recv_sem.at[k],
+            device_id={axis: peer},
+            device_id_type=mesh_ids,
+        )
+        copy.start()
+        copies.append(copy)
+    o_ref[me] = x_ref[...]
+    for copy in copies:
+        copy.wait()
+
+
+def gather_all(block, axis, collective_id):
+    size = lax.axis_size(axis)
+    vmem = pltpu.VMEM
+    return pl.pallas_call(
+        functools.partial(gather_kernel, axis, size),
+        out_shape=jax.ShapeDtypeStruct((size,) + block.shape, block.dtype),
+        in_specs=[pl.BlockSpec(memory_space=vmem)],
+        out_specs=pl.BlockSpec(memory_space=vmem),
+        scratch_shapes=[pltpu.SemaphoreType.DMA((size,)), pltpu.SemaphoreType.DMA((size,))],
+        compiler_params=pltpu.CompilerParams(collective_id=collective_id, has_side_effects=True),
+    )(block)
+
+
 def spectrum_blocks(strain, psd):
     freq_count = lax.axis_size(FREQ)
     freq_index = lax.axis_index(FREQ)
@@ -192,7 +231,8 @@
 def on_device(strain, psd, templates, cutoffs, lags):
     freq_index = lax.axis_index(FREQ)
     local_data = spectrum_blocks(strain, psd)
-    seg_piece = lax.all_gather(local_data, "tmpl", axis=0, tiled=True)
+    seg_piece = gather_all(local_data, "tmpl", 4)
+    seg_piece = seg_piece.reshape((-1,) + local_data.shape[1:])
     x_size, z_size, c_size = (lax.axis_size(name) for name in FREQ)
     seg_order = seg_piece.reshape((x_size, z_size, c_size) + seg_piece.shape[1:])
     seg_order = seg_order.transpose(2, 0, 1, 3, 4, 5).reshape(seg_piece.shape)

time: 223 us -> 203 us (0.910)
  waiting for transfers between devices: 59.8 us -> 36.7 us
  Pallas kernels: 55.7 us -> 72.2 us
  between operations: 13.7 us -> 0.29 us
    pallas_call x0 -> x1, Pallas kernels: none -> 17.5 us  [gather_all(): pl.pallas_call(functools.partial(gather_kernel, axis, size), out_shape=ja...]
    all_gather x1 -> x0, waiting for transfers between devices: 10.5 us -> none  [on_device(): seg_piece = lax.all_gather(local_data, 'tmpl', axis=0, tiled=True)]
    all_to_all x1, waiting for transfers between devices: 11.7 us -> 1.26 us  [spectrum_blocks(): lax.all_to_all(whitened, FREQ, split_axis=2, concat_axis=3, tiled=True)]
    another operation x0 -> x1, local copies, waits for them, and re-layouts: none -> 2.78 us  [on_device(): seg_piece.reshape((x_size, z_size, c_size) + seg_piece.shape[1:])]
    transpose x1 -> x0, local copies, waits for them, and re-layouts: 2.78 us -> none  [on_device(): seg_order = seg_order.transpose(2, 0, 1, 3, 4, 5).reshape(seg_piece.shape)]
    unnamed x13 -> x15, local copies, waits for them, and re-layouts: 5.75 us -> 5.76 us
  transfers between devices with their start and end apart: 4 -> 3, of which waited for: 4 -> 3; matrix products, arithmetic and copies ran while one was open for 9% -> 10% of each run, Pallas kernels for 0% -> 0%
where the time goes in v9:
time: 203 us
  Pallas kernels  72.2 us (36%)
  local copies, waits for them, and re-layouts  39.9 us (20%)
  waiting for transfers between devices  36.7 us (18%)
  starting transfers between devices  25.5 us (13%)
  other arithmetic  20.2 us (10%)
  matrix products  7.78 us (4%)
    pallas_call x3, Pallas kernels, scatter_sum(): pl.pallas_call(functools.partial(scatter_kernel, axis, size), out_shape=j...  36 us
    all_to_all x1, waiting for transfers between devices, spectrum_blocks(): lax.all_to_all(twisted, FREQ, 0, 0, tiled=True)  23.8 us
    pallas_call x1, Pallas kernels, intersect(): pl.pallas_call(intersect_kernel, out_shape=jax.ShapeDtypeStruct((seg_coun...  18.7 us
    pallas_call x1, Pallas kernels, gather_all(): pl.pallas_call(functools.partial(gather_kernel, axis, size), out_shape=ja...  17.5 us
    all_to_all x1, starting transfers between devices, spectrum_blocks(): lax.all_to_all(sent, FREQ, 0, 0, tiled=True)  13 us
    another operation x4, local copies, waits for them, and re-layouts, spectrum_blocks(): jnp.stack([real_part * twist_cos + imag_part * twist_sin, imag_part * twi...  12.5 us
    all_to_all x1, waiting for transfers between devices, spectrum_blocks(): lax.all_to_all(sent, FREQ, 0, 0, tiled=True)  11.6 us
    transpose x1, other arithmetic, intersect(): jnp.where(keep, templates, jnp.zeros_like(templates)).transpose(2, 1, 0, 3)  9.88 us
  transfers between devices with their start and end apart: 3, of which 3 were waited for; matrix products, arithmetic and copies ran while one was open for 10% of the time, Pallas kernels for 0%

profile of v9, /device:TPU:1, one launch (start us, length us, event | category | flops | bytes accessed | tf_op | source)
XLA Modules:
  0.0 202.5 jit_solution(11242965076779268802)
XLA Ops:
  0.0 3.7 %reshape.323 = f32[16,8,64,16]{3,2,1,0:T(8,128)} reshape(f32[16,8192]{1,0:T(8,128)} %param.5) | data formatting | bytes 1048576 | tf_op jit(solution)/shard_map/reshape | solution.py:195
  3.7 2.9 %copy.40 = f32[64,8,16,16]{0,3,2,1:T(8,128)S(1)} copy(f32[64,8,16,16]{2,0,1,3:T(8,128)} %bitcast.44) | data formatting | bytes 1048576 | tf_op jit(solution)/shard_map/transpose | solution.py:195
  6.6 1.1 copy.41
  7.7 13.0 %all-to-all-start = ((f32[64,8,256]{2,1,0:T(8,128)}), f32[64,8,256]{2,1,0:T(8,128)S(1)}, u32[]{:S(2)}, u32[]{:S(2)}) async-start(f32[64,8,256]{2,1,0:T(8,128)} %copy.41), calls=%async_computation | async-start | bytes 1048576 | tf_op jit(solution)/shard_map/all_to_all | solution.py:197
  20.7 0.2 fusion.49
  21.0 0.1 broadcast_in_dim.11
  21.0 0.2 copy.42
  21.2 0.1 broadcast_in_dim.12
  21.3 1.0 copy.43
  22.3 4.1 %sine_negate_fusion = (f32[512,512]{1,0:T(8,128)S(1)}, f32[512,512]{1,0:T(8,128)S(1)}) fusion(), kind=kLoop, calls=%fused_computation.16 | loop fusion | flops 3932160 | bytes 2097152 | tf_op jit(solution)/shard_map/neg | solution.py:194
  26.4 11.6 %all-to-all-done = f32[64,8,256]{2,1,0:T(8,128)S(1)} async-done(((f32[64,8,256]{2,1,0:T(8,128)}), f32[64,8,256]{2,1,0:T(8,128)S(1)}, u32[]{:S(2)}, u32[]{:S(2)}) %all-to-all-start) | async-done | bytes 524320 | tf_op jit(solution)/shard_map/all_to_all | solution.py:197
  38.0 0.0 copy-start
  38.0 1.8 fusion.1
  39.9 0.0 copy-done
  39.9 0.1 multiply_add_fusion.1
  40.0 2.6 %stack.21 = f32[1,64,8,16,16]{4,3,2,1,0:T(8,128)} reshape(f32[512,256]{1,0:T(8,128)S(1)} %get-tuple-element.5) | data formatting | bytes 1048576 | tf_op jit(solution)/shard_map/stack | solution.py:205
  42.6 3.6 %copy.46 = f32[1,64,8,16,16]{1,4,3,2,0:T(8,128)S(1)} copy(f32[1,64,8,16,16]{4,3,2,1,0:T(8,128)} %stack.21) | data formatting | bytes 1048576 | tf_op jit(solution)/shard_map/stack | solution.py:205
  46.3 2.6 %stack.22 = f32[1,64,8,16,16]{4,3,2,1,0:T(8,128)} reshape(f32[512,256]{1,0:T(8,128)S(1)} %get-tuple-element.6) | data formatting | bytes 1048576 | tf_op jit(solution)/shard_map/stack | solution.py:205
  48.9 3.6 %copy.47 = f32[1,64,8,16,16]{1,4,3,2,0:T(8,128)S(1)} copy(f32[1,64,8,16,16]{4,3,2,1,0:T(8,128)} %stack.22) | data formatting | bytes 1048576 | tf_op jit(solution)/shard_map/stack | solution.py:205
  52.5 0.2 maximum_bitcast_fusion
  52.7 0.2 copy.48
  52.9 0.0 copy-start.5
  53.0 0.0 copy-start.4
  53.0 0.0 copy-start.3
  53.0 1.8 copy.49
  54.7 6.3 %all-to-all-start.1 = ((f32[64,16,256]{2,1,0:T(8,128)}), f32[64,16,256]{2,1,0:T(8,128)S(1)}, u32[]{:S(2)}, u32[]{:S(2)}) async-start(f32[64,16,256]{2,1,0:T(8,128)} %copy.49), calls=%async_computation.1 | async-start | bytes 2097152 | tf_op jit(solution)/shard_map/all_to_all | solution.py:211
  61.1 0.3 fusion.40
  61.3 0.0 copy-done.5
  61.3 0.1 broadcast_compare_fusion
  61.4 0.0 copy-done.4
  61.4 0.1 fusion.50
  61.5 0.0 copy-done.3
  61.5 0.1 add_select_fusion.6
  61.6 0.3 fusion.43
  61.9 1.9 fusion.21
  63.8 2.0 multiply_subtract_fusion
  65.8 23.8 %all-to-all-done.1 = f32[64,16,256]{2,1,0:T(8,128)S(1)} async-done(((f32[64,16,256]{2,1,0:T(8,128)}), f32[64,16,256]{2,1,0:T(8,128)S(1)}, u32[]{:S(2)}, u32[]{:S(2)}) %all-to-all-start.1) | async-done | bytes 1048608 | tf_op jit(solution)/shard_map/all_to_all | solution.py:211
  89.6 1.3 copy.50
  90.9 0.0 copy-start.1
  90.9 3.9 %fusion.53 = f32[512,2,8,16]{0,3,2,1:T(8,128)S(1)} fusion(f32[512,1024,1,1]{0,1,3,2:T(8,128)} %bitcast.53, f32[2,8,16,1024]{3,2,1,0:T(8,128)} %bitcast.56), kind=kOutput, calls=%fused_computation.95 | convolution fusion | flops 1610612736 | bytes 3670016 | tf_op jit(solution)/shard_map/dot_general | solution.py:222
  94.8 0.0 copy-done.1
  94.8 2.0 %fusion.54 = f32[512,2,8,16]{0,3,2,1:T(8,128)S(1)} fusion(f32[512,1024,1,1]{0,1,3,2:T(8,128)S(1)} %bitcast.52, f32[2,8,16,1024]{3,2,1,0:T(8,128)S(1)} %bitcast.57), kind=kOutput, calls=%fused_computation.96 | convolution fusion | flops 1610612736 | bytes 3670016 | tf_op jit(solution)/shard_map/dot_general | solution.py:223
  96.9 0.1 fusion.19
  97.0 0.0 copy-start.2
  97.1 2.0 copy.53
  99.0 2.9 %reshape.333 = bf16[64,2,1024]{2,1,0:T(2,128)(2,1)} reshape(bf16[512,2,8,16]{3,2,1,0:T(8,128)(2,1)S(1)} %bitcast.45) | data formatting | bytes 524288
  102.0 6.2 %all-to-all-start.2 = ((bf16[64,2,1024]{2,1,0:T(2,128)(2,1)}), bf16[64,2,1024]{2,1,0:T(2,128)(2,1)S(1)}, u32[]{:S(2)}, u32[]{:S(2)}) async-start(bf16[64,2,1024]{2,1,0:T(2,128)(2,1)} %reshape.333), calls=%async_computation.2 | async-start | bytes 524288 | tf_op jit(solution)/shard_map/all_to_all | solution.py:228
  108.2 0.0 copy-done.2
  108.2 0.8 maximum_bitcast_fusion.1.ph_ref
  109.0 9.9 %fusion.tm_ref = bf16[8,2,256,512]{3,2,1,0:T(8,128)(2,1)} fusion(bf16[256,2,8,512]{3,2,1,0:T(8,128)(2,1)} %param.7, pred[256,8]{0,1:T(8,128)(4,1)S(1)} %broadcast_compare_fusion), kind=kLoop, calls=%fused_computation.1 | loop fusion | flops 2097152 | bytes 8390656 | tf_op jit(solution)/shard_map/transpose | solution.py:76
  118.9 1.3 all-to-all-done.2
  120.2 1.4 reshape.334
  121.6 1.9 copy.68
  123.5 2.6 %copy.56.x_ref = bf16[16,2,8,512]{3,2,1,0:T(8,128)(2,1)} copy(bf16[16,2,8,512]{0,3,2,1:T(8,128)(2,1)} %bitcast.48) | data formatting | bytes 524288 | tf_op jit(solution)/shard_map/all_to_all | solution.py:228
  126.1 17.5 %shard_map.55 = bf16[4,16,2,8,512]{4,3,2,1,0:T(8,128)(2,1)} custom-call(bf16[16,2,8,512]{3,2,1,0:T(8,128)(2,1)} %copy.56.x_ref), custom_call_target="tpu_custom_call" | custom-call | tf_op jit(solution)/shard_map/pallas_call | solution.py:174
  143.6 2.8 %copy.57 = bf16[4,8,2,2,8,512]{5,1,0,2,3,4:T(8,128)(2,1)} copy(bf16[4,8,2,2,8,512]{5,4,3,2,1,0:T(8,128)(2,1)} %bitcast.50) | data formatting | bytes 2097152 | tf_op jit(solution)/shard_map/reshape;reshape | solution.py:237
  146.4 18.7 %shard_map.56.x_ref = f32[64,32,256]{2,1,0:T(8,128)} custom-call(f32[8,2,16,512]{3,2,1,0:T(8,128)} %maximum_bitcast_fusion.1.ph_ref, bf16[8,2,64,512]{3,2,1,0:T(8,128)(2,1)} %bitcast.58, bf16[8,2,256,512]{3,2,1,0:T(8,128)(2,1)} %fusion.tm_ref), custom_call_target="tpu_custom_call" | custom-call | flops 8589934592 | bytes 7864320 | tf_op jit(solution)/shard_map/pallas_call | solution.py:80
  165.1 6.3 %shard_map.57.x_ref = f32[32,32,256]{2,1,0:T(8,128)} custom-call(f32[64,32,256]{2,1,0:T(8,128)} %shard_map.56.x_ref), custom_call_target="tpu_custom_call" | custom-call | tf_op jit(solution)/shard_map/pallas_call | solution.py:131
  171.4 17.4 %shard_map.58.x_ref = f32[8,32,256]{2,1,0:T(8,128)} custom-call(f32[32,32,256]{2,1,0:T(8,128)} %shard_map.57.x_ref), custom_call_target="tpu_custom_call" | custom-call | tf_op jit(solution)/shard_map/pallas_call | solution.py:131
  188.8 12.3 %shard_map.59 = f32[1,32,256]{2,1,0:T(8,128)} custom-call(f32[8,32,256]{2,1,0:T(8,128)} %shard_map.58.x_ref), custom_call_target="tpu_custom_call" | custom-call | tf_op jit(solution)/shard_map/pallas_call | solution.py:131
  201.2 1.4 copy.70
  (5 shorter events, 0.1 us)
Async XLA Ops:
  7.7 30.3 %all-to-all-start = ((f32[64,8,256]{2,1,0:T(8,128)}), f32[64,8,256]{2,1,0:T(8,128)S(1)}, u32[]{:S(2)}, u32[]{:S(2)}) async-start(f32[64,8,256]{2,1,0:T(8,128)} %copy.41), calls=%async_computation | async-start | bytes 1048576 | tf_op jit(solution)/shard_map/all_to_all | solution.py:197
  38.0 1.8 copy-start
  52.9 8.4 %copy-start.5 = (s32[256]{0:T(256)S(1)}, s32[256]{0:T(256)}, u32[]{:S(2)}) copy-start(s32[256]{0:T(256)} %param.8) | copy-start | bytes 3076
  53.0 8.5 %copy-start.4 = (s32[16]{0:T(128)S(1)}, s32[16]{0:T(128)}, u32[]{:S(2)}) copy-start(s32[16]{0:T(128)} %param.9) | copy-start | bytes 196
  53.0 8.5 %copy-start.3 = (f32[512,8]{0,1:T(8,128)S(1)}, f32[512,8]{0,1:T(8,128)}, u32[]{:S(2)}) copy-start(f32[512,8]{0,1:T(8,128)} %param.6) | copy-start | bytes 49156
  54.7 34.8 %all-to-all-start.1 = ((f32[64,16,256]{2,1,0:T(8,128)}), f32[64,16,256]{2,1,0:T(8,128)S(1)}, u32[]{:S(2)}, u32[]{:S(2)}) async-start(f32[64,16,256]{2,1,0:T(8,128)} %copy.49), calls=%async_computation.1 | async-start | bytes 2097152 | tf_op jit(solution)/shard_map/all_to_all | solution.py:211
  90.9 3.9 %copy-start.1 = (f32[256,1024]{1,0:T(8,128)S(1)}, f32[256,1024]{1,0:T(8,128)}, u32[]{:S(2)}) copy-start(f32[256,1024]{1,0:T(8,128)} %copy.50) | copy-start | bytes 3145732
  97.0 11.1 %copy-start.2 = (f32[1,16,8,512]{3,1,0,2:T(8,128)S(1)}, f32[1,16,8,512]{3,1,0,2:T(8,128)}, u32[]{:S(2)}) copy-start(f32[1,16,8,512]{3,1,0,2:T(8,128)} %get-tuple-element.12) | copy-start | bytes 786436
  102.0 18.2 %all-to-all-start.2 = ((bf16[64,2,1024]{2,1,0:T(2,128)(2,1)}), bf16[64,2,1024]{2,1,0:T(2,128)(2,1)S(1)}, u32[]{:S(2)}, u32[]{:S(2)}) async-start(bf16[64,2,1024]{2,1,0:T(2,128)(2,1)} %reshape.333), calls=%async_computation.2 | async-start | bytes 524288 | tf_op jit(solution)/shard_map/all_to_all | solution.py:228

commit v10 on v9

--- a/solution.py
+++ b/solution.py
@@ -200,15 +200,20 @@
     imag_part = both_parts[A:]
     time_ids = freq_index * cols_here + jnp.arange(cols_here, dtype=jnp.int32)
     twist_cos, twist_sin = cos_sin_table(jnp.arange(A, dtype=jnp.int32), time_ids, LEN)
-    twist_cos = jnp.repeat(twist_cos, seg_local, axis=1)
-    twist_sin = jnp.repeat(twist_sin, seg_local, axis=1)
+    p_here = A // freq_count
+    shaped = (freq_count, p_here, cols_here * seg_local)
+    real_part = real_part.reshape(shaped)
+    imag_part = imag_part.reshape(shaped)
+    twist_cos = jnp.repeat(twist_cos, seg_local, axis=1).reshape(shaped)
+    twist_sin = jnp.repeat(twist_sin, seg_local, axis=1).reshape(shaped)
     twisted = jnp.stack(
-        [real_part * twist_cos + imag_part * twist_sin, imag_part * twist_cos - real_part * twist_sin]
-    )
-    p_here = A // freq_count
-    twisted = twisted.reshape(2, freq_count, p_here, cols_here, seg_local).transpose(1, 3, 0, 2, 4)
-    twisted = twisted.reshape(freq_count, cols_here, 2 * p_here * seg_local)
-    columns = lax.all_to_all(twisted, FREQ, 0, 0, tiled=True).reshape(B, 2 * p_here * seg_local)
+        [real_part * twist_cos + imag_part * twist_sin, imag_part * twist_cos - real_part * twist_sin],
+        axis=1,
+    )
+    twisted = twisted.reshape(freq_count, 2 * p_here, cols_here * seg_local)
+    columns = lax.all_to_all(twisted, FREQ, 0, 0, tiled=True)
+    columns = columns.reshape(freq_count, 2, p_here, cols_here, seg_local).transpose(0, 3, 1, 2, 4)
+    columns = columns.reshape(B, 2 * p_here * seg_local)
     split = 32
     j_ids = jnp.arange(NB, dtype=jnp.int32)
     high_cos, high_sin = cos_sin_table(j_ids, split * jnp.arange(B // split, dtype=jnp.int32), B)

time: 203 us -> 208 us (1.025)
  waiting for transfers between devices: 36.7 us -> 24.4 us
  local copies, waits for them, and re-layouts: 39.9 us -> 52.1 us
  starting transfers between devices: 25.5 us -> 29.5 us
    all_to_all x1, waiting for transfers between devices: 11.6 us -> 0.01 us  [spectrum_blocks(): lax.all_to_all(sent, FREQ, 0, 0, tiled=True)]
    transpose x1, local copies, waits for them, and re-layouts: 0.23 us -> 7.47 us  [spectrum_blocks(): columns.reshape(freq_count, 2, p_here, cols_here, seg_local)]
    broadcast_in_dim x2, local copies, waits for them, and re-layouts: 0.1 us -> 5.14 us  [the longest x1 2.57 us: spectrum_blocks(): twist_sin = jnp.repeat(twist_sin, seg_local, axis=1).reshape(shaped)]
    another operation x4 -> x2, local copies, waits for them, and re-layouts: 12.5 us -> 7.7 us  [the longest x1 4.22 us: spectrum_blocks(): twist_cos = jnp.repeat(twist_cos, seg_local, axis=1).reshape(shaped)]
    all_to_all x1, starting transfers between devices: 6.28 us -> 10.3 us  [spectrum_blocks(): columns = lax.all_to_all(twisted, FREQ, 0, 0, tiled=True)]
    reshape x3 -> x1, local copies, waits for them, and re-layouts: 2.96 us -> 6.09 us  [spectrum_blocks(): columns = columns.reshape(B, 2 * p_here * seg_local)]
    unnamed x15 -> x19, local copies, waits for them, and re-layouts: 5.76 us -> 6.41 us
  transfers between devices with their start and end apart: 3 -> 3, of which waited for: 3 -> 2; matrix products, arithmetic and copies ran while one was open for 10% -> 16% of each run, Pallas kernels for 0% -> 0%
where the time goes in v10:
time: 208 us; the launch traced here: 207 us
  Pallas kernels  72.2 us (35%)
  local copies, waits for them, and re-layouts  52.1 us (25%)
  starting transfers between devices  29.5 us (14%)
  waiting for transfers between devices  24.4 us (12%)
  other arithmetic  21.8 us (10%)
  matrix products  7.21 us (3%)
    pallas_call x3, Pallas kernels, scatter_sum(): pl.pallas_call(functools.partial(scatter_kernel, axis, size), out_shape=j...  36 us
    all_to_all x1, waiting for transfers between devices, spectrum_blocks(): columns = lax.all_to_all(twisted, FREQ, 0, 0, tiled=True)  23.1 us
    pallas_call x1, Pallas kernels, intersect(): pl.pallas_call(intersect_kernel, out_shape=jax.ShapeDtypeStruct((seg_coun...  18.7 us
    pallas_call x1, Pallas kernels, gather_all(): pl.pallas_call(functools.partial(gather_kernel, axis, size), out_shape=ja...  17.5 us
    all_to_all x1, starting transfers between devices, spectrum_blocks(): lax.all_to_all(sent, FREQ, 0, 0, tiled=True)  13 us
    all_to_all x1, starting transfers between devices, spectrum_blocks(): columns = lax.all_to_all(twisted, FREQ, 0, 0, tiled=True)  10.3 us
    transpose x1, other arithmetic, intersect(): jnp.where(keep, templates, jnp.zeros_like(templates)).transpose(2, 1, 0, 3)  9.87 us
    transpose x1, local copies, waits for them, and re-layouts, spectrum_blocks(): columns.reshape(freq_count, 2, p_here, cols_here, seg_local)  7.47 us
  transfers between devices with their start and end apart: 3, of which 2 were waited for; matrix products, arithmetic and copies ran while one was open for 16% of the time, Pallas kernels for 0%

profile of v10, /device:TPU:1, one launch (start us, length us, event | category | flops | bytes accessed | tf_op | source)
XLA Modules:
  0.0 207.5 jit_solution(14824344633690765179)
XLA Ops:
  0.0 3.7 %reshape.395 = f32[16,8,64,16]{3,2,1,0:T(8,128)} reshape(f32[16,8192]{1,0:T(8,128)} %param.5) | data formatting | bytes 1048576 | tf_op jit(solution)/shard_map/reshape | solution.py:195
  3.7 2.9 %copy.48 = f32[64,8,16,16]{0,3,2,1:T(8,128)S(1)} copy(f32[64,8,16,16]{2,0,1,3:T(8,128)} %bitcast.56) | data formatting | bytes 1048576 | tf_op jit(solution)/shard_map/transpose | solution.py:195
  6.6 1.1 copy.49
  7.7 13.0 %all-to-all-start = ((f32[64,8,256]{2,1,0:T(8,128)}), f32[64,8,256]{2,1,0:T(8,128)S(1)}, u32[]{:S(2)}, u32[]{:S(2)}) async-start(f32[64,8,256]{2,1,0:T(8,128)} %copy.49), calls=%async_computation | async-start | bytes 1048576 | tf_op jit(solution)/shard_map/all_to_all | solution.py:197
  20.7 0.2 fusion.49
  21.0 0.1 copy.51
  21.1 2.6 %broadcast_in_dim.12 = f32[512,16,16]{2,1,0:T(8,128)} broadcast(f32[512,16]{1,0:T(8,128)S(1)} %copy.51), dimensions={0,1} | broadcast | bytes 557056 | tf_op jit(solution)/shard_map/broadcast_in_dim | solution.py:208
  23.7 3.5 %reshape_reshape.10 = f32[64,1,8,256]{3,2,0,1:T(8,128)S(1)} reshape(f32[512,16,16]{2,1,0:T(8,128)} %broadcast_in_dim.12) | data formatting | bytes 1048576 | tf_op jit(solution)/shard_map/reshape;reshape | solution.py:208
  27.1 0.1 copy.50
  27.3 2.6 %broadcast_in_dim.11 = f32[512,16,16]{2,1,0:T(8,128)} broadcast(f32[512,16]{1,0:T(8,128)S(1)} %copy.50), dimensions={0,1} | broadcast | bytes 557056 | tf_op jit(solution)/shard_map/broadcast_in_dim | solution.py:207
  29.8 4.2 %reshape_reshape.9 = f32[64,1,8,256]{3,2,0,1:T(8,128)} reshape(f32[512,16,16]{2,1,0:T(8,128)} %broadcast_in_dim.11) | data formatting | bytes 1048576 | tf_op jit(solution)/shard_map/reshape;reshape | solution.py:207
  34.1 4.1 %sine_negate_fusion = (f32[512,512]{1,0:T(8,128)S(1)}, f32[512,512]{1,0:T(8,128)S(1)}) fusion(), kind=kLoop, calls=%fused_computation.17 | loop fusion | flops 3932160 | bytes 2097152 | tf_op jit(solution)/shard_map/neg | solution.py:194
  38.2 0.0 all-to-all-done
  38.2 0.0 copy-start.2
  38.2 1.8 fusion.1
  40.0 0.0 copy-done.2
  40.0 0.1 multiply_add_fusion.1
  40.2 0.0 copy-start.7
  40.2 0.0 copy-start.6
  40.2 0.0 copy-start.5
  40.2 1.1 copy_bitcast_fusion.1
  41.3 10.3 %all-to-all-start.1 = ((f32[64,16,256]{2,1,0:T(8,128)}), f32[64,16,256]{2,1,0:T(8,128)S(1)}, u32[]{:S(2)}, u32[]{:S(2)}) async-start(f32[64,16,256]{2,1,0:T(8,128)} %copy_bitcast_fusion.1), calls=%async_computation.1 | async-start | bytes 2097152 | tf_op jit(solution)/shard_map/all_to_all | solution.py:214
  51.6 0.3 fusion.40
  51.9 0.0 copy-done.7
  51.9 0.1 broadcast_compare_fusion
  52.0 0.0 copy-done.6
  52.0 0.1 fusion.50
  52.1 0.0 copy-done.5
  52.1 0.1 add_select_fusion.6
  52.2 0.3 fusion.43
  52.5 1.9 fusion.21
  54.5 2.6 %multiply_subtract_fusion = (f32[512,32,32]{0,2,1:T(8,128)}, f32[512,32,32]{0,2,1:T(8,128)}) fusion(f32[512,32]{0,1:T(8,128)S(1)} %get-tuple-element.17, f32[512,32]{0,1:T(8,128)S(1)} %get-tuple-element.16, f32[512,32]{0,1:T(8,128)S(1)} %get-tuple-element.18, f32[512,32]{0,1:T(8,128)S(1)} %get-tuple-element.15), kind=kLoop, calls=%fused_computation.8 | loop fusion | flops 3145728 | bytes 4456448 | tf_op jit(solution)/shard_map/sub | solution.py:222
  57.0 23.1 %all-to-all-done.1 = f32[64,16,256]{2,1,0:T(8,128)S(1)} async-done(((f32[64,16,256]{2,1,0:T(8,128)}), f32[64,16,256]{2,1,0:T(8,128)S(1)}, u32[]{:S(2)}, u32[]{:S(2)}) %all-to-all-start.1) | async-done | bytes 1048608 | tf_op jit(solution)/shard_map/all_to_all | solution.py:214
  80.2 0.7 copy.53
  80.9 7.5 %copy.54 = f32[64,16,2,8,16]{4,3,2,1,0:T(8,128)} copy(f32[64,16,2,8,16]{0,4,1,3,2:T(8,128)S(1)} %bitcast.57) | data formatting | bytes 2097152 | tf_op jit(solution)/shard_map/transpose | solution.py:215
  88.3 6.1 %reshape.402 = f32[1024,256]{1,0:T(8,128)S(1)} reshape(f32[64,16,2,8,16]{4,3,2,1,0:T(8,128)} %copy.54) | data formatting | bytes 2097152 | tf_op jit(solution)/shard_map/reshape | solution.py:216
  94.4 0.0 copy-start.1
  94.4 1.3 copy.55
  95.8 0.6 copy-done.1
  96.4 0.0 copy-start
  96.4 0.0 copy-start.3
  96.4 3.4 %fusion.53 = f32[512,2,8,16]{0,3,2,1:T(8,128)S(1)} fusion(f32[512,1024,1,1]{0,1,3,2:T(8,128)S(1)} %bitcast.65, f32[2,8,16,1024]{3,2,1,0:T(8,128)} %bitcast.66), kind=kOutput, calls=%fused_computation.98 | convolution fusion | flops 1610612736 | bytes 3670016 | tf_op jit(solution)/shard_map/dot_general | solution.py:227
  99.8 0.0 copy-done
  99.8 0.0 copy-done.3
  99.8 2.0 fusion.54
  101.8 0.1 fusion.19
  102.0 0.0 copy-start.4
  102.0 2.0 copy.58
  104.0 2.9 %reshape.406 = bf16[64,2,1024]{2,1,0:T(2,128)(2,1)} reshape(bf16[512,2,8,16]{3,2,1,0:T(8,128)(2,1)S(1)} %bitcast.58) | data formatting | bytes 524288
  106.9 6.2 %all-to-all-start.2 = ((bf16[64,2,1024]{2,1,0:T(2,128)(2,1)}), bf16[64,2,1024]{2,1,0:T(2,128)(2,1)S(1)}, u32[]{:S(2)}, u32[]{:S(2)}) async-start(bf16[64,2,1024]{2,1,0:T(2,128)(2,1)} %reshape.406), calls=%async_computation.2 | async-start | bytes 524288 | tf_op jit(solution)/shard_map/all_to_all | solution.py:233
  113.1 0.0 copy-done.4
  113.1 0.9 maximum_bitcast_fusion.ph_ref
  114.0 9.9 %fusion.tm_ref = bf16[8,2,256,512]{3,2,1,0:T(8,128)(2,1)} fusion(bf16[256,2,8,512]{3,2,1,0:T(8,128)(2,1)} %param.7, pred[256,8]{0,1:T(8,128)(4,1)S(1)} %broadcast_compare_fusion), kind=kLoop, calls=%fused_computation.1 | loop fusion | flops 2097152 | bytes 8390656 | tf_op jit(solution)/shard_map/transpose | solution.py:76
  123.9 1.3 all-to-all-done.2
  125.1 1.4 reshape.407
  126.6 1.9 copy.74
  128.5 2.6 %copy.61.x_ref = bf16[16,2,8,512]{3,2,1,0:T(8,128)(2,1)} copy(bf16[16,2,8,512]{0,3,2,1:T(8,128)(2,1)} %bitcast.60) | data formatting | bytes 524288 | tf_op jit(solution)/shard_map/all_to_all | solution.py:233
  131.1 17.5 %shard_map.55 = bf16[4,16,2,8,512]{4,3,2,1,0:T(8,128)(2,1)} custom-call(bf16[16,2,8,512]{3,2,1,0:T(8,128)(2,1)} %copy.61.x_ref), custom_call_target="tpu_custom_call" | custom-call | tf_op jit(solution)/shard_map/pallas_call | solution.py:174
  148.6 2.8 %copy.62 = bf16[4,8,2,2,8,512]{5,1,0,2,3,4:T(8,128)(2,1)} copy(bf16[4,8,2,2,8,512]{5,4,3,2,1,0:T(8,128)(2,1)} %bitcast.63) | data formatting | bytes 2097152 | tf_op jit(solution)/shard_map/reshape;reshape | solution.py:242
  151.4 18.7 %shard_map.56.x_ref = f32[64,32,256]{2,1,0:T(8,128)} custom-call(f32[8,2,16,512]{3,2,1,0:T(8,128)} %maximum_bitcast_fusion.ph_ref, bf16[8,2,64,512]{3,2,1,0:T(8,128)(2,1)} %bitcast.68, bf16[8,2,256,512]{3,2,1,0:T(8,128)(2,1)} %fusion.tm_ref), custom_call_target="tpu_custom_call" | custom-call | flops 8589934592 | bytes 7864320 | tf_op jit(solution)/shard_map/pallas_call | solution.py:80
  170.1 6.3 %shard_map.57.x_ref = f32[32,32,256]{2,1,0:T(8,128)} custom-call(f32[64,32,256]{2,1,0:T(8,128)} %shard_map.56.x_ref), custom_call_target="tpu_custom_call" | custom-call | tf_op jit(solution)/shard_map/pallas_call | solution.py:131
  176.4 17.4 %shard_map.58.x_ref = f32[8,32,256]{2,1,0:T(8,128)} custom-call(f32[32,32,256]{2,1,0:T(8,128)} %shard_map.57.x_ref), custom_call_target="tpu_custom_call" | custom-call | tf_op jit(solution)/shard_map/pallas_call | solution.py:131
  193.8 12.3 %shard_map.59 = f32[1,32,256]{2,1,0:T(8,128)} custom-call(f32[8,32,256]{2,1,0:T(8,128)} %shard_map.58.x_ref), custom_call_target="tpu_custom_call" | custom-call | tf_op jit(solution)/shard_map/pallas_call | solution.py:131
  206.1 1.4 copy.76
  (5 shorter events, 0.1 us)
Async XLA Ops:
  7.7 30.5 %all-to-all-start = ((f32[64,8,256]{2,1,0:T(8,128)}), f32[64,8,256]{2,1,0:T(8,128)S(1)}, u32[]{:S(2)}, u32[]{:S(2)}) async-start(f32[64,8,256]{2,1,0:T(8,128)} %copy.49), calls=%async_computation | async-start | bytes 1048576 | tf_op jit(solution)/shard_map/all_to_all | solution.py:197
  38.2 1.8 copy-start.2
  40.2 11.7 %copy-start.7 = (s32[256]{0:T(256)S(1)}, s32[256]{0:T(256)}, u32[]{:S(2)}) copy-start(s32[256]{0:T(256)} %param.8) | copy-start | bytes 3076
  40.2 11.8 %copy-start.6 = (s32[16]{0:T(128)S(1)}, s32[16]{0:T(128)}, u32[]{:S(2)}) copy-start(s32[16]{0:T(128)} %param.9) | copy-start | bytes 196
  40.2 11.9 %copy-start.5 = (f32[512,8]{0,1:T(8,128)S(1)}, f32[512,8]{0,1:T(8,128)}, u32[]{:S(2)}) copy-start(f32[512,8]{0,1:T(8,128)} %param.6) | copy-start | bytes 49156
  41.3 38.9 %all-to-all-start.1 = ((f32[64,16,256]{2,1,0:T(8,128)}), f32[64,16,256]{2,1,0:T(8,128)S(1)}, u32[]{:S(2)}, u32[]{:S(2)}) async-start(f32[64,16,256]{2,1,0:T(8,128)} %copy_bitcast_fusion.1), calls=%async_computation.1 | async-start | bytes 2097152 | tf_op jit(solution)/shard_map/all_to_all | solution.py:214
  94.4 2.0 copy-start.1
  96.4 3.4 %copy-start = (f32[512,32,32]{0,2,1:T(8,128)S(1)}, f32[512,32,32]{0,2,1:T(8,128)}, u32[]{:S(2)}) copy-start(f32[512,32,32]{0,2,1:T(8,128)} %get-tuple-element.10) | copy-start | bytes 6291460
  96.4 3.4 %copy-start.3 = (f32[256,1024]{1,0:T(8,128)S(1)}, f32[256,1024]{1,0:T(8,128)}, u32[]{:S(2)}) copy-start(f32[256,1024]{1,0:T(8,128)} %copy.55) | copy-start | bytes 3145732
  102.0 11.1 %copy-start.4 = (f32[1,16,8,512]{3,1,0,2:T(8,128)S(1)}, f32[1,16,8,512]{3,1,0,2:T(8,128)}, u32[]{:S(2)}) copy-start(f32[1,16,8,512]{3,1,0,2:T(8,128)} %get-tuple-element.12) | copy-start | bytes 786436
  106.9 18.2 %all-to-all-start.2 = ((bf16[64,2,1024]{2,1,0:T(2,128)(2,1)}), bf16[64,2,1024]{2,1,0:T(2,128)(2,1)S(1)}, u32[]{:S(2)}, u32[]{:S(2)}) async-start(bf16[64,2,1024]{2,1,0:T(2,128)(2,1)} %reshape.406), calls=%async_computation.2 | async-start | bytes 524288 | tf_op jit(solution)/shard_map/all_to_all | solution.py:233

commit v11 on v10

--- a/solution.py
+++ b/solution.py
@@ -198,14 +198,15 @@
     both_parts = jnp.dot(first_table, slab, precision=highest)
     real_part = both_parts[:A]
     imag_part = both_parts[A:]
-    time_ids = freq_index * cols_here + jnp.arange(cols_here, dtype=jnp.int32)
+    column_ids = jnp.arange(cols_here * seg_local, dtype=jnp.int32) // seg_local
+    time_ids = freq_index * cols_here + column_ids
     twist_cos, twist_sin = cos_sin_table(jnp.arange(A, dtype=jnp.int32), time_ids, LEN)
     p_here = A // freq_count
     shaped = (freq_count, p_here, cols_here * seg_local)
     real_part = real_part.reshape(shaped)
     imag_part = imag_part.reshape(shaped)
-    twist_cos = jnp.repeat(twist_cos, seg_local, axis=1).reshape(shaped)
-    twist_sin = jnp.repeat(twist_sin, seg_local, axis=1).reshape(shaped)
+    twist_cos = twist_cos.reshape(shaped)
+    twist_sin = twist_sin.reshape(shaped)
     twisted = jnp.stack(
         [real_part * twist_cos + imag_part * twist_sin, imag_part * twist_cos - real_part * twist_sin],
         axis=1,

time: 208 us -> 206 us (level)
  local copies, waits for them, and re-layouts: 52.1 us -> 38.9 us
  waiting for transfers between devices: 24.4 us -> 37.5 us
  starting transfers between devices: 29.5 us -> 25.5 us
    all_to_all x1, waiting for transfers between devices: 0.01 us -> 13.2 us  [spectrum_blocks(): lax.all_to_all(sent, FREQ, 0, 0, tiled=True)]
    another operation x2 -> x0, local copies, waits for them, and re-layouts: 7.7 us -> none  [the longest x1 4.22 us: spectrum_blocks(): twist_cos = jnp.repeat(twist_cos, seg_local, axis=1).reshape(shaped)]
    broadcast_in_dim x2 -> x0, local copies, waits for them, and re-layouts: 5.14 us -> none  [the longest x1 2.57 us: spectrum_blocks(): twist_sin = jnp.repeat(twist_sin, seg_local, axis=1).reshape(shaped)]
    all_to_all x1, starting transfers between devices: 10.3 us -> 6.28 us  [spectrum_blocks(): columns = lax.all_to_all(twisted, FREQ, 0, 0, tiled=True)]
    add x1, other arithmetic: 0.14 us -> 2.34 us  [spectrum_blocks(): real_part * twist_cos + imag_part * twist_sin]
    unnamed x19 -> x17, local copies, waits for them, and re-layouts: 6.41 us -> 6.41 us
  transfers between devices with their start and end apart: 3 -> 3, of which waited for: 2 -> 3; matrix products, arithmetic and copies ran while one was open for 16% -> 10% of each run, Pallas kernels for 0% -> 0%
where the time goes in v11:
time: 206 us; the launch traced here: 205 us
  Pallas kernels  72.2 us (35%)
  local copies, waits for them, and re-layouts  38.9 us (19%)
  waiting for transfers between devices  37.5 us (18%)
  starting transfers between devices  25.5 us (12%)
  other arithmetic  23.8 us (12%)
  matrix products  7.21 us (4%)
    pallas_call x3, Pallas kernels, scatter_sum(): pl.pallas_call(functools.partial(scatter_kernel, axis, size), out_shape=j...  36 us
    all_to_all x1, waiting for transfers between devices, spectrum_blocks(): columns = lax.all_to_all(twisted, FREQ, 0, 0, tiled=True)  23.1 us
    pallas_call x1, Pallas kernels, intersect(): pl.pallas_call(intersect_kernel, out_shape=jax.ShapeDtypeStruct((seg_coun...  18.7 us
    pallas_call x1, Pallas kernels, gather_all(): pl.pallas_call(functools.partial(gather_kernel, axis, size), out_shape=ja...  17.5 us
    all_to_all x1, waiting for transfers between devices, spectrum_blocks(): lax.all_to_all(sent, FREQ, 0, 0, tiled=True)  13.2 us
    all_to_all x1, starting transfers between devices, spectrum_blocks(): lax.all_to_all(sent, FREQ, 0, 0, tiled=True)  13 us
    transpose x1, other arithmetic, intersect(): jnp.where(keep, templates, jnp.zeros_like(templates)).transpose(2, 1, 0, 3)  9.88 us
    transpose x1, local copies, waits for them, and re-layouts, spectrum_blocks(): columns.reshape(freq_count, 2, p_here, cols_here, seg_local)  7.44 us
  transfers between devices with their start and end apart: 3, of which 3 were waited for; matrix products, arithmetic and copies ran while one was open for 10% of the time, Pallas kernels for 0%

profile of v11, /device:TPU:1, one launch (start us, length us, event | category | flops | bytes accessed | tf_op | source)
XLA Modules:
  0.0 205.5 jit_solution(1200607915152995682)
XLA Ops:
  0.0 3.7 %reshape.455 = f32[16,8,64,16]{3,2,1,0:T(8,128)} reshape(f32[16,8192]{1,0:T(8,128)} %param.5) | data formatting | bytes 1048576 | tf_op jit(solution)/shard_map/reshape | solution.py:195
  3.7 2.9 %copy.40 = f32[64,8,16,16]{0,3,2,1:T(8,128)S(1)} copy(f32[64,8,16,16]{2,0,1,3:T(8,128)} %bitcast.62) | data formatting | bytes 1048576 | tf_op jit(solution)/shard_map/transpose | solution.py:195
  6.6 1.1 copy.41
  7.7 13.0 %all-to-all-start = ((f32[64,8,256]{2,1,0:T(8,128)}), f32[64,8,256]{2,1,0:T(8,128)S(1)}, u32[]{:S(2)}, u32[]{:S(2)}) async-start(f32[64,8,256]{2,1,0:T(8,128)} %copy.41), calls=%async_computation | async-start | bytes 1048576 | tf_op jit(solution)/shard_map/all_to_all | solution.py:197
  20.8 4.1 %sine_negate_fusion = (f32[512,512]{1,0:T(8,128)S(1)}, f32[512,512]{1,0:T(8,128)S(1)}) fusion(), kind=kLoop, calls=%fused_computation.16 | loop fusion | flops 3932160 | bytes 2097152 | tf_op jit(solution)/shard_map/neg | solution.py:194
  24.9 13.2 %all-to-all-done = f32[64,8,256]{2,1,0:T(8,128)S(1)} async-done(((f32[64,8,256]{2,1,0:T(8,128)}), f32[64,8,256]{2,1,0:T(8,128)S(1)}, u32[]{:S(2)}, u32[]{:S(2)}) %all-to-all-start) | async-done | bytes 524320 | tf_op jit(solution)/shard_map/all_to_all | solution.py:197
  38.0 1.8 fusion.1
  39.9 2.3 %multiply_add_fusion.1 = (f32[64,1,8,256]{3,2,1,0:T(8,128)S(1)}, f32[64,1,8,256]{3,2,1,0:T(8,128)S(1)}) fusion(f32[1024,256]{1,0:T(8,128)S(1)} %fusion.1, s32[256]{0:T(256)S(1)} %fusion.49, s32[64,8]{1,0:T(8,128)S(1)} %multiply_add_fusion.2), kind=kLoop, calls=%fused_computation.33 | loop fusion | flops 2621440 | bytes 2100224 | tf_op jit(solution)/shard_map/add | solution.py:211
  42.2 0.0 copy-start.6
  42.2 0.0 copy-start.5
  42.2 0.0 copy-start.4
  42.2 1.1 maximum_bitcast_fusion
  43.3 6.3 %all-to-all-start.1 = ((f32[64,16,256]{2,1,0:T(8,128)}), f32[64,16,256]{2,1,0:T(8,128)S(1)}, u32[]{:S(2)}, u32[]{:S(2)}) async-start(f32[64,16,256]{2,1,0:T(8,128)} %maximum_bitcast_fusion), calls=%async_computation.1 | async-start | bytes 2097152 | tf_op jit(solution)/shard_map/all_to_all | solution.py:215
  49.6 0.3 fusion.40
  49.9 0.0 copy-done.6
  49.9 0.1 broadcast_compare_fusion
  50.0 0.0 copy-done.5
  50.0 0.1 fusion.47
  50.1 0.0 copy-done.4
  50.1 0.1 add_select_fusion.6
  50.2 0.3 fusion.43
  50.5 1.9 fusion.26
  52.4 2.6 %multiply_subtract_fusion = (f32[512,32,32]{0,2,1:T(8,128)}, f32[512,32,32]{0,2,1:T(8,128)}) fusion(f32[512,32]{0,1:T(8,128)S(1)} %get-tuple-element.15, f32[512,32]{0,1:T(8,128)S(1)} %get-tuple-element.14, f32[512,32]{0,1:T(8,128)S(1)} %get-tuple-element.16, f32[512,32]{0,1:T(8,128)S(1)} %get-tuple-element.13), kind=kLoop, calls=%fused_computation.8 | loop fusion | flops 3145728 | bytes 4456448 | tf_op jit(solution)/shard_map/sub | solution.py:223
  55.1 23.1 %all-to-all-done.1 = f32[64,16,256]{2,1,0:T(8,128)S(1)} async-done(((f32[64,16,256]{2,1,0:T(8,128)}), f32[64,16,256]{2,1,0:T(8,128)S(1)}, u32[]{:S(2)}, u32[]{:S(2)}) %all-to-all-start.1) | async-done | bytes 1048608 | tf_op jit(solution)/shard_map/all_to_all | solution.py:215
  78.1 0.7 copy.46
  78.8 7.4 %copy.47 = f32[64,16,2,8,16]{4,3,2,1,0:T(8,128)} copy(f32[64,16,2,8,16]{0,4,1,3,2:T(8,128)S(1)} %bitcast.63) | data formatting | bytes 2097152 | tf_op jit(solution)/shard_map/transpose | solution.py:216
  86.3 6.1 %reshape.462 = f32[1024,256]{1,0:T(8,128)S(1)} reshape(f32[64,16,2,8,16]{4,3,2,1,0:T(8,128)} %copy.47) | data formatting | bytes 2097152 | tf_op jit(solution)/shard_map/reshape | solution.py:217
  92.4 0.0 copy-start.1
  92.4 1.3 copy.48
  93.7 0.6 copy-done.1
  94.4 0.0 copy-start
  94.4 0.0 copy-start.2
  94.4 3.4 %fusion.51 = f32[512,2,8,16]{0,3,2,1:T(8,128)S(1)} fusion(f32[512,1024,1,1]{0,1,3,2:T(8,128)S(1)} %bitcast.71, f32[2,8,16,1024]{3,2,1,0:T(8,128)} %bitcast.72), kind=kOutput, calls=%fused_computation.101 | convolution fusion | flops 1610612736 | bytes 3670016 | tf_op jit(solution)/shard_map/dot_general | solution.py:228
  97.7 0.0 copy-done
  97.7 0.0 copy-done.2
  97.8 2.0 fusion.52
  99.8 0.1 fusion.22
  100.0 0.0 copy-start.3
  100.0 2.0 copy.51
  101.9 2.9 %reshape.466 = bf16[64,2,1024]{2,1,0:T(2,128)(2,1)} reshape(bf16[512,2,8,16]{3,2,1,0:T(8,128)(2,1)S(1)} %bitcast.64) | data formatting | bytes 524288
  104.9 6.2 %all-to-all-start.2 = ((bf16[64,2,1024]{2,1,0:T(2,128)(2,1)}), bf16[64,2,1024]{2,1,0:T(2,128)(2,1)S(1)}, u32[]{:S(2)}, u32[]{:S(2)}) async-start(bf16[64,2,1024]{2,1,0:T(2,128)(2,1)} %reshape.466), calls=%async_computation.2 | async-start | bytes 524288 | tf_op jit(solution)/shard_map/all_to_all | solution.py:234
  111.1 0.0 copy-done.3
  111.1 0.8 maximum_bitcast_fusion.1.ph_ref
  111.9 9.9 %fusion.tm_ref = bf16[8,2,256,512]{3,2,1,0:T(8,128)(2,1)} fusion(bf16[256,2,8,512]{3,2,1,0:T(8,128)(2,1)} %param.7, pred[256,8]{0,1:T(8,128)(4,1)S(1)} %broadcast_compare_fusion), kind=kLoop, calls=%fused_computation.1 | loop fusion | flops 2097152 | bytes 8390656 | tf_op jit(solution)/shard_map/transpose | solution.py:76
  121.8 1.3 all-to-all-done.2
  123.1 1.4 reshape.467
  124.5 1.9 copy.66
  126.4 2.6 %copy.54.x_ref = bf16[16,2,8,512]{3,2,1,0:T(8,128)(2,1)} copy(bf16[16,2,8,512]{0,3,2,1:T(8,128)(2,1)} %bitcast.66) | data formatting | bytes 524288 | tf_op jit(solution)/shard_map/all_to_all | solution.py:234
  129.0 17.5 %shard_map.55 = bf16[4,16,2,8,512]{4,3,2,1,0:T(8,128)(2,1)} custom-call(bf16[16,2,8,512]{3,2,1,0:T(8,128)(2,1)} %copy.54.x_ref), custom_call_target="tpu_custom_call" | custom-call | tf_op jit(solution)/shard_map/pallas_call | solution.py:174
  146.5 2.8 %copy.55 = bf16[4,8,2,2,8,512]{5,1,0,2,3,4:T(8,128)(2,1)} copy(bf16[4,8,2,2,8,512]{5,4,3,2,1,0:T(8,128)(2,1)} %bitcast.69) | data formatting | bytes 2097152 | tf_op jit(solution)/shard_map/reshape;reshape | solution.py:243
  149.3 18.7 %shard_map.56.x_ref = f32[64,32,256]{2,1,0:T(8,128)} custom-call(f32[8,2,16,512]{3,2,1,0:T(8,128)} %maximum_bitcast_fusion.1.ph_ref, bf16[8,2,64,512]{3,2,1,0:T(8,128)(2,1)} %bitcast.74, bf16[8,2,256,512]{3,2,1,0:T(8,128)(2,1)} %fusion.tm_ref), custom_call_target="tpu_custom_call" | custom-call | flops 8589934592 | bytes 7864320 | tf_op jit(solution)/shard_map/pallas_call | solution.py:80
  168.0 6.3 %shard_map.57.x_ref = f32[32,32,256]{2,1,0:T(8,128)} custom-call(f32[64,32,256]{2,1,0:T(8,128)} %shard_map.56.x_ref), custom_call_target="tpu_custom_call" | custom-call | tf_op jit(solution)/shard_map/pallas_call | solution.py:131
  174.3 17.4 %shard_map.58.x_ref = f32[8,32,256]{2,1,0:T(8,128)} custom-call(f32[32,32,256]{2,1,0:T(8,128)} %shard_map.57.x_ref), custom_call_target="tpu_custom_call" | custom-call | tf_op jit(solution)/shard_map/pallas_call | solution.py:131
  191.7 12.3 %shard_map.59 = f32[1,32,256]{2,1,0:T(8,128)} custom-call(f32[8,32,256]{2,1,0:T(8,128)} %shard_map.58.x_ref), custom_call_target="tpu_custom_call" | custom-call | tf_op jit(solution)/shard_map/pallas_call | solution.py:131
  204.1 1.4 copy.68
  (6 shorter events, 0.1 us)
Async XLA Ops:
  7.7 30.3 %all-to-all-start = ((f32[64,8,256]{2,1,0:T(8,128)}), f32[64,8,256]{2,1,0:T(8,128)S(1)}, u32[]{:S(2)}, u32[]{:S(2)}) async-start(f32[64,8,256]{2,1,0:T(8,128)} %copy.41), calls=%async_computation | async-start | bytes 1048576 | tf_op jit(solution)/shard_map/all_to_all | solution.py:197
  42.2 7.7 %copy-start.6 = (s32[256]{0:T(256)S(1)}, s32[256]{0:T(256)}, u32[]{:S(2)}) copy-start(s32[256]{0:T(256)} %param.8) | copy-start | bytes 3076
  42.2 7.8 %copy-start.5 = (s32[16]{0:T(128)S(1)}, s32[16]{0:T(128)}, u32[]{:S(2)}) copy-start(s32[16]{0:T(128)} %param.9) | copy-start | bytes 196
  42.2 7.8 %copy-start.4 = (f32[512,8]{0,1:T(8,128)S(1)}, f32[512,8]{0,1:T(8,128)}, u32[]{:S(2)}) copy-start(f32[512,8]{0,1:T(8,128)} %param.6) | copy-start | bytes 49156
  43.3 34.8 %all-to-all-start.1 = ((f32[64,16,256]{2,1,0:T(8,128)}), f32[64,16,256]{2,1,0:T(8,128)S(1)}, u32[]{:S(2)}, u32[]{:S(2)}) async-start(f32[64,16,256]{2,1,0:T(8,128)} %maximum_bitcast_fusion), calls=%async_computation.1 | async-start | bytes 2097152 | tf_op jit(solution)/shard_map/all_to_all | solution.py:215
  92.4 2.0 copy-start.1
  94.4 3.4 %copy-start = (f32[512,32,32]{0,2,1:T(8,128)S(1)}, f32[512,32,32]{0,2,1:T(8,128)}, u32[]{:S(2)}) copy-start(f32[512,32,32]{0,2,1:T(8,128)} %get-tuple-element.10) | copy-start | bytes 6291460
  94.4 3.4 %copy-start.2 = (f32[256,1024]{1,0:T(8,128)S(1)}, f32[256,1024]{1,0:T(8,128)}, u32[]{:S(2)}) copy-start(f32[256,1024]{1,0:T(8,128)} %copy.48) | copy-start | bytes 3145732
  100.0 11.1 %copy-start.3 = (f32[1,16,8,512]{3,1,0,2:T(8,128)S(1)}, f32[1,16,8,512]{3,1,0,2:T(8,128)}, u32[]{:S(2)}) copy-start(f32[1,16,8,512]{3,1,0,2:T(8,128)} %get-tuple-element.12) | copy-start | bytes 786436
  104.9 18.2 %all-to-all-start.2 = ((bf16[64,2,1024]{2,1,0:T(2,128)(2,1)}), bf16[64,2,1024]{2,1,0:T(2,128)(2,1)S(1)}, u32[]{:S(2)}, u32[]{:S(2)}) async-start(bf16[64,2,1024]{2,1,0:T(2,128)(2,1)} %reshape.466), calls=%async_computation.2 | async-start | bytes 524288 | tf_op jit(solution)/shard_map/all_to_all | solution.py:234

commit v12 on v9

--- a/solution.py
+++ b/solution.py
@@ -50,7 +50,7 @@
         return carry
 
     lax.fori_loop(0, seg_count // chunk, build, 0)
-    dims = (((1,), (1,)), ((), ()))
+    dims = (((1,), (0,)), ((), ()))
     lhs = lhs_ref[...]
     with_re = lax.dot_general(lhs, tm_ref[0, 0], dims, preferred_element_type=jnp.float32)
     with_im = lax.dot_general(lhs, tm_ref[0, 1], dims, preferred_element_type=jnp.float32)
@@ -73,7 +73,7 @@
     phase_angle = (phase_int % LEN).astype(jnp.float32) * (two_pi / LEN)
     phases = jnp.stack([jnp.cos(phase_angle), jnp.sin(phase_angle)], axis=0).transpose(2, 0, 1, 3)
     keep = block_ids[None, None, :, None] < cutoffs[:, None, None, None]
-    masked = jnp.where(keep, templates, jnp.zeros_like(templates)).transpose(2, 1, 0, 3)
+    masked = jnp.where(keep, templates, jnp.zeros_like(templates)).transpose(2, 1, 3, 0)
     rows = seg_count * lag_total
     flops = 2 * 2 * (2 * rows) * width * tmpl_local * blocks_here
     moved = masked.size * 2 + data.size * 2 + phases.size * 4 + seg_count * 2 * lag_total * tmpl_local * 4
@@ -84,7 +84,7 @@
         in_specs=[
             pl.BlockSpec((1, 2, lag_total, width), lambda j: (j, 0, 0, 0)),
             pl.BlockSpec((1, 2, seg_count, width), lambda j: (j, 0, 0, 0)),
-            pl.BlockSpec((1, 2, tmpl_local, width), lambda j: (j, 0, 0, 0)),
+            pl.BlockSpec((1, 2, width, tmpl_local), lambda j: (j, 0, 0, 0)),
         ],
         out_specs=pl.BlockSpec((seg_count, 2 * lag_total, tmpl_local), lambda j: (0, 0, 0)),
         scratch_shapes=[pltpu.VMEM((2 * rows, width), jnp.bfloat16)],

time: 203 us -> 203 us (level)
  local copies, waits for them, and re-layouts: 39.9 us -> 47.4 us
  other arithmetic: 20.2 us -> 14.8 us
  waiting for transfers between devices: 36.7 us -> 34.6 us
    all_to_all x1, waiting for transfers between devices: 23.8 us -> 16.2 us  [spectrum_blocks(): lax.all_to_all(twisted, FREQ, 0, 0, tiled=True)]
    unnamed x15 -> x16, local copies, waits for them, and re-layouts: 5.76 us -> 13.3 us
    transpose x1, other arithmetic: 9.88 us -> 4.43 us  [intersect(): jnp.where(keep, templates, jnp.zeros_like(templates)).transpose(2, 1, 3, 0)]
    all_to_all x1, waiting for transfers between devices: 1.26 us -> 6.71 us  [spectrum_blocks(): lax.all_to_all(whitened, FREQ, split_axis=2, concat_axis=3, tiled=True)]
  transfers between devices with their start and end apart: 3 -> 3, of which waited for: 3 -> 3; matrix products, arithmetic and copies ran while one was open for 10% -> 12% of each run, Pallas kernels for 0% -> 0%
where the time goes in v12:
time: 203 us; the launch traced here: 201 us
  Pallas kernels  71.1 us (35%)
  local copies, waits for them, and re-layouts  47.4 us (23%)
  waiting for transfers between devices  34.6 us (17%)
  starting transfers between devices  25.5 us (13%)
  other arithmetic  14.8 us (7%)
  matrix products  7.78 us (4%)
    pallas_call x3, Pallas kernels, scatter_sum(): pl.pallas_call(functools.partial(scatter_kernel, axis, size), out_shape=j...  35.2 us
    pallas_call x1, Pallas kernels, intersect(): pl.pallas_call(intersect_kernel, out_shape=jax.ShapeDtypeStruct((seg_coun...  18.4 us
    pallas_call x1, Pallas kernels, gather_all(): pl.pallas_call(functools.partial(gather_kernel, axis, size), out_shape=ja...  17.5 us
    all_to_all x1, waiting for transfers between devices, spectrum_blocks(): lax.all_to_all(twisted, FREQ, 0, 0, tiled=True)  16.2 us
    unnamed x16, local copies, waits for them, and re-layouts  13.3 us
    all_to_all x1, starting transfers between devices, spectrum_blocks(): lax.all_to_all(sent, FREQ, 0, 0, tiled=True)  13 us
    another operation x4, local copies, waits for them, and re-layouts, spectrum_blocks(): jnp.stack([real_part * twist_cos + imag_part * twist_sin, imag_part * twi...  12.5 us
    all_to_all x1, waiting for transfers between devices, spectrum_blocks(): lax.all_to_all(sent, FREQ, 0, 0, tiled=True)  11.6 us
  transfers between devices with their start and end apart: 3, of which 3 were waited for; matrix products, arithmetic and copies ran while one was open for 12% of the time, Pallas kernels for 0%

profile of v12, /device:TPU:1, one launch (start us, length us, event | category | flops | bytes accessed | tf_op | source)
XLA Modules:
  0.0 201.4 jit_solution(14843319971857790366)
XLA Ops:
  0.0 3.7 %reshape.323 = f32[16,8,64,16]{3,2,1,0:T(8,128)} reshape(f32[16,8192]{1,0:T(8,128)} %param.5) | data formatting | bytes 1048576 | tf_op jit(solution)/shard_map/reshape | solution.py:195
  3.7 2.9 %copy.40 = f32[64,8,16,16]{0,3,2,1:T(8,128)S(1)} copy(f32[64,8,16,16]{2,0,1,3:T(8,128)} %bitcast.44) | data formatting | bytes 1048576 | tf_op jit(solution)/shard_map/transpose | solution.py:195
  6.6 1.1 copy.41
  7.7 13.0 %all-to-all-start = ((f32[64,8,256]{2,1,0:T(8,128)}), f32[64,8,256]{2,1,0:T(8,128)S(1)}, u32[]{:S(2)}, u32[]{:S(2)}) async-start(f32[64,8,256]{2,1,0:T(8,128)} %copy.41), calls=%async_computation | async-start | bytes 1048576 | tf_op jit(solution)/shard_map/all_to_all | solution.py:197
  20.7 0.2 fusion.48
  21.0 0.1 broadcast_in_dim.11
  21.0 0.2 copy.42
  21.2 0.1 broadcast_in_dim.12
  21.3 1.0 copy.43
  22.3 4.1 %sine_negate_fusion = (f32[512,512]{1,0:T(8,128)S(1)}, f32[512,512]{1,0:T(8,128)S(1)}) fusion(), kind=kLoop, calls=%fused_computation.15 | loop fusion | flops 3932160 | bytes 2097152 | tf_op jit(solution)/shard_map/neg | solution.py:194
  26.4 11.6 %all-to-all-done = f32[64,8,256]{2,1,0:T(8,128)S(1)} async-done(((f32[64,8,256]{2,1,0:T(8,128)}), f32[64,8,256]{2,1,0:T(8,128)S(1)}, u32[]{:S(2)}, u32[]{:S(2)}) %all-to-all-start) | async-done | bytes 524320 | tf_op jit(solution)/shard_map/all_to_all | solution.py:197
  38.0 0.0 copy-start
  38.0 1.8 fusion
  39.9 0.0 copy-done
  39.9 0.1 multiply_add_fusion.1
  40.0 2.6 %stack.21 = f32[1,64,8,16,16]{4,3,2,1,0:T(8,128)} reshape(f32[512,256]{1,0:T(8,128)S(1)} %get-tuple-element.5) | data formatting | bytes 1048576 | tf_op jit(solution)/shard_map/stack | solution.py:205
  42.6 3.6 %copy.46 = f32[1,64,8,16,16]{1,4,3,2,0:T(8,128)S(1)} copy(f32[1,64,8,16,16]{4,3,2,1,0:T(8,128)} %stack.21) | data formatting | bytes 1048576 | tf_op jit(solution)/shard_map/stack | solution.py:205
  46.3 2.6 %stack.22 = f32[1,64,8,16,16]{4,3,2,1,0:T(8,128)} reshape(f32[512,256]{1,0:T(8,128)S(1)} %get-tuple-element.6) | data formatting | bytes 1048576 | tf_op jit(solution)/shard_map/stack | solution.py:205
  48.9 3.6 %copy.47 = f32[1,64,8,16,16]{1,4,3,2,0:T(8,128)S(1)} copy(f32[1,64,8,16,16]{4,3,2,1,0:T(8,128)} %stack.22) | data formatting | bytes 1048576 | tf_op jit(solution)/shard_map/stack | solution.py:205
  52.5 0.2 maximum_bitcast_fusion
  52.7 0.2 copy.48
  52.9 1.8 copy.49
  54.7 6.3 %all-to-all-start.1 = ((f32[64,16,256]{2,1,0:T(8,128)}), f32[64,16,256]{2,1,0:T(8,128)S(1)}, u32[]{:S(2)}, u32[]{:S(2)}) async-start(f32[64,16,256]{2,1,0:T(8,128)} %copy.49), calls=%async_computation.1 | async-start | bytes 2097152 | tf_op jit(solution)/shard_map/all_to_all | solution.py:211
  61.0 0.0 copy-start.5
  61.0 0.0 copy-start.4
  61.0 0.0 copy-start.3
  61.0 7.5 %copy.58 = bf16[256,2,8,512]{0,3,1,2:T(8,128)(2,1)} copy(bf16[256,2,8,512]{3,2,1,0:T(8,128)(2,1)} %param.7) | data formatting | bytes 8388608 | tf_op args[2]
  68.6 0.3 fusion.39
  68.9 0.0 copy-done.5
  68.9 0.1 broadcast_compare_fusion
  69.0 0.0 copy-done.4
  69.0 0.1 fusion.49
  69.0 0.0 copy-done.3
  69.0 0.1 add_select_fusion.6
  69.1 0.3 fusion.42
  69.5 1.9 fusion.20
  71.4 2.0 multiply_subtract_fusion
  73.3 16.2 %all-to-all-done.1 = f32[64,16,256]{2,1,0:T(8,128)S(1)} async-done(((f32[64,16,256]{2,1,0:T(8,128)}), f32[64,16,256]{2,1,0:T(8,128)S(1)}, u32[]{:S(2)}, u32[]{:S(2)}) %all-to-all-start.1) | async-done | bytes 1048608 | tf_op jit(solution)/shard_map/all_to_all | solution.py:211
  89.6 1.3 copy.50
  90.9 0.0 copy-start.1
  90.9 3.9 %fusion.52 = f32[512,2,8,16]{0,3,2,1:T(8,128)S(1)} fusion(f32[512,1024,1,1]{0,1,3,2:T(8,128)} %bitcast.53, f32[2,8,16,1024]{3,2,1,0:T(8,128)} %bitcast.56), kind=kOutput, calls=%fused_computation.94 | convolution fusion | flops 1610612736 | bytes 3670016 | tf_op jit(solution)/shard_map/dot_general | solution.py:222
  94.8 0.0 copy-done.1
  94.8 2.0 %fusion.53 = f32[512,2,8,16]{0,3,2,1:T(8,128)S(1)} fusion(f32[512,1024,1,1]{0,1,3,2:T(8,128)S(1)} %bitcast.52, f32[2,8,16,1024]{3,2,1,0:T(8,128)S(1)} %bitcast.57), kind=kOutput, calls=%fused_computation.95 | convolution fusion | flops 1610612736 | bytes 3670016 | tf_op jit(solution)/shard_map/dot_general | solution.py:223
  96.9 0.1 fusion.18
  97.0 0.0 copy-start.2
  97.0 2.0 copy.53
  99.0 2.9 %reshape.333 = bf16[64,2,1024]{2,1,0:T(2,128)(2,1)} reshape(bf16[512,2,8,16]{3,2,1,0:T(8,128)(2,1)S(1)} %bitcast.45) | data formatting | bytes 524288
  101.9 6.2 %all-to-all-start.2 = ((bf16[64,2,1024]{2,1,0:T(2,128)(2,1)}), bf16[64,2,1024]{2,1,0:T(2,128)(2,1)S(1)}, u32[]{:S(2)}, u32[]{:S(2)}) async-start(bf16[64,2,1024]{2,1,0:T(2,128)(2,1)} %reshape.333), calls=%async_computation.2 | async-start | bytes 524288 | tf_op jit(solution)/shard_map/all_to_all | solution.py:228
  108.2 0.0 copy-done.2
  108.2 0.8 maximum_bitcast_fusion.1.ph_ref
  109.0 4.4 %select_bitcast_fusion.tm_ref = bf16[8,2,512,256]{3,2,1,0:T(8,128)(2,1)} fusion(bf16[256,2,8,512]{0,3,1,2:T(8,128)(2,1)} %copy.58, pred[256,8]{0,1:T(8,128)(4,1)S(1)} %broadcast_compare_fusion), kind=kLoop, calls=%fused_computation | loop fusion | flops 2097152 | bytes 8390656 | tf_op jit(solution)/shard_map/transpose | solution.py:76
  113.4 6.7 %all-to-all-done.2 = bf16[64,2,1024]{2,1,0:T(2,128)(2,1)S(1)} async-done(((bf16[64,2,1024]{2,1,0:T(2,128)(2,1)}), bf16[64,2,1024]{2,1,0:T(2,128)(2,1)S(1)}, u32[]{:S(2)}, u32[]{:S(2)}) %all-to-all-start.2) | async-done | bytes 262176 | tf_op jit(solution)/shard_map/all_to_all | solution.py:228
  120.2 1.4 reshape.334
  121.6 1.9 copy.65
  123.5 2.6 %copy.56.x_ref = bf16[16,2,8,512]{3,2,1,0:T(8,128)(2,1)} copy(bf16[16,2,8,512]{0,3,2,1:T(8,128)(2,1)} %bitcast.48) | data formatting | bytes 524288 | tf_op jit(solution)/shard_map/all_to_all | solution.py:228
  126.1 17.5 %shard_map.55 = bf16[4,16,2,8,512]{4,3,2,1,0:T(8,128)(2,1)} custom-call(bf16[16,2,8,512]{3,2,1,0:T(8,128)(2,1)} %copy.56.x_ref), custom_call_target="tpu_custom_call" | custom-call | tf_op jit(solution)/shard_map/pallas_call | solution.py:174
  143.6 2.8 %copy.57 = bf16[4,8,2,2,8,512]{5,1,0,2,3,4:T(8,128)(2,1)} copy(bf16[4,8,2,2,8,512]{5,4,3,2,1,0:T(8,128)(2,1)} %bitcast.50) | data formatting | bytes 2097152 | tf_op jit(solution)/shard_map/reshape;reshape | solution.py:237
  146.4 18.4 %shard_map.56.x_ref = f32[64,32,256]{2,1,0:T(8,128)} custom-call(f32[8,2,16,512]{3,2,1,0:T(8,128)} %maximum_bitcast_fusion.1.ph_ref, bf16[8,2,64,512]{3,2,1,0:T(8,128)(2,1)} %bitcast.58, bf16[8,2,512,256]{3,2,1,0:T(8,128)(2,1)} %select_bitcast_fusion.tm_ref), custom_call_target="tpu_custom_call" | custom-call | flops 8589934592 | bytes 7864320 | tf_op jit(solution)/shard_map/pallas_call | solution.py:80
  164.8 6.3 %shard_map.57.x_ref = f32[32,32,256]{2,1,0:T(8,128)} custom-call(f32[64,32,256]{2,1,0:T(8,128)} %shard_map.56.x_ref), custom_call_target="tpu_custom_call" | custom-call | tf_op jit(solution)/shard_map/pallas_call | solution.py:131
  171.1 17.4 %shard_map.58.x_ref = f32[8,32,256]{2,1,0:T(8,128)} custom-call(f32[32,32,256]{2,1,0:T(8,128)} %shard_map.57.x_ref), custom_call_target="tpu_custom_call" | custom-call | tf_op jit(solution)/shard_map/pallas_call | solution.py:131
  188.6 11.5 %shard_map.59 = f32[1,32,256]{2,1,0:T(8,128)} custom-call(f32[8,32,256]{2,1,0:T(8,128)} %shard_map.58.x_ref), custom_call_target="tpu_custom_call" | custom-call | tf_op jit(solution)/shard_map/pallas_call | solution.py:131
  200.0 1.4 copy.67
  (5 shorter events, 0.0 us)
Async XLA Ops:
  7.7 30.3 %all-to-all-start = ((f32[64,8,256]{2,1,0:T(8,128)}), f32[64,8,256]{2,1,0:T(8,128)S(1)}, u32[]{:S(2)}, u32[]{:S(2)}) async-start(f32[64,8,256]{2,1,0:T(8,128)} %copy.41), calls=%async_computation | async-start | bytes 1048576 | tf_op jit(solution)/shard_map/all_to_all | solution.py:197
  38.0 1.8 copy-start
  54.7 34.8 %all-to-all-start.1 = ((f32[64,16,256]{2,1,0:T(8,128)}), f32[64,16,256]{2,1,0:T(8,128)S(1)}, u32[]{:S(2)}, u32[]{:S(2)}) async-start(f32[64,16,256]{2,1,0:T(8,128)} %copy.49), calls=%async_computation.1 | async-start | bytes 2097152 | tf_op jit(solution)/shard_map/all_to_all | solution.py:211
  61.0 7.9 %copy-start.5 = (s32[256]{0:T(256)S(1)}, s32[256]{0:T(256)}, u32[]{:S(2)}) copy-start(s32[256]{0:T(256)} %param.8) | copy-start | bytes 3076
  61.0 7.9 %copy-start.4 = (s32[16]{0:T(128)S(1)}, s32[16]{0:T(128)}, u32[]{:S(2)}) copy-start(s32[16]{0:T(128)} %param.9) | copy-start | bytes 196
  61.0 8.0 %copy-start.3 = (f32[512,8]{0,1:T(8,128)S(1)}, f32[512,8]{0,1:T(8,128)}, u32[]{:S(2)}) copy-start(f32[512,8]{0,1:T(8,128)} %param.6) | copy-start | bytes 49156
  90.9 3.9 %copy-start.1 = (f32[256,1024]{1,0:T(8,128)S(1)}, f32[256,1024]{1,0:T(8,128)}, u32[]{:S(2)}) copy-start(f32[256,1024]{1,0:T(8,128)} %copy.50) | copy-start | bytes 3145732
  97.0 11.1 %copy-start.2 = (f32[1,16,8,512]{3,1,0,2:T(8,128)S(1)}, f32[1,16,8,512]{3,1,0,2:T(8,128)}, u32[]{:S(2)}) copy-start(f32[1,16,8,512]{3,1,0,2:T(8,128)} %get-tuple-element.12) | copy-start | bytes 786436
  101.9 18.2 %all-to-all-start.2 = ((bf16[64,2,1024]{2,1,0:T(2,128)(2,1)}), bf16[64,2,1024]{2,1,0:T(2,128)(2,1)S(1)}, u32[]{:S(2)}, u32[]{:S(2)}) async-start(bf16[64,2,1024]{2,1,0:T(2,128)(2,1)} %reshape.333), calls=%async_computation.2 | async-start | bytes 524288 | tf_op jit(solution)/shard_map/all_to_all | solution.py:228

commit v13 on v12

--- a/solution.py
+++ b/solution.py
@@ -26,10 +26,10 @@
 
 def intersect_kernel(ph_ref, dat_ref, tm_ref, out_ref, lhs_ref):
     step = pl.program_id(0)
-    seg_count = dat_ref.shape[2]
+    tmpl_count, _, _, core_count, chunk, _ = dat_ref.shape
+    seg_count = tmpl_count * core_count * chunk
     lag_total = ph_ref.shape[2]
     rows = seg_count * lag_total
-    chunk = 8
 
     @pl.when(step == 0)
     def _():
@@ -39,9 +39,10 @@
     lag_sin = ph_ref[0, 1][None]
 
     def build(i, carry):
-        s0 = pl.multiple_of(i * chunk, chunk)
-        data_real = dat_ref[0, 0, pl.ds(s0, chunk), :].astype(jnp.float32)[:, None, :]
-        data_imag = dat_ref[0, 1, pl.ds(s0, chunk), :].astype(jnp.float32)[:, None, :]
+        row = lax.rem(i, tmpl_count)
+        core = i // tmpl_count
+        data_real = dat_ref[row, 0, 0, core].astype(jnp.float32)[:, None, :]
+        data_imag = dat_ref[row, 0, 1, core].astype(jnp.float32)[:, None, :]
         real_q = data_real * lag_cos - data_imag * lag_sin
         imag_q = data_real * lag_sin + data_imag * lag_cos
         r0 = pl.multiple_of(i * chunk * lag_total, chunk * lag_total)
@@ -62,7 +63,8 @@
 
 
 def intersect(data, templates, cutoffs, lags, first_block):
-    blocks_here, _, seg_count, width = data.shape
+    tmpl_count, blocks_here, _, core_count, chunk, width = data.shape
+    seg_count = tmpl_count * core_count * chunk
     tmpl_local = templates.shape[0]
     lag_total = lags.shape[0]
     block_ids = first_block + jnp.arange(blocks_here, dtype=jnp.int32)
@@ -83,7 +85,7 @@
         grid=(blocks_here,),
         in_specs=[
             pl.BlockSpec((1, 2, lag_total, width), lambda j: (j, 0, 0, 0)),
-            pl.BlockSpec((1, 2, seg_count, width), lambda j: (j, 0, 0, 0)),
+            pl.BlockSpec((tmpl_count, 1, 2, core_count, chunk, width), lambda j: (0, j, 0, 0, 0, 0)),
             pl.BlockSpec((1, 2, width, tmpl_local), lambda j: (j, 0, 0, 0)),
         ],
         out_specs=pl.BlockSpec((seg_count, 2 * lag_total, tmpl_local), lambda j: (0, 0, 0)),
@@ -231,13 +233,10 @@
 def on_device(strain, psd, templates, cutoffs, lags):
     freq_index = lax.axis_index(FREQ)
     local_data = spectrum_blocks(strain, psd)
-    seg_piece = gather_all(local_data, "tmpl", 4)
-    seg_piece = seg_piece.reshape((-1,) + local_data.shape[1:])
     x_size, z_size, c_size = (lax.axis_size(name) for name in FREQ)
-    seg_order = seg_piece.reshape((x_size, z_size, c_size) + seg_piece.shape[1:])
-    seg_order = seg_order.transpose(2, 0, 1, 3, 4, 5).reshape(seg_piece.shape)
-    data = seg_order.transpose(2, 1, 0, 3)
-    j_here = data.shape[0]
+    seg_local, _, j_here, width = local_data.shape
+    local = local_data.reshape(z_size, c_size, 2, j_here, width).transpose(3, 2, 1, 0, 4)
+    data = gather_all(local, "tmpl", 4)
     first_block = freq_index * j_here
     partial_sums = intersect(data, templates, cutoffs, lags, first_block)
     for collective_id, name in enumerate(("fc", "fx", "fz")):

time: 203 us -> 212 us (1.044)
  local copies, waits for them, and re-layouts: 47.4 us -> 55.9 us
    reshape x0 -> x2, local copies, waits for them, and re-layouts: none -> 7.89 us  [on_device(): local_data.reshape(z_size, c_size, 2, j_here, width)]
    all_to_all x2 -> x1, local copies, waits for them, and re-layouts: 4.53 us -> 7.92 us  [spectrum_blocks(): lax.all_to_all(whitened, FREQ, split_axis=2, concat_axis=3, tiled=True)]
    another operation x1 -> x0, local copies, waits for them, and re-layouts: 2.78 us -> none  [on_device(): seg_piece.reshape((x_size, z_size, c_size) + seg_piece.shape[1:])]
  transfers between devices with their start and end apart: 3 -> 3, of which waited for: 3 -> 3; matrix products, arithmetic and copies ran while one was open for 12% -> 11% of each run, Pallas kernels for 0% -> 0%
where the time goes in v13:
time: 212 us; the launch traced here: 210 us
  Pallas kernels  71.5 us (34%)
  local copies, waits for them, and re-layouts  55.9 us (26%)
  waiting for transfers between devices  34.5 us (16%)
  starting transfers between devices  25.5 us (12%)
  other arithmetic  14.8 us (7%)
  matrix products  7.78 us (4%)
    pallas_call x3, Pallas kernels, scatter_sum(): pl.pallas_call(functools.partial(scatter_kernel, axis, size), out_shape=j...  35.2 us
    pallas_call x1, Pallas kernels, intersect(): pl.pallas_call(intersect_kernel, out_shape=jax.ShapeDtypeStruct((seg_coun...  18.8 us
    pallas_call x1, Pallas kernels, gather_all(): pl.pallas_call(functools.partial(gather_kernel, axis, size), out_shape=ja...  17.5 us
    all_to_all x1, waiting for transfers between devices, spectrum_blocks(): lax.all_to_all(twisted, FREQ, 0, 0, tiled=True)  16.2 us
    unnamed x16, local copies, waits for them, and re-layouts  13.3 us
    all_to_all x1, starting transfers between devices, spectrum_blocks(): lax.all_to_all(sent, FREQ, 0, 0, tiled=True)  13 us
    another operation x4, local copies, waits for them, and re-layouts, spectrum_blocks(): jnp.stack([real_part * twist_cos + imag_part * twist_sin, imag_part * twi...  12.5 us
    all_to_all x1, waiting for transfers between devices, spectrum_blocks(): lax.all_to_all(sent, FREQ, 0, 0, tiled=True)  11.6 us
  transfers between devices with their start and end apart: 3, of which 3 were waited for; matrix products, arithmetic and copies ran while one was open for 11% of the time, Pallas kernels for 0%

profile of v13, /device:TPU:1, one launch (start us, length us, event | category | flops | bytes accessed | tf_op | source)
XLA Modules:
  0.0 210.3 jit_solution(8024606676161121726)
XLA Ops:
  0.0 3.7 %reshape.324 = f32[16,8,64,16]{3,2,1,0:T(8,128)} reshape(f32[16,8192]{1,0:T(8,128)} %param.5) | data formatting | bytes 1048576 | tf_op jit(solution)/shard_map/reshape | solution.py:197
  3.7 2.9 %copy.36 = f32[64,8,16,16]{0,3,2,1:T(8,128)S(1)} copy(f32[64,8,16,16]{2,0,1,3:T(8,128)} %bitcast.40) | data formatting | bytes 1048576 | tf_op jit(solution)/shard_map/transpose | solution.py:197
  6.6 1.1 copy.37
  7.7 13.0 %all-to-all-start = ((f32[64,8,256]{2,1,0:T(8,128)}), f32[64,8,256]{2,1,0:T(8,128)S(1)}, u32[]{:S(2)}, u32[]{:S(2)}) async-start(f32[64,8,256]{2,1,0:T(8,128)} %copy.37), calls=%async_computation | async-start | bytes 1048576 | tf_op jit(solution)/shard_map/all_to_all | solution.py:199
  20.7 0.2 fusion.48
  21.0 0.1 broadcast_in_dim.11
  21.0 0.2 copy.38
  21.2 0.1 broadcast_in_dim.12
  21.3 1.0 copy.39
  22.3 4.1 %sine_negate_fusion = (f32[512,512]{1,0:T(8,128)S(1)}, f32[512,512]{1,0:T(8,128)S(1)}) fusion(), kind=kLoop, calls=%fused_computation.14 | loop fusion | flops 3932160 | bytes 2097152 | tf_op jit(solution)/shard_map/neg | solution.py:196
  26.4 11.6 %all-to-all-done = f32[64,8,256]{2,1,0:T(8,128)S(1)} async-done(((f32[64,8,256]{2,1,0:T(8,128)}), f32[64,8,256]{2,1,0:T(8,128)S(1)}, u32[]{:S(2)}, u32[]{:S(2)}) %all-to-all-start) | async-done | bytes 524320 | tf_op jit(solution)/shard_map/all_to_all | solution.py:199
  38.0 0.0 copy-start
  38.0 1.8 fusion
  39.9 0.0 copy-done
  39.9 0.1 multiply_add_fusion.1
  40.0 2.6 %stack.21 = f32[1,64,8,16,16]{4,3,2,1,0:T(8,128)} reshape(f32[512,256]{1,0:T(8,128)S(1)} %get-tuple-element.5) | data formatting | bytes 1048576 | tf_op jit(solution)/shard_map/stack | solution.py:207
  42.6 3.6 %copy.42 = f32[1,64,8,16,16]{1,4,3,2,0:T(8,128)S(1)} copy(f32[1,64,8,16,16]{4,3,2,1,0:T(8,128)} %stack.21) | data formatting | bytes 1048576 | tf_op jit(solution)/shard_map/stack | solution.py:207
  46.3 2.6 %stack.22 = f32[1,64,8,16,16]{4,3,2,1,0:T(8,128)} reshape(f32[512,256]{1,0:T(8,128)S(1)} %get-tuple-element.6) | data formatting | bytes 1048576 | tf_op jit(solution)/shard_map/stack | solution.py:207
  48.9 3.6 %copy.43 = f32[1,64,8,16,16]{1,4,3,2,0:T(8,128)S(1)} copy(f32[1,64,8,16,16]{4,3,2,1,0:T(8,128)} %stack.22) | data formatting | bytes 1048576 | tf_op jit(solution)/shard_map/stack | solution.py:207
  52.5 0.2 maximum_bitcast_fusion
  52.7 0.2 copy.44
  52.9 1.8 copy.45
  54.7 6.3 %all-to-all-start.1 = ((f32[64,16,256]{2,1,0:T(8,128)}), f32[64,16,256]{2,1,0:T(8,128)S(1)}, u32[]{:S(2)}, u32[]{:S(2)}) async-start(f32[64,16,256]{2,1,0:T(8,128)} %copy.45), calls=%async_computation.1 | async-start | bytes 2097152 | tf_op jit(solution)/shard_map/all_to_all | solution.py:213
  61.0 0.0 copy-start.5
  61.0 0.0 copy-start.4
  61.0 0.0 copy-start.3
  61.0 7.5 %copy.53 = bf16[256,2,8,512]{0,3,1,2:T(8,128)(2,1)} copy(bf16[256,2,8,512]{3,2,1,0:T(8,128)(2,1)} %param.7) | data formatting | bytes 8388608 | tf_op args[2]
  68.6 0.3 fusion.39
  68.9 0.0 copy-done.5
  68.9 0.1 broadcast_compare_fusion
  69.0 0.0 copy-done.4
  69.0 0.1 fusion.49
  69.0 0.0 copy-done.3
  69.0 0.1 add_select_fusion.6
  69.1 0.3 fusion.42
  69.5 1.9 fusion.20
  71.4 2.0 multiply_subtract_fusion
  73.3 16.2 %all-to-all-done.1 = f32[64,16,256]{2,1,0:T(8,128)S(1)} async-done(((f32[64,16,256]{2,1,0:T(8,128)}), f32[64,16,256]{2,1,0:T(8,128)S(1)}, u32[]{:S(2)}, u32[]{:S(2)}) %all-to-all-start.1) | async-done | bytes 1048608 | tf_op jit(solution)/shard_map/all_to_all | solution.py:213
  89.6 1.3 copy.46
  90.9 0.0 copy-start.1
  90.9 3.9 %fusion.52 = f32[512,2,8,16]{0,3,2,1:T(8,128)S(1)} fusion(f32[512,1024,1,1]{0,1,3,2:T(8,128)} %bitcast.47, f32[2,8,16,1024]{3,2,1,0:T(8,128)} %bitcast.51), kind=kOutput, calls=%fused_computation.94 | convolution fusion | flops 1610612736 | bytes 3670016 | tf_op jit(solution)/shard_map/dot_general | solution.py:224
  94.8 0.0 copy-done.1
  94.8 2.0 fusion.53
  96.9 0.1 fusion.18
  97.0 0.0 copy-start.2
  97.0 2.0 copy.49
  99.0 2.9 %reshape.334 = bf16[64,2,1024]{2,1,0:T(2,128)(2,1)} reshape(bf16[512,2,8,16]{3,2,1,0:T(8,128)(2,1)S(1)} %bitcast.42) | data formatting | bytes 524288
  101.9 6.2 %all-to-all-start.2 = ((bf16[64,2,1024]{2,1,0:T(2,128)(2,1)}), bf16[64,2,1024]{2,1,0:T(2,128)(2,1)S(1)}, u32[]{:S(2)}, u32[]{:S(2)}) async-start(bf16[64,2,1024]{2,1,0:T(2,128)(2,1)} %reshape.334), calls=%async_computation.2 | async-start | bytes 524288 | tf_op jit(solution)/shard_map/all_to_all | solution.py:230
  108.2 0.0 copy-done.2
  108.2 0.9 maximum_bitcast_fusion.1.ph_ref
  109.1 4.4 %select_bitcast_fusion.tm_ref = bf16[8,2,512,256]{3,2,1,0:T(8,128)(2,1)} fusion(bf16[256,2,8,512]{0,3,1,2:T(8,128)(2,1)} %copy.53, pred[256,8]{0,1:T(8,128)(4,1)S(1)} %broadcast_compare_fusion), kind=kLoop, calls=%fused_computation | loop fusion | flops 2097152 | bytes 8390656 | tf_op jit(solution)/shard_map/transpose | solution.py:78
  113.5 6.7 %all-to-all-done.2 = bf16[64,2,1024]{2,1,0:T(2,128)(2,1)S(1)} async-done(((bf16[64,2,1024]{2,1,0:T(2,128)(2,1)}), bf16[64,2,1024]{2,1,0:T(2,128)(2,1)S(1)}, u32[]{:S(2)}, u32[]{:S(2)}) %all-to-all-start.2) | async-done | bytes 262176 | tf_op jit(solution)/shard_map/all_to_all | solution.py:230
  120.1 1.4 reshape.335
  121.6 7.9 %copy.51 = bf16[16,2,8,64,8]{4,3,2,1,0:T(8,128)(2,1)} copy(bf16[16,2,8,64,8]{0,4,1,2,3:T(8,128)(2,1)S(1)} %bitcast.41) | data formatting | bytes 524288 | tf_op jit(solution)/shard_map/all_to_all | solution.py:230
  129.5 7.0 %reshape.331 = bf16[8,2,2,8,512]{4,3,2,1,0:T(8,128)(2,1)S(1)} reshape(bf16[16,2,8,64,8]{4,3,2,1,0:T(8,128)(2,1)} %copy.51) | data formatting | bytes 524288 | tf_op jit(solution)/shard_map/reshape | solution.py:238
  136.5 0.8 copy.60
  137.4 17.5 %shard_map.55.dat_ref = bf16[4,8,2,2,8,512]{5,4,3,2,1,0:T(8,128)(2,1)} custom-call(bf16[8,2,2,8,512]{4,3,2,1,0:T(8,128)(2,1)} %bitcast.50), custom_call_target="tpu_custom_call" | custom-call | tf_op jit(solution)/shard_map/pallas_call | solution.py:176
  154.9 18.8 %shard_map.56.x_ref = f32[64,32,256]{2,1,0:T(8,128)} custom-call(f32[8,2,16,512]{3,2,1,0:T(8,128)} %maximum_bitcast_fusion.1.ph_ref, bf16[4,8,2,2,8,512]{5,4,3,2,1,0:T(8,128)(2,1)} %shard_map.55.dat_ref, bf16[8,2,512,256]{3,2,1,0:T(8,128)(2,1)} %select_bitcast_fusion.tm_ref), custom_call_target="tpu_custom_call" | custom-call | flops 8589934592 | bytes 7864320 | tf_op jit(solution)/shard_map/pallas_call | solution.py:82
  173.8 6.3 %shard_map.57.x_ref = f32[32,32,256]{2,1,0:T(8,128)} custom-call(f32[64,32,256]{2,1,0:T(8,128)} %shard_map.56.x_ref), custom_call_target="tpu_custom_call" | custom-call | tf_op jit(solution)/shard_map/pallas_call | solution.py:133
  180.0 17.4 %shard_map.58.x_ref = f32[8,32,256]{2,1,0:T(8,128)} custom-call(f32[32,32,256]{2,1,0:T(8,128)} %shard_map.57.x_ref), custom_call_target="tpu_custom_call" | custom-call | tf_op jit(solution)/shard_map/pallas_call | solution.py:133
  197.5 11.5 %shard_map.59 = f32[1,32,256]{2,1,0:T(8,128)} custom-call(f32[8,32,256]{2,1,0:T(8,128)} %shard_map.58.x_ref), custom_call_target="tpu_custom_call" | custom-call | tf_op jit(solution)/shard_map/pallas_call | solution.py:133
  208.9 1.4 copy.62
  (5 shorter events, 0.0 us)
Async XLA Ops:
  7.7 30.3 %all-to-all-start = ((f32[64,8,256]{2,1,0:T(8,128)}), f32[64,8,256]{2,1,0:T(8,128)S(1)}, u32[]{:S(2)}, u32[]{:S(2)}) async-start(f32[64,8,256]{2,1,0:T(8,128)} %copy.37), calls=%async_computation | async-start | bytes 1048576 | tf_op jit(solution)/shard_map/all_to_all | solution.py:199
  38.0 1.8 copy-start
  54.7 34.8 %all-to-all-start.1 = ((f32[64,16,256]{2,1,0:T(8,128)}), f32[64,16,256]{2,1,0:T(8,128)S(1)}, u32[]{:S(2)}, u32[]{:S(2)}) async-start(f32[64,16,256]{2,1,0:T(8,128)} %copy.45), calls=%async_computation.1 | async-start | bytes 2097152 | tf_op jit(solution)/shard_map/all_to_all | solution.py:213
  61.0 7.9 %copy-start.5 = (s32[256]{0:T(256)S(1)}, s32[256]{0:T(256)}, u32[]{:S(2)}) copy-start(s32[256]{0:T(256)} %param.8) | copy-start | bytes 3076
  61.0 7.9 %copy-start.4 = (s32[16]{0:T(128)S(1)}, s32[16]{0:T(128)}, u32[]{:S(2)}) copy-start(s32[16]{0:T(128)} %param.9) | copy-start | bytes 196
  61.0 8.0 %copy-start.3 = (f32[512,8]{0,1:T(8,128)S(1)}, f32[512,8]{0,1:T(8,128)}, u32[]{:S(2)}) copy-start(f32[512,8]{0,1:T(8,128)} %param.6) | copy-start | bytes 49156
  90.9 3.9 %copy-start.1 = (f32[256,1024]{1,0:T(8,128)S(1)}, f32[256,1024]{1,0:T(8,128)}, u32[]{:S(2)}) copy-start(f32[256,1024]{1,0:T(8,128)} %copy.46) | copy-start | bytes 3145732
  97.0 11.1 %copy-start.2 = (f32[1,16,8,512]{3,1,0,2:T(8,128)S(1)}, f32[1,16,8,512]{3,1,0,2:T(8,128)}, u32[]{:S(2)}) copy-start(f32[1,16,8,512]{3,1,0,2:T(8,128)} %get-tuple-element.12) | copy-start | bytes 786436
  101.9 18.2 %all-to-all-start.2 = ((bf16[64,2,1024]{2,1,0:T(2,128)(2,1)}), bf16[64,2,1024]{2,1,0:T(2,128)(2,1)S(1)}, u32[]{:S(2)}, u32[]{:S(2)}) async-start(bf16[64,2,1024]{2,1,0:T(2,128)(2,1)} %reshape.334), calls=%async_computation.2 | async-start | bytes 524288 | tf_op jit(solution)/shard_map/all_to_all | solution.py:230

commit v14 on v9

--- a/solution.py
+++ b/solution.py
@@ -93,24 +93,32 @@
     )(phases, data, masked)
 
 
-def scatter_kernel(axis, size, x_ref, o_ref, recv_ref, send_sem, recv_sem):
-    me = lax.axis_index(axis)
+def peer_id(axes, flat):
+    coords = {}
+    for name in reversed(axes):
+        coords[name] = lax.rem(flat, lax.axis_size(name))
+        flat = flat // lax.axis_size(name)
+    return coords
+
+
+def scatter_kernel(axes, size, x_ref, o_ref, recv_ref, send_sem, recv_sem):
+    me = lax.axis_index(axes)
     piece = o_ref.shape[0]
     mesh_ids = pl.DeviceIdType.MESH
     barrier = pltpu.get_barrier_semaphore()
     for k in range(1, size):
-        peer = lax.rem(me + k, size)
-        pl.semaphore_signal(barrier, inc=1, device_id={axis: peer}, device_id_type=mesh_ids)
+        peer = peer_id(axes, lax.rem(me + k, size))
+        pl.semaphore_signal(barrier, inc=1, device_id=peer, device_id_type=mesh_ids)
     pl.semaphore_wait(barrier, size - 1)
     copies = []
     for k in range(1, size):
-        peer = lax.rem(me + k, size)
+        flat = lax.rem(me + k, size)
         copy = pltpu.make_async_remote_copy(
-            src_ref=x_ref.at[pl.ds(peer * piece, piece)],
+            src_ref=x_ref.at[pl.ds(flat * piece, piece)],
             dst_ref=recv_ref.at[k],
             send_sem=send_sem.at[k],
             recv_sem=recv_sem.at[k],
-            device_id={axis: peer},
+            device_id=peer_id(axes, flat),
             device_id_type=mesh_ids,
         )
         copy.start()
@@ -123,13 +131,13 @@
     o_ref[...] = total
 
 
-def scatter_sum(parts, axis, collective_id):
-    size = lax.axis_size(axis)
+def scatter_sum(parts, axes, collective_id):
+    size = lax.axis_size(axes)
     piece = parts.shape[0] // size
     out_shape = (piece,) + parts.shape[1:]
     vmem = pltpu.VMEM
     return pl.pallas_call(
-        functools.partial(scatter_kernel, axis, size),
+        functools.partial(scatter_kernel, axes, size),
         out_shape=jax.ShapeDtypeStruct(out_shape, parts.dtype),
         in_specs=[pl.BlockSpec(memory_space=vmem)],
         out_specs=pl.BlockSpec(memory_space=vmem),
@@ -240,8 +248,8 @@
     j_here = data.shape[0]
     first_block = freq_index * j_here
     partial_sums = intersect(data, templates, cutoffs, lags, first_block)
-    for collective_id, name in enumerate(("fc", "fx", "fz")):
-        partial_sums = scatter_sum(partial_sums, name, collective_id + 1)
+    for collective_id, axes in enumerate((("fc",), ("fx", "fz"))):
+        partial_sums = scatter_sum(partial_sums, axes, collective_id + 1)
     return partial_sums
 
 

time: 203 us -> 206 us (1.015)
  Pallas kernels: 72.2 us -> 75.6 us
    pallas_call x3 -> x2, Pallas kernels: 36 us -> 39.4 us  [scatter_sum(): pl.pallas_call(functools.partial(scatter_kernel, axes, size), out_shape=j...]
where the time goes in v14:
time: 206 us
  Pallas kernels  75.6 us (37%)
  local copies, waits for them, and re-layouts  39.9 us (19%)
  waiting for transfers between devices  36.7 us (18%)
  starting transfers between devices  25.5 us (12%)
  other arithmetic  20.2 us (10%)
  matrix products  7.78 us (4%)
    pallas_call x2, Pallas kernels, scatter_sum(): pl.pallas_call(functools.partial(scatter_kernel, axes, size), out_shape=j...  39.4 us
    all_to_all x1, waiting for transfers between devices, spectrum_blocks(): lax.all_to_all(twisted, FREQ, 0, 0, tiled=True)  23.8 us
    pallas_call x1, Pallas kernels, intersect(): pl.pallas_call(intersect_kernel, out_shape=jax.ShapeDtypeStruct((seg_coun...  18.7 us
    pallas_call x1, Pallas kernels, gather_all(): pl.pallas_call(functools.partial(gather_kernel, axis, size), out_shape=ja...  17.5 us
    all_to_all x1, starting transfers between devices, spectrum_blocks(): lax.all_to_all(sent, FREQ, 0, 0, tiled=True)  13 us
    another operation x4, local copies, waits for them, and re-layouts, spectrum_blocks(): jnp.stack([real_part * twist_cos + imag_part * twist_sin, imag_part * twi...  12.5 us
    all_to_all x1, waiting for transfers between devices, spectrum_blocks(): lax.all_to_all(sent, FREQ, 0, 0, tiled=True)  11.6 us
    transpose x1, other arithmetic, intersect(): jnp.where(keep, templates, jnp.zeros_like(templates)).transpose(2, 1, 0, 3)  9.88 us
  transfers between devices with their start and end apart: 3, of which 3 were waited for; matrix products, arithmetic and copies ran while one was open for 10% of the time, Pallas kernels for 0%

profile of v14, /device:TPU:1, one launch (start us, length us, event | category | flops | bytes accessed | tf_op | source)
XLA Modules:
  0.0 205.9 jit_solution(6200482076564531537)
XLA Ops:
  0.0 3.7 %reshape.323 = f32[16,8,64,16]{3,2,1,0:T(8,128)} reshape(f32[16,8192]{1,0:T(8,128)} %param.5) | data formatting | bytes 1048576 | tf_op jit(solution)/shard_map/reshape | solution.py:203
  3.7 2.9 %copy.40 = f32[64,8,16,16]{0,3,2,1:T(8,128)S(1)} copy(f32[64,8,16,16]{2,0,1,3:T(8,128)} %bitcast.44) | data formatting | bytes 1048576 | tf_op jit(solution)/shard_map/transpose | solution.py:203
  6.6 1.1 copy.41
  7.7 13.0 %all-to-all-start = ((f32[64,8,256]{2,1,0:T(8,128)}), f32[64,8,256]{2,1,0:T(8,128)S(1)}, u32[]{:S(2)}, u32[]{:S(2)}) async-start(f32[64,8,256]{2,1,0:T(8,128)} %copy.41), calls=%async_computation | async-start | bytes 1048576 | tf_op jit(solution)/shard_map/all_to_all | solution.py:205
  20.7 0.2 fusion.49
  21.0 0.1 broadcast_in_dim.11
  21.0 0.2 copy.42
  21.2 0.1 broadcast_in_dim.12
  21.3 1.0 copy.43
  22.3 4.1 %sine_negate_fusion = (f32[512,512]{1,0:T(8,128)S(1)}, f32[512,512]{1,0:T(8,128)S(1)}) fusion(), kind=kLoop, calls=%fused_computation.16 | loop fusion | flops 3932160 | bytes 2097152 | tf_op jit(solution)/shard_map/neg | solution.py:202
  26.4 11.6 %all-to-all-done = f32[64,8,256]{2,1,0:T(8,128)S(1)} async-done(((f32[64,8,256]{2,1,0:T(8,128)}), f32[64,8,256]{2,1,0:T(8,128)S(1)}, u32[]{:S(2)}, u32[]{:S(2)}) %all-to-all-start) | async-done | bytes 524320 | tf_op jit(solution)/shard_map/all_to_all | solution.py:205
  38.0 0.0 copy-start
  38.0 1.8 fusion.1
  39.9 0.0 copy-done
  39.9 0.1 multiply_add_fusion.1
  40.0 2.6 %stack.21 = f32[1,64,8,16,16]{4,3,2,1,0:T(8,128)} reshape(f32[512,256]{1,0:T(8,128)S(1)} %get-tuple-element.5) | data formatting | bytes 1048576 | tf_op jit(solution)/shard_map/stack | solution.py:213
  42.6 3.6 %copy.46 = f32[1,64,8,16,16]{1,4,3,2,0:T(8,128)S(1)} copy(f32[1,64,8,16,16]{4,3,2,1,0:T(8,128)} %stack.21) | data formatting | bytes 1048576 | tf_op jit(solution)/shard_map/stack | solution.py:213
  46.3 2.6 %stack.22 = f32[1,64,8,16,16]{4,3,2,1,0:T(8,128)} reshape(f32[512,256]{1,0:T(8,128)S(1)} %get-tuple-element.6) | data formatting | bytes 1048576 | tf_op jit(solution)/shard_map/stack | solution.py:213
  48.9 3.6 %copy.47 = f32[1,64,8,16,16]{1,4,3,2,0:T(8,128)S(1)} copy(f32[1,64,8,16,16]{4,3,2,1,0:T(8,128)} %stack.22) | data formatting | bytes 1048576 | tf_op jit(solution)/shard_map/stack | solution.py:213
  52.5 0.2 maximum_bitcast_fusion
  52.7 0.2 copy.48
  52.9 0.0 copy-start.5
  53.0 0.0 copy-start.4
  53.0 0.0 copy-start.3
  53.0 1.8 copy.49
  54.7 6.3 %all-to-all-start.1 = ((f32[64,16,256]{2,1,0:T(8,128)}), f32[64,16,256]{2,1,0:T(8,128)S(1)}, u32[]{:S(2)}, u32[]{:S(2)}) async-start(f32[64,16,256]{2,1,0:T(8,128)} %copy.49), calls=%async_computation.1 | async-start | bytes 2097152 | tf_op jit(solution)/shard_map/all_to_all | solution.py:219
  61.1 0.3 fusion.40
  61.3 0.0 copy-done.5
  61.3 0.1 broadcast_compare_fusion
  61.4 0.0 copy-done.4
  61.4 0.1 fusion.50
  61.5 0.0 copy-done.3
  61.5 0.1 add_select_fusion.6
  61.6 0.3 fusion.43
  61.9 1.9 fusion.21
  63.8 2.0 multiply_subtract_fusion
  65.8 23.8 %all-to-all-done.1 = f32[64,16,256]{2,1,0:T(8,128)S(1)} async-done(((f32[64,16,256]{2,1,0:T(8,128)}), f32[64,16,256]{2,1,0:T(8,128)S(1)}, u32[]{:S(2)}, u32[]{:S(2)}) %all-to-all-start.1) | async-done | bytes 1048608 | tf_op jit(solution)/shard_map/all_to_all | solution.py:219
  89.6 1.3 copy.50
  90.9 0.0 copy-start.1
  90.9 3.9 %fusion.53 = f32[512,2,8,16]{0,3,2,1:T(8,128)S(1)} fusion(f32[512,1024,1,1]{0,1,3,2:T(8,128)} %bitcast.53, f32[2,8,16,1024]{3,2,1,0:T(8,128)} %bitcast.56), kind=kOutput, calls=%fused_computation.95 | convolution fusion | flops 1610612736 | bytes 3670016 | tf_op jit(solution)/shard_map/dot_general | solution.py:230
  94.8 0.0 copy-done.1
  94.8 2.0 fusion.54
  96.9 0.1 fusion.19
  97.0 0.0 copy-start.2
  97.1 2.0 copy.53
  99.0 2.9 %reshape.333 = bf16[64,2,1024]{2,1,0:T(2,128)(2,1)} reshape(bf16[512,2,8,16]{3,2,1,0:T(8,128)(2,1)S(1)} %bitcast.45) | data formatting | bytes 524288
  102.0 6.2 %all-to-all-start.2 = ((bf16[64,2,1024]{2,1,0:T(2,128)(2,1)}), bf16[64,2,1024]{2,1,0:T(2,128)(2,1)S(1)}, u32[]{:S(2)}, u32[]{:S(2)}) async-start(bf16[64,2,1024]{2,1,0:T(2,128)(2,1)} %reshape.333), calls=%async_computation.2 | async-start | bytes 524288 | tf_op jit(solution)/shard_map/all_to_all | solution.py:236
  108.2 0.0 copy-done.2
  108.2 0.8 maximum_bitcast_fusion.1.ph_ref
  109.0 9.9 %fusion.tm_ref = bf16[8,2,256,512]{3,2,1,0:T(8,128)(2,1)} fusion(bf16[256,2,8,512]{3,2,1,0:T(8,128)(2,1)} %param.7, pred[256,8]{0,1:T(8,128)(4,1)S(1)} %broadcast_compare_fusion), kind=kLoop, calls=%fused_computation.1 | loop fusion | flops 2097152 | bytes 8390656 | tf_op jit(solution)/shard_map/transpose | solution.py:76
  118.9 1.3 all-to-all-done.2
  120.2 1.4 reshape.334
  121.6 1.9 copy.68
  123.5 2.6 %copy.56.x_ref = bf16[16,2,8,512]{3,2,1,0:T(8,128)(2,1)} copy(bf16[16,2,8,512]{0,3,2,1:T(8,128)(2,1)} %bitcast.48) | data formatting | bytes 524288 | tf_op jit(solution)/shard_map/all_to_all | solution.py:236
  126.1 17.5 %shard_map.55 = bf16[4,16,2,8,512]{4,3,2,1,0:T(8,128)(2,1)} custom-call(bf16[16,2,8,512]{3,2,1,0:T(8,128)(2,1)} %copy.56.x_ref), custom_call_target="tpu_custom_call" | custom-call | tf_op jit(solution)/shard_map/pallas_call | solution.py:182
  143.6 2.8 %copy.57 = bf16[4,8,2,2,8,512]{5,1,0,2,3,4:T(8,128)(2,1)} copy(bf16[4,8,2,2,8,512]{5,4,3,2,1,0:T(8,128)(2,1)} %bitcast.50) | data formatting | bytes 2097152 | tf_op jit(solution)/shard_map/reshape;reshape | solution.py:245
  146.4 18.7 %shard_map.56.x_ref = f32[64,32,256]{2,1,0:T(8,128)} custom-call(f32[8,2,16,512]{3,2,1,0:T(8,128)} %maximum_bitcast_fusion.1.ph_ref, bf16[8,2,64,512]{3,2,1,0:T(8,128)(2,1)} %bitcast.58, bf16[8,2,256,512]{3,2,1,0:T(8,128)(2,1)} %fusion.tm_ref), custom_call_target="tpu_custom_call" | custom-call | flops 8589934592 | bytes 7864320 | tf_op jit(solution)/shard_map/pallas_call | solution.py:80
  165.1 6.3 %shard_map.57.x_ref = f32[32,32,256]{2,1,0:T(8,128)} custom-call(f32[64,32,256]{2,1,0:T(8,128)} %shard_map.56.x_ref), custom_call_target="tpu_custom_call" | custom-call | tf_op jit(solution)/shard_map/pallas_call | solution.py:139
  171.4 33.1 %shard_map.58 = f32[1,32,256]{2,1,0:T(8,128)} custom-call(f32[32,32,256]{2,1,0:T(8,128)} %shard_map.57.x_ref), custom_call_target="tpu_custom_call" | custom-call | tf_op jit(solution)/shard_map/pallas_call | solution.py:139
  204.5 1.4 copy.70
  (5 shorter events, 0.1 us)
Async XLA Ops:
  7.7 30.3 %all-to-all-start = ((f32[64,8,256]{2,1,0:T(8,128)}), f32[64,8,256]{2,1,0:T(8,128)S(1)}, u32[]{:S(2)}, u32[]{:S(2)}) async-start(f32[64,8,256]{2,1,0:T(8,128)} %copy.41), calls=%async_computation | async-start | bytes 1048576 | tf_op jit(solution)/shard_map/all_to_all | solution.py:205
  38.0 1.8 copy-start
  52.9 8.4 %copy-start.5 = (s32[256]{0:T(256)S(1)}, s32[256]{0:T(256)}, u32[]{:S(2)}) copy-start(s32[256]{0:T(256)} %param.8) | copy-start | bytes 3076
  53.0 8.5 %copy-start.4 = (s32[16]{0:T(128)S(1)}, s32[16]{0:T(128)}, u32[]{:S(2)}) copy-start(s32[16]{0:T(128)} %param.9) | copy-start | bytes 196
  53.0 8.5 %copy-start.3 = (f32[512,8]{0,1:T(8,128)S(1)}, f32[512,8]{0,1:T(8,128)}, u32[]{:S(2)}) copy-start(f32[512,8]{0,1:T(8,128)} %param.6) | copy-start | bytes 49156
  54.7 34.8 %all-to-all-start.1 = ((f32[64,16,256]{2,1,0:T(8,128)}), f32[64,16,256]{2,1,0:T(8,128)S(1)}, u32[]{:S(2)}, u32[]{:S(2)}) async-start(f32[64,16,256]{2,1,0:T(8,128)} %copy.49), calls=%async_computation.1 | async-start | bytes 2097152 | tf_op jit(solution)/shard_map/all_to_all | solution.py:219
  90.9 3.9 %copy-start.1 = (f32[256,1024]{1,0:T(8,128)S(1)}, f32[256,1024]{1,0:T(8,128)}, u32[]{:S(2)}) copy-start(f32[256,1024]{1,0:T(8,128)} %copy.50) | copy-start | bytes 3145732
  97.0 11.1 %copy-start.2 = (f32[1,16,8,512]{3,1,0,2:T(8,128)S(1)}, f32[1,16,8,512]{3,1,0,2:T(8,128)}, u32[]{:S(2)}) copy-start(f32[1,16,8,512]{3,1,0,2:T(8,128)} %get-tuple-element.12) | copy-start | bytes 786436
  102.0 18.2 %all-to-all-start.2 = ((bf16[64,2,1024]{2,1,0:T(2,128)(2,1)}), bf16[64,2,1024]{2,1,0:T(2,128)(2,1)S(1)}, u32[]{:S(2)}, u32[]{:S(2)}) async-start(bf16[64,2,1024]{2,1,0:T(2,128)(2,1)} %reshape.333), calls=%async_computation.2 | async-start | bytes 524288 | tf_op jit(solution)/shard_map/all_to_all | solution.py:236

commit v15 on v9

--- a/solution.py
+++ b/solution.py
@@ -137,6 +137,65 @@
             vmem((size,) + out_shape, parts.dtype),
             pltpu.SemaphoreType.DMA((size,)),
             pltpu.SemaphoreType.DMA((size,)),
+        ],
+        compiler_params=pltpu.CompilerParams(collective_id=collective_id, has_side_effects=True),
+    )(parts)
+
+
+def ring4_kernel(axis, x_ref, o_ref, near_ref, far_ref, relay_ref, send_sem, recv_sem):
+    me = lax.axis_index(axis)
+    piece = o_ref.shape[0]
+    half = piece // 2
+    mesh_ids = pl.DeviceIdType.MESH
+    ahead, across, behind = (lax.rem(me + k, 4) for k in (1, 2, 3))
+    barrier = pltpu.get_barrier_semaphore()
+    for peer in (ahead, across, behind):
+        pl.semaphore_signal(barrier, inc=1, device_id={axis: peer}, device_id_type=mesh_ids)
+    pl.semaphore_wait(barrier, 3)
+
+    def send(src, dst, slot, peer):
+        return pltpu.make_async_remote_copy(
+            src_ref=src, dst_ref=dst, send_sem=send_sem.at[slot], recv_sem=recv_sem.at[slot],
+            device_id={axis: peer}, device_id_type=mesh_ids,
+        )
+
+    far_start = across * piece
+    to_ahead = send(x_ref.at[pl.ds(ahead * piece, piece)], near_ref.at[0], 0, ahead)
+    to_behind = send(x_ref.at[pl.ds(behind * piece, piece)], near_ref.at[1], 1, behind)
+    direct = send(x_ref.at[pl.ds(far_start, half)], far_ref.at[0], 2, across)
+    relay_out = send(x_ref.at[pl.ds(far_start + half, piece - half)], relay_ref, 3, behind)
+    for copy in (to_ahead, to_behind, direct, relay_out):
+        copy.start()
+    relay_out.wait_recv()
+    forward = send(relay_ref, far_ref.at[1], 4, behind)
+    forward.start()
+    to_ahead.wait()
+    to_behind.wait()
+    direct.wait()
+    relay_out.wait_send()
+    forward.wait()
+    own = x_ref[pl.ds(me * piece, piece)]
+    near = near_ref[0] + near_ref[1]
+    o_ref[0:half] = own[0:half] + near[0:half] + far_ref[0]
+    o_ref[half:] = own[half:] + near[half:] + far_ref[1]
+
+
+def ring4_sum(parts, axis, collective_id):
+    piece = parts.shape[0] // 4
+    out_shape = (piece,) + parts.shape[1:]
+    half_shape = (piece // 2,) + parts.shape[1:]
+    vmem = pltpu.VMEM
+    return pl.pallas_call(
+        functools.partial(ring4_kernel, axis),
+        out_shape=jax.ShapeDtypeStruct(out_shape, parts.dtype),
+        in_specs=[pl.BlockSpec(memory_space=vmem)],
+        out_specs=pl.BlockSpec(memory_space=vmem),
+        scratch_shapes=[
+            vmem((2,) + out_shape, parts.dtype),
+            vmem((2,) + half_shape, parts.dtype),
+            vmem(half_shape, parts.dtype),
+            pltpu.SemaphoreType.DMA((5,)),
+            pltpu.SemaphoreType.DMA((5,)),
         ],
         compiler_params=pltpu.CompilerParams(collective_id=collective_id, has_side_effects=True),
     )(parts)
@@ -240,8 +299,12 @@
     j_here = data.shape[0]
     first_block = freq_index * j_here
     partial_sums = intersect(data, templates, cutoffs, lags, first_block)
-    for collective_id, name in enumerate(("fc", "fx", "fz")):
-        partial_sums = scatter_sum(partial_sums, name, collective_id + 1)
+    partial_sums = scatter_sum(partial_sums, "fc", 1)
+    if lax.axis_size("fx") == 4:
+        partial_sums = ring4_sum(partial_sums, "fx", 2)
+    else:
+        partial_sums = scatter_sum(partial_sums, "fx", 2)
+    partial_sums = scatter_sum(partial_sums, "fz", 3)
     return partial_sums
 
 

time: 203 us -> 206 us (1.015)
    pallas_call x0 -> x1, Pallas kernels: none -> 19.5 us  [ring4_sum(): pl.pallas_call(functools.partial(ring4_kernel, axis), out_shape=jax.Shape...]
    pallas_call x3 -> x2, Pallas kernels: 36 us -> 17.9 us  [scatter_sum(): pl.pallas_call(functools.partial(scatter_kernel, axis, size), out_shape=j...]
where the time goes in v15:
time: 206 us; the launch traced here: 204 us
  Pallas kernels  73.5 us (36%)
  local copies, waits for them, and re-layouts  39.9 us (19%)
  waiting for transfers between devices  36.7 us (18%)
  starting transfers between devices  25.5 us (12%)
  other arithmetic  20.2 us (10%)
  matrix products  7.78 us (4%)
    all_to_all x1, waiting for transfers between devices, spectrum_blocks(): lax.all_to_all(twisted, FREQ, 0, 0, tiled=True)  23.8 us
    pallas_call x1, Pallas kernels, ring4_sum(): pl.pallas_call(functools.partial(ring4_kernel, axis), out_shape=jax.Shape...  19.5 us
    pallas_call x1, Pallas kernels, intersect(): pl.pallas_call(intersect_kernel, out_shape=jax.ShapeDtypeStruct((seg_coun...  18.7 us
    pallas_call x2, Pallas kernels, scatter_sum(): pl.pallas_call(functools.partial(scatter_kernel, axis, size), out_shape=j...  17.9 us
    pallas_call x1, Pallas kernels, gather_all(): pl.pallas_call(functools.partial(gather_kernel, axis, size), out_shape=ja...  17.5 us
    all_to_all x1, starting transfers between devices, spectrum_blocks(): lax.all_to_all(sent, FREQ, 0, 0, tiled=True)  13 us
    another operation x4, local copies, waits for them, and re-layouts, spectrum_blocks(): jnp.stack([real_part * twist_cos + imag_part * twist_sin, imag_part * twi...  12.5 us
    all_to_all x1, waiting for transfers between devices, spectrum_blocks(): lax.all_to_all(sent, FREQ, 0, 0, tiled=True)  11.6 us
  transfers between devices with their start and end apart: 3, of which 3 were waited for; matrix products, arithmetic and copies ran while one was open for 10% of the time, Pallas kernels for 0%

profile of v15, /device:TPU:1, one launch (start us, length us, event | category | flops | bytes accessed | tf_op | source)
XLA Modules:
  0.0 203.9 jit_solution(330581956490706783)
XLA Ops:
  0.0 3.7 %reshape.323 = f32[16,8,64,16]{3,2,1,0:T(8,128)} reshape(f32[16,8192]{1,0:T(8,128)} %param.5) | data formatting | bytes 1048576 | tf_op jit(solution)/shard_map/reshape | solution.py:254
  3.7 2.9 %copy.40 = f32[64,8,16,16]{0,3,2,1:T(8,128)S(1)} copy(f32[64,8,16,16]{2,0,1,3:T(8,128)} %bitcast.44) | data formatting | bytes 1048576 | tf_op jit(solution)/shard_map/transpose | solution.py:254
  6.6 1.1 copy.41
  7.7 13.0 %all-to-all-start = ((f32[64,8,256]{2,1,0:T(8,128)}), f32[64,8,256]{2,1,0:T(8,128)S(1)}, u32[]{:S(2)}, u32[]{:S(2)}) async-start(f32[64,8,256]{2,1,0:T(8,128)} %copy.41), calls=%async_computation | async-start | bytes 1048576 | tf_op jit(solution)/shard_map/all_to_all | solution.py:256
  20.7 0.2 fusion.49
  21.0 0.1 broadcast_in_dim.11
  21.0 0.2 copy.42
  21.2 0.1 broadcast_in_dim.12
  21.3 1.0 copy.43
  22.3 4.1 %sine_negate_fusion = (f32[512,512]{1,0:T(8,128)S(1)}, f32[512,512]{1,0:T(8,128)S(1)}) fusion(), kind=kLoop, calls=%fused_computation.16 | loop fusion | flops 3932160 | bytes 2097152 | tf_op jit(solution)/shard_map/neg | solution.py:253
  26.4 11.6 %all-to-all-done = f32[64,8,256]{2,1,0:T(8,128)S(1)} async-done(((f32[64,8,256]{2,1,0:T(8,128)}), f32[64,8,256]{2,1,0:T(8,128)S(1)}, u32[]{:S(2)}, u32[]{:S(2)}) %all-to-all-start) | async-done | bytes 524320 | tf_op jit(solution)/shard_map/all_to_all | solution.py:256
  38.0 0.0 copy-start
  38.0 1.8 fusion.1
  39.9 0.0 copy-done
  39.9 0.1 multiply_add_fusion.1
  40.0 2.6 %stack.21 = f32[1,64,8,16,16]{4,3,2,1,0:T(8,128)} reshape(f32[512,256]{1,0:T(8,128)S(1)} %get-tuple-element.5) | data formatting | bytes 1048576 | tf_op jit(solution)/shard_map/stack | solution.py:264
  42.6 3.6 %copy.46 = f32[1,64,8,16,16]{1,4,3,2,0:T(8,128)S(1)} copy(f32[1,64,8,16,16]{4,3,2,1,0:T(8,128)} %stack.21) | data formatting | bytes 1048576 | tf_op jit(solution)/shard_map/stack | solution.py:264
  46.3 2.6 %stack.22 = f32[1,64,8,16,16]{4,3,2,1,0:T(8,128)} reshape(f32[512,256]{1,0:T(8,128)S(1)} %get-tuple-element.6) | data formatting | bytes 1048576 | tf_op jit(solution)/shard_map/stack | solution.py:264
  48.9 3.6 %copy.47 = f32[1,64,8,16,16]{1,4,3,2,0:T(8,128)S(1)} copy(f32[1,64,8,16,16]{4,3,2,1,0:T(8,128)} %stack.22) | data formatting | bytes 1048576 | tf_op jit(solution)/shard_map/stack | solution.py:264
  52.5 0.2 maximum_bitcast_fusion
  52.7 0.2 copy.48
  52.9 0.0 copy-start.5
  53.0 0.0 copy-start.4
  53.0 0.0 copy-start.3
  53.0 1.8 copy.49
  54.7 6.3 %all-to-all-start.1 = ((f32[64,16,256]{2,1,0:T(8,128)}), f32[64,16,256]{2,1,0:T(8,128)S(1)}, u32[]{:S(2)}, u32[]{:S(2)}) async-start(f32[64,16,256]{2,1,0:T(8,128)} %copy.49), calls=%async_computation.1 | async-start | bytes 2097152 | tf_op jit(solution)/shard_map/all_to_all | solution.py:270
  61.1 0.3 fusion.40
  61.3 0.0 copy-done.5
  61.3 0.1 broadcast_compare_fusion
  61.4 0.0 copy-done.4
  61.4 0.1 fusion.50
  61.5 0.0 copy-done.3
  61.5 0.1 add_select_fusion.6
  61.6 0.3 fusion.43
  61.9 1.9 fusion.21
  63.8 2.0 multiply_subtract_fusion
  65.8 23.8 %all-to-all-done.1 = f32[64,16,256]{2,1,0:T(8,128)S(1)} async-done(((f32[64,16,256]{2,1,0:T(8,128)}), f32[64,16,256]{2,1,0:T(8,128)S(1)}, u32[]{:S(2)}, u32[]{:S(2)}) %all-to-all-start.1) | async-done | bytes 1048608 | tf_op jit(solution)/shard_map/all_to_all | solution.py:270
  89.6 1.3 copy.50
  90.9 0.0 copy-start.1
  90.9 3.9 %fusion.53 = f32[512,2,8,16]{0,3,2,1:T(8,128)S(1)} fusion(f32[512,1024,1,1]{0,1,3,2:T(8,128)} %bitcast.53, f32[2,8,16,1024]{3,2,1,0:T(8,128)} %bitcast.56), kind=kOutput, calls=%fused_computation.95 | convolution fusion | flops 1610612736 | bytes 3670016 | tf_op jit(solution)/shard_map/dot_general | solution.py:281
  94.8 0.0 copy-done.1
  94.8 2.0 %fusion.54 = f32[512,2,8,16]{0,3,2,1:T(8,128)S(1)} fusion(f32[512,1024,1,1]{0,1,3,2:T(8,128)S(1)} %bitcast.52, f32[2,8,16,1024]{3,2,1,0:T(8,128)S(1)} %bitcast.57), kind=kOutput, calls=%fused_computation.96 | convolution fusion | flops 1610612736 | bytes 3670016 | tf_op jit(solution)/shard_map/dot_general | solution.py:282
  96.9 0.1 fusion.19
  97.0 0.0 copy-start.2
  97.1 2.0 copy.53
  99.0 2.9 %reshape.333 = bf16[64,2,1024]{2,1,0:T(2,128)(2,1)} reshape(bf16[512,2,8,16]{3,2,1,0:T(8,128)(2,1)S(1)} %bitcast.45) | data formatting | bytes 524288
  102.0 6.2 %all-to-all-start.2 = ((bf16[64,2,1024]{2,1,0:T(2,128)(2,1)}), bf16[64,2,1024]{2,1,0:T(2,128)(2,1)S(1)}, u32[]{:S(2)}, u32[]{:S(2)}) async-start(bf16[64,2,1024]{2,1,0:T(2,128)(2,1)} %reshape.333), calls=%async_computation.2 | async-start | bytes 524288 | tf_op jit(solution)/shard_map/all_to_all | solution.py:287
  108.2 0.0 copy-done.2
  108.2 0.8 maximum_bitcast_fusion.1.ph_ref
  109.0 9.9 %fusion.tm_ref = bf16[8,2,256,512]{3,2,1,0:T(8,128)(2,1)} fusion(bf16[256,2,8,512]{3,2,1,0:T(8,128)(2,1)} %param.7, pred[256,8]{0,1:T(8,128)(4,1)S(1)} %broadcast_compare_fusion), kind=kLoop, calls=%fused_computation.1 | loop fusion | flops 2097152 | bytes 8390656 | tf_op jit(solution)/shard_map/transpose | solution.py:76
  118.9 1.3 all-to-all-done.2
  120.2 1.4 reshape.334
  121.6 1.9 copy.68
  123.5 2.6 %copy.56.x_ref = bf16[16,2,8,512]{3,2,1,0:T(8,128)(2,1)} copy(bf16[16,2,8,512]{0,3,2,1:T(8,128)(2,1)} %bitcast.48) | data formatting | bytes 524288 | tf_op jit(solution)/shard_map/all_to_all | solution.py:287
  126.1 17.5 %shard_map.55 = bf16[4,16,2,8,512]{4,3,2,1,0:T(8,128)(2,1)} custom-call(bf16[16,2,8,512]{3,2,1,0:T(8,128)(2,1)} %copy.56.x_ref), custom_call_target="tpu_custom_call" | custom-call | tf_op jit(solution)/shard_map/pallas_call | solution.py:233
  143.6 2.8 %copy.57 = bf16[4,8,2,2,8,512]{5,1,0,2,3,4:T(8,128)(2,1)} copy(bf16[4,8,2,2,8,512]{5,4,3,2,1,0:T(8,128)(2,1)} %bitcast.50) | data formatting | bytes 2097152 | tf_op jit(solution)/shard_map/reshape;reshape | solution.py:296
  146.4 18.7 %shard_map.56.x_ref = f32[64,32,256]{2,1,0:T(8,128)} custom-call(f32[8,2,16,512]{3,2,1,0:T(8,128)} %maximum_bitcast_fusion.1.ph_ref, bf16[8,2,64,512]{3,2,1,0:T(8,128)(2,1)} %bitcast.58, bf16[8,2,256,512]{3,2,1,0:T(8,128)(2,1)} %fusion.tm_ref), custom_call_target="tpu_custom_call" | custom-call | flops 8589934592 | bytes 7864320 | tf_op jit(solution)/shard_map/pallas_call | solution.py:80
  165.1 6.3 %shard_map.57.x_ref = f32[32,32,256]{2,1,0:T(8,128)} custom-call(f32[64,32,256]{2,1,0:T(8,128)} %shard_map.56.x_ref), custom_call_target="tpu_custom_call" | custom-call | tf_op jit(solution)/shard_map/pallas_call | solution.py:131
  171.4 19.5 %shard_map.58.x_ref = f32[8,32,256]{2,1,0:T(8,128)} custom-call(f32[32,32,256]{2,1,0:T(8,128)} %shard_map.57.x_ref), custom_call_target="tpu_custom_call" | custom-call | tf_op jit(solution)/shard_map/pallas_call | solution.py:188
  190.9 11.6 %shard_map.59 = f32[1,32,256]{2,1,0:T(8,128)} custom-call(f32[8,32,256]{2,1,0:T(8,128)} %shard_map.58.x_ref), custom_call_target="tpu_custom_call" | custom-call | tf_op jit(solution)/shard_map/pallas_call | solution.py:131
  202.5 1.4 copy.70
  (5 shorter events, 0.1 us)
Async XLA Ops:
  7.7 30.3 %all-to-all-start = ((f32[64,8,256]{2,1,0:T(8,128)}), f32[64,8,256]{2,1,0:T(8,128)S(1)}, u32[]{:S(2)}, u32[]{:S(2)}) async-start(f32[64,8,256]{2,1,0:T(8,128)} %copy.41), calls=%async_computation | async-start | bytes 1048576 | tf_op jit(solution)/shard_map/all_to_all | solution.py:256
  38.0 1.8 copy-start
  52.9 8.4 %copy-start.5 = (s32[256]{0:T(256)S(1)}, s32[256]{0:T(256)}, u32[]{:S(2)}) copy-start(s32[256]{0:T(256)} %param.8) | copy-start | bytes 3076
  53.0 8.5 %copy-start.4 = (s32[16]{0:T(128)S(1)}, s32[16]{0:T(128)}, u32[]{:S(2)}) copy-start(s32[16]{0:T(128)} %param.9) | copy-start | bytes 196
  53.0 8.5 %copy-start.3 = (f32[512,8]{0,1:T(8,128)S(1)}, f32[512,8]{0,1:T(8,128)}, u32[]{:S(2)}) copy-start(f32[512,8]{0,1:T(8,128)} %param.6) | copy-start | bytes 49156
  54.7 34.8 %all-to-all-start.1 = ((f32[64,16,256]{2,1,0:T(8,128)}), f32[64,16,256]{2,1,0:T(8,128)S(1)}, u32[]{:S(2)}, u32[]{:S(2)}) async-start(f32[64,16,256]{2,1,0:T(8,128)} %copy.49), calls=%async_computation.1 | async-start | bytes 2097152 | tf_op jit(solution)/shard_map/all_to_all | solution.py:270
  90.9 3.9 %copy-start.1 = (f32[256,1024]{1,0:T(8,128)S(1)}, f32[256,1024]{1,0:T(8,128)}, u32[]{:S(2)}) copy-start(f32[256,1024]{1,0:T(8,128)} %copy.50) | copy-start | bytes 3145732
  97.0 11.1 %copy-start.2 = (f32[1,16,8,512]{3,1,0,2:T(8,128)S(1)}, f32[1,16,8,512]{3,1,0,2:T(8,128)}, u32[]{:S(2)}) copy-start(f32[1,16,8,512]{3,1,0,2:T(8,128)} %get-tuple-element.12) | copy-start | bytes 786436
  102.0 18.2 %all-to-all-start.2 = ((bf16[64,2,1024]{2,1,0:T(2,128)(2,1)}), bf16[64,2,1024]{2,1,0:T(2,128)(2,1)S(1)}, u32[]{:S(2)}, u32[]{:S(2)}) async-start(bf16[64,2,1024]{2,1,0:T(2,128)(2,1)} %reshape.333), calls=%async_computation.2 | async-start | bytes 524288 | tf_op jit(solution)/shard_map/all_to_all | solution.py:287

commit v16 on v9

--- a/solution.py
+++ b/solution.py
@@ -103,7 +103,7 @@
         pl.semaphore_signal(barrier, inc=1, device_id={axis: peer}, device_id_type=mesh_ids)
     pl.semaphore_wait(barrier, size - 1)
     copies = []
-    for k in range(1, size):
+    for k in sorted(range(1, size), key=lambda k: -min(k, size - k)):
         peer = lax.rem(me + k, size)
         copy = pltpu.make_async_remote_copy(
             src_ref=x_ref.at[pl.ds(peer * piece, piece)],

time: 203 us -> 204 us (level)
  no operation moved by 1% of the time
where the time goes in v16:
time: 204 us
  Pallas kernels  73.2 us (36%)
  local copies, waits for them, and re-layouts  39.9 us (20%)
  waiting for transfers between devices  36.7 us (18%)
  starting transfers between devices  25.5 us (12%)
  other arithmetic  20.2 us (10%)
  matrix products  7.78 us (4%)
    pallas_call x3, Pallas kernels, scatter_sum(): pl.pallas_call(functools.partial(scatter_kernel, axis, size), out_shape=j...  37.1 us
    all_to_all x1, waiting for transfers between devices, spectrum_blocks(): lax.all_to_all(twisted, FREQ, 0, 0, tiled=True)  23.8 us
    pallas_call x1, Pallas kernels, intersect(): pl.pallas_call(intersect_kernel, out_shape=jax.ShapeDtypeStruct((seg_coun...  18.7 us
    pallas_call x1, Pallas kernels, gather_all(): pl.pallas_call(functools.partial(gather_kernel, axis, size), out_shape=ja...  17.5 us
    all_to_all x1, starting transfers between devices, spectrum_blocks(): lax.all_to_all(sent, FREQ, 0, 0, tiled=True)  13 us
    another operation x4, local copies, waits for them, and re-layouts, spectrum_blocks(): jnp.stack([real_part * twist_cos + imag_part * twist_sin, imag_part * twi...  12.5 us
    all_to_all x1, waiting for transfers between devices, spectrum_blocks(): lax.all_to_all(sent, FREQ, 0, 0, tiled=True)  11.6 us
    transpose x1, other arithmetic, intersect(): jnp.where(keep, templates, jnp.zeros_like(templates)).transpose(2, 1, 0, 3)  9.88 us
  transfers between devices with their start and end apart: 3, of which 3 were waited for; matrix products, arithmetic and copies ran while one was open for 10% of the time, Pallas kernels for 0%

profile of v16, /device:TPU:1, one launch (start us, length us, event | category | flops | bytes accessed | tf_op | source)
XLA Modules:
  0.0 203.6 jit_solution(23316594892934654)
XLA Ops:
  0.0 3.7 %reshape.323 = f32[16,8,64,16]{3,2,1,0:T(8,128)} reshape(f32[16,8192]{1,0:T(8,128)} %param.5) | data formatting | bytes 1048576 | tf_op jit(solution)/shard_map/reshape | solution.py:195
  3.7 2.9 %copy.40 = f32[64,8,16,16]{0,3,2,1:T(8,128)S(1)} copy(f32[64,8,16,16]{2,0,1,3:T(8,128)} %bitcast.44) | data formatting | bytes 1048576 | tf_op jit(solution)/shard_map/transpose | solution.py:195
  6.6 1.1 copy.41
  7.7 13.0 %all-to-all-start = ((f32[64,8,256]{2,1,0:T(8,128)}), f32[64,8,256]{2,1,0:T(8,128)S(1)}, u32[]{:S(2)}, u32[]{:S(2)}) async-start(f32[64,8,256]{2,1,0:T(8,128)} %copy.41), calls=%async_computation | async-start | bytes 1048576 | tf_op jit(solution)/shard_map/all_to_all | solution.py:197
  20.7 0.2 fusion.49
  21.0 0.1 broadcast_in_dim.11
  21.0 0.2 copy.42
  21.2 0.1 broadcast_in_dim.12
  21.3 1.0 copy.43
  22.3 4.1 %sine_negate_fusion = (f32[512,512]{1,0:T(8,128)S(1)}, f32[512,512]{1,0:T(8,128)S(1)}) fusion(), kind=kLoop, calls=%fused_computation.16 | loop fusion | flops 3932160 | bytes 2097152 | tf_op jit(solution)/shard_map/neg | solution.py:194
  26.4 11.6 %all-to-all-done = f32[64,8,256]{2,1,0:T(8,128)S(1)} async-done(((f32[64,8,256]{2,1,0:T(8,128)}), f32[64,8,256]{2,1,0:T(8,128)S(1)}, u32[]{:S(2)}, u32[]{:S(2)}) %all-to-all-start) | async-done | bytes 524320 | tf_op jit(solution)/shard_map/all_to_all | solution.py:197
  38.0 0.0 copy-start
  38.0 1.8 fusion.1
  39.9 0.0 copy-done
  39.9 0.1 multiply_add_fusion.1
  40.0 2.6 %stack.21 = f32[1,64,8,16,16]{4,3,2,1,0:T(8,128)} reshape(f32[512,256]{1,0:T(8,128)S(1)} %get-tuple-element.5) | data formatting | bytes 1048576 | tf_op jit(solution)/shard_map/stack | solution.py:205
  42.6 3.6 %copy.46 = f32[1,64,8,16,16]{1,4,3,2,0:T(8,128)S(1)} copy(f32[1,64,8,16,16]{4,3,2,1,0:T(8,128)} %stack.21) | data formatting | bytes 1048576 | tf_op jit(solution)/shard_map/stack | solution.py:205
  46.3 2.6 %stack.22 = f32[1,64,8,16,16]{4,3,2,1,0:T(8,128)} reshape(f32[512,256]{1,0:T(8,128)S(1)} %get-tuple-element.6) | data formatting | bytes 1048576 | tf_op jit(solution)/shard_map/stack | solution.py:205
  48.9 3.6 %copy.47 = f32[1,64,8,16,16]{1,4,3,2,0:T(8,128)S(1)} copy(f32[1,64,8,16,16]{4,3,2,1,0:T(8,128)} %stack.22) | data formatting | bytes 1048576 | tf_op jit(solution)/shard_map/stack | solution.py:205
  52.5 0.2 maximum_bitcast_fusion
  52.7 0.2 copy.48
  52.9 0.0 copy-start.5
  53.0 0.0 copy-start.4
  53.0 0.0 copy-start.3
  53.0 1.8 copy.49
  54.7 6.3 %all-to-all-start.1 = ((f32[64,16,256]{2,1,0:T(8,128)}), f32[64,16,256]{2,1,0:T(8,128)S(1)}, u32[]{:S(2)}, u32[]{:S(2)}) async-start(f32[64,16,256]{2,1,0:T(8,128)} %copy.49), calls=%async_computation.1 | async-start | bytes 2097152 | tf_op jit(solution)/shard_map/all_to_all | solution.py:211
  61.1 0.3 fusion.40
  61.3 0.0 copy-done.5
  61.3 0.1 broadcast_compare_fusion
  61.4 0.0 copy-done.4
  61.4 0.1 fusion.50
  61.5 0.0 copy-done.3
  61.5 0.1 add_select_fusion.6
  61.6 0.3 fusion.43
  61.9 1.9 fusion.21
  63.8 2.0 multiply_subtract_fusion
  65.8 23.8 %all-to-all-done.1 = f32[64,16,256]{2,1,0:T(8,128)S(1)} async-done(((f32[64,16,256]{2,1,0:T(8,128)}), f32[64,16,256]{2,1,0:T(8,128)S(1)}, u32[]{:S(2)}, u32[]{:S(2)}) %all-to-all-start.1) | async-done | bytes 1048608 | tf_op jit(solution)/shard_map/all_to_all | solution.py:211
  89.6 1.3 copy.50
  90.9 0.0 copy-start.1
  90.9 3.9 %fusion.53 = f32[512,2,8,16]{0,3,2,1:T(8,128)S(1)} fusion(f32[512,1024,1,1]{0,1,3,2:T(8,128)} %bitcast.53, f32[2,8,16,1024]{3,2,1,0:T(8,128)} %bitcast.56), kind=kOutput, calls=%fused_computation.95 | convolution fusion | flops 1610612736 | bytes 3670016 | tf_op jit(solution)/shard_map/dot_general | solution.py:222
  94.8 0.0 copy-done.1
  94.8 2.0 %fusion.54 = f32[512,2,8,16]{0,3,2,1:T(8,128)S(1)} fusion(f32[512,1024,1,1]{0,1,3,2:T(8,128)S(1)} %bitcast.52, f32[2,8,16,1024]{3,2,1,0:T(8,128)S(1)} %bitcast.57), kind=kOutput, calls=%fused_computation.96 | convolution fusion | flops 1610612736 | bytes 3670016 | tf_op jit(solution)/shard_map/dot_general | solution.py:223
  96.9 0.1 fusion.19
  97.0 0.0 copy-start.2
  97.1 2.0 copy.53
  99.0 2.9 %reshape.333 = bf16[64,2,1024]{2,1,0:T(2,128)(2,1)} reshape(bf16[512,2,8,16]{3,2,1,0:T(8,128)(2,1)S(1)} %bitcast.45) | data formatting | bytes 524288
  102.0 6.2 %all-to-all-start.2 = ((bf16[64,2,1024]{2,1,0:T(2,128)(2,1)}), bf16[64,2,1024]{2,1,0:T(2,128)(2,1)S(1)}, u32[]{:S(2)}, u32[]{:S(2)}) async-start(bf16[64,2,1024]{2,1,0:T(2,128)(2,1)} %reshape.333), calls=%async_computation.2 | async-start | bytes 524288 | tf_op jit(solution)/shard_map/all_to_all | solution.py:228
  108.2 0.0 copy-done.2
  108.2 0.8 maximum_bitcast_fusion.1.ph_ref
  109.0 9.9 %fusion.tm_ref = bf16[8,2,256,512]{3,2,1,0:T(8,128)(2,1)} fusion(bf16[256,2,8,512]{3,2,1,0:T(8,128)(2,1)} %param.7, pred[256,8]{0,1:T(8,128)(4,1)S(1)} %broadcast_compare_fusion), kind=kLoop, calls=%fused_computation.1 | loop fusion | flops 2097152 | bytes 8390656 | tf_op jit(solution)/shard_map/transpose | solution.py:76
  118.9 1.3 all-to-all-done.2
  120.2 1.4 reshape.334
  121.6 1.9 copy.68
  123.5 2.6 %copy.56.x_ref = bf16[16,2,8,512]{3,2,1,0:T(8,128)(2,1)} copy(bf16[16,2,8,512]{0,3,2,1:T(8,128)(2,1)} %bitcast.48) | data formatting | bytes 524288 | tf_op jit(solution)/shard_map/all_to_all | solution.py:228
  126.1 17.5 %shard_map.55 = bf16[4,16,2,8,512]{4,3,2,1,0:T(8,128)(2,1)} custom-call(bf16[16,2,8,512]{3,2,1,0:T(8,128)(2,1)} %copy.56.x_ref), custom_call_target="tpu_custom_call" | custom-call | tf_op jit(solution)/shard_map/pallas_call | solution.py:174
  143.6 2.8 %copy.57 = bf16[4,8,2,2,8,512]{5,1,0,2,3,4:T(8,128)(2,1)} copy(bf16[4,8,2,2,8,512]{5,4,3,2,1,0:T(8,128)(2,1)} %bitcast.50) | data formatting | bytes 2097152 | tf_op jit(solution)/shard_map/reshape;reshape | solution.py:237
  146.4 18.7 %shard_map.56.x_ref = f32[64,32,256]{2,1,0:T(8,128)} custom-call(f32[8,2,16,512]{3,2,1,0:T(8,128)} %maximum_bitcast_fusion.1.ph_ref, bf16[8,2,64,512]{3,2,1,0:T(8,128)(2,1)} %bitcast.58, bf16[8,2,256,512]{3,2,1,0:T(8,128)(2,1)} %fusion.tm_ref), custom_call_target="tpu_custom_call" | custom-call | flops 8589934592 | bytes 7864320 | tf_op jit(solution)/shard_map/pallas_call | solution.py:80
  165.1 6.3 %shard_map.57.x_ref = f32[32,32,256]{2,1,0:T(8,128)} custom-call(f32[64,32,256]{2,1,0:T(8,128)} %shard_map.56.x_ref), custom_call_target="tpu_custom_call" | custom-call | tf_op jit(solution)/shard_map/pallas_call | solution.py:131
  171.4 17.7 %shard_map.58.x_ref = f32[8,32,256]{2,1,0:T(8,128)} custom-call(f32[32,32,256]{2,1,0:T(8,128)} %shard_map.57.x_ref), custom_call_target="tpu_custom_call" | custom-call | tf_op jit(solution)/shard_map/pallas_call | solution.py:131
  189.1 13.1 %shard_map.59 = f32[1,32,256]{2,1,0:T(8,128)} custom-call(f32[8,32,256]{2,1,0:T(8,128)} %shard_map.58.x_ref), custom_call_target="tpu_custom_call" | custom-call | tf_op jit(solution)/shard_map/pallas_call | solution.py:131
  202.2 1.4 copy.70
  (5 shorter events, 0.1 us)
Async XLA Ops:
  7.7 30.3 %all-to-all-start = ((f32[64,8,256]{2,1,0:T(8,128)}), f32[64,8,256]{2,1,0:T(8,128)S(1)}, u32[]{:S(2)}, u32[]{:S(2)}) async-start(f32[64,8,256]{2,1,0:T(8,128)} %copy.41), calls=%async_computation | async-start | bytes 1048576 | tf_op jit(solution)/shard_map/all_to_all | solution.py:197
  38.0 1.8 copy-start
  52.9 8.4 %copy-start.5 = (s32[256]{0:T(256)S(1)}, s32[256]{0:T(256)}, u32[]{:S(2)}) copy-start(s32[256]{0:T(256)} %param.8) | copy-start | bytes 3076
  53.0 8.5 %copy-start.4 = (s32[16]{0:T(128)S(1)}, s32[16]{0:T(128)}, u32[]{:S(2)}) copy-start(s32[16]{0:T(128)} %param.9) | copy-start | bytes 196
  53.0 8.5 %copy-start.3 = (f32[512,8]{0,1:T(8,128)S(1)}, f32[512,8]{0,1:T(8,128)}, u32[]{:S(2)}) copy-start(f32[512,8]{0,1:T(8,128)} %param.6) | copy-start | bytes 49156
  54.7 34.8 %all-to-all-start.1 = ((f32[64,16,256]{2,1,0:T(8,128)}), f32[64,16,256]{2,1,0:T(8,128)S(1)}, u32[]{:S(2)}, u32[]{:S(2)}) async-start(f32[64,16,256]{2,1,0:T(8,128)} %copy.49), calls=%async_computation.1 | async-start | bytes 2097152 | tf_op jit(solution)/shard_map/all_to_all | solution.py:211
  90.9 3.9 %copy-start.1 = (f32[256,1024]{1,0:T(8,128)S(1)}, f32[256,1024]{1,0:T(8,128)}, u32[]{:S(2)}) copy-start(f32[256,1024]{1,0:T(8,128)} %copy.50) | copy-start | bytes 3145732
  97.0 11.1 %copy-start.2 = (f32[1,16,8,512]{3,1,0,2:T(8,128)S(1)}, f32[1,16,8,512]{3,1,0,2:T(8,128)}, u32[]{:S(2)}) copy-start(f32[1,16,8,512]{3,1,0,2:T(8,128)} %get-tuple-element.12) | copy-start | bytes 786436
  102.0 18.2 %all-to-all-start.2 = ((bf16[64,2,1024]{2,1,0:T(2,128)(2,1)}), bf16[64,2,1024]{2,1,0:T(2,128)(2,1)S(1)}, u32[]{:S(2)}, u32[]{:S(2)}) async-start(bf16[64,2,1024]{2,1,0:T(2,128)(2,1)} %reshape.333), calls=%async_computation.2 | async-start | bytes 524288 | tf_op jit(solution)/shard_map/all_to_all | solution.py:228

commit v17 on v9

--- a/solution.py
+++ b/solution.py
@@ -49,7 +49,7 @@
         lhs_ref[pl.ds(rows + r0, chunk * lag_total), :] = imag_q.reshape(chunk * lag_total, -1).astype(jnp.bfloat16)
         return carry
 
-    lax.fori_loop(0, seg_count // chunk, build, 0)
+    lax.fori_loop(0, seg_count // chunk, build, 0, unroll=True)
     dims = (((1,), (1,)), ((), ()))
     lhs = lhs_ref[...]
     with_re = lax.dot_general(lhs, tm_ref[0, 0], dims, preferred_element_type=jnp.float32)

time: 203 us -> 198 us (0.975)
  Pallas kernels: 72.2 us -> 66.8 us
    pallas_call x1, Pallas kernels: 18.7 us -> 13.3 us  [intersect(): pl.pallas_call(intersect_kernel, out_shape=jax.ShapeDtypeStruct((seg_coun...]
  transfers between devices with their start and end apart: 3 -> 3, of which waited for: 3 -> 3; matrix products, arithmetic and copies ran while one was open for 10% -> 11% of each run, Pallas kernels for 0% -> 0%
where the time goes in v17:
time: 198 us; the launch traced here: 197 us
  Pallas kernels  66.8 us (34%)
  local copies, waits for them, and re-layouts  39.9 us (20%)
  waiting for transfers between devices  36.7 us (19%)
  starting transfers between devices  25.5 us (13%)
  other arithmetic  20.2 us (10%)
  matrix products  7.78 us (4%)
    pallas_call x3, Pallas kernels, scatter_sum(): pl.pallas_call(functools.partial(scatter_kernel, axis, size), out_shape=j...  36 us
    all_to_all x1, waiting for transfers between devices, spectrum_blocks(): lax.all_to_all(twisted, FREQ, 0, 0, tiled=True)  23.8 us
    pallas_call x1, Pallas kernels, gather_all(): pl.pallas_call(functools.partial(gather_kernel, axis, size), out_shape=ja...  17.5 us
    pallas_call x1, Pallas kernels, intersect(): pl.pallas_call(intersect_kernel, out_shape=jax.ShapeDtypeStruct((seg_coun...  13.3 us
    all_to_all x1, starting transfers between devices, spectrum_blocks(): lax.all_to_all(sent, FREQ, 0, 0, tiled=True)  13 us
    another operation x4, local copies, waits for them, and re-layouts, spectrum_blocks(): jnp.stack([real_part * twist_cos + imag_part * twist_sin, imag_part * twi...  12.5 us
    all_to_all x1, waiting for transfers between devices, spectrum_blocks(): lax.all_to_all(sent, FREQ, 0, 0, tiled=True)  11.6 us
    transpose x1, other arithmetic, intersect(): jnp.where(keep, templates, jnp.zeros_like(templates)).transpose(2, 1, 0, 3)  9.88 us
  transfers between devices with their start and end apart: 3, of which 3 were waited for; matrix products, arithmetic and copies ran while one was open for 11% of the time, Pallas kernels for 0%

profile of v17, /device:TPU:1, one launch (start us, length us, event | category | flops | bytes accessed | tf_op | source)
XLA Modules:
  0.0 197.1 jit_solution(12108060410860771654)
XLA Ops:
  0.0 3.7 %reshape.323 = f32[16,8,64,16]{3,2,1,0:T(8,128)} reshape(f32[16,8192]{1,0:T(8,128)} %param.5) | data formatting | bytes 1048576 | tf_op jit(solution)/shard_map/reshape | solution.py:195
  3.7 2.9 %copy.40 = f32[64,8,16,16]{0,3,2,1:T(8,128)S(1)} copy(f32[64,8,16,16]{2,0,1,3:T(8,128)} %bitcast.44) | data formatting | bytes 1048576 | tf_op jit(solution)/shard_map/transpose | solution.py:195
  6.6 1.1 copy.41
  7.7 13.0 %all-to-all-start = ((f32[64,8,256]{2,1,0:T(8,128)}), f32[64,8,256]{2,1,0:T(8,128)S(1)}, u32[]{:S(2)}, u32[]{:S(2)}) async-start(f32[64,8,256]{2,1,0:T(8,128)} %copy.41), calls=%async_computation | async-start | bytes 1048576 | tf_op jit(solution)/shard_map/all_to_all | solution.py:197
  20.7 0.2 fusion.49
  21.0 0.1 broadcast_in_dim.11
  21.0 0.2 copy.42
  21.2 0.1 broadcast_in_dim.12
  21.3 1.0 copy.43
  22.3 4.1 %sine_negate_fusion = (f32[512,512]{1,0:T(8,128)S(1)}, f32[512,512]{1,0:T(8,128)S(1)}) fusion(), kind=kLoop, calls=%fused_computation.16 | loop fusion | flops 3932160 | bytes 2097152 | tf_op jit(solution)/shard_map/neg | solution.py:194
  26.4 11.6 %all-to-all-done = f32[64,8,256]{2,1,0:T(8,128)S(1)} async-done(((f32[64,8,256]{2,1,0:T(8,128)}), f32[64,8,256]{2,1,0:T(8,128)S(1)}, u32[]{:S(2)}, u32[]{:S(2)}) %all-to-all-start) | async-done | bytes 524320 | tf_op jit(solution)/shard_map/all_to_all | solution.py:197
  38.0 0.0 copy-start
  38.0 1.8 fusion.1
  39.9 0.0 copy-done
  39.9 0.1 multiply_add_fusion.1
  40.0 2.6 %stack.21 = f32[1,64,8,16,16]{4,3,2,1,0:T(8,128)} reshape(f32[512,256]{1,0:T(8,128)S(1)} %get-tuple-element.5) | data formatting | bytes 1048576 | tf_op jit(solution)/shard_map/stack | solution.py:205
  42.6 3.6 %copy.46 = f32[1,64,8,16,16]{1,4,3,2,0:T(8,128)S(1)} copy(f32[1,64,8,16,16]{4,3,2,1,0:T(8,128)} %stack.21) | data formatting | bytes 1048576 | tf_op jit(solution)/shard_map/stack | solution.py:205
  46.3 2.6 %stack.22 = f32[1,64,8,16,16]{4,3,2,1,0:T(8,128)} reshape(f32[512,256]{1,0:T(8,128)S(1)} %get-tuple-element.6) | data formatting | bytes 1048576 | tf_op jit(solution)/shard_map/stack | solution.py:205
  48.9 3.6 %copy.47 = f32[1,64,8,16,16]{1,4,3,2,0:T(8,128)S(1)} copy(f32[1,64,8,16,16]{4,3,2,1,0:T(8,128)} %stack.22) | data formatting | bytes 1048576 | tf_op jit(solution)/shard_map/stack | solution.py:205
  52.5 0.2 maximum_bitcast_fusion
  52.7 0.2 copy.48
  52.9 0.0 copy-start.5
  53.0 0.0 copy-start.4
  53.0 0.0 copy-start.3
  53.0 1.8 copy.49
  54.7 6.3 %all-to-all-start.1 = ((f32[64,16,256]{2,1,0:T(8,128)}), f32[64,16,256]{2,1,0:T(8,128)S(1)}, u32[]{:S(2)}, u32[]{:S(2)}) async-start(f32[64,16,256]{2,1,0:T(8,128)} %copy.49), calls=%async_computation.1 | async-start | bytes 2097152 | tf_op jit(solution)/shard_map/all_to_all | solution.py:211
  61.1 0.3 fusion.40
  61.3 0.0 copy-done.5
  61.3 0.1 broadcast_compare_fusion
  61.4 0.0 copy-done.4
  61.4 0.1 fusion.50
  61.5 0.0 copy-done.3
  61.5 0.1 add_select_fusion.6
  61.6 0.3 fusion.43
  61.9 1.9 fusion.21
  63.8 2.0 multiply_subtract_fusion
  65.8 23.8 %all-to-all-done.1 = f32[64,16,256]{2,1,0:T(8,128)S(1)} async-done(((f32[64,16,256]{2,1,0:T(8,128)}), f32[64,16,256]{2,1,0:T(8,128)S(1)}, u32[]{:S(2)}, u32[]{:S(2)}) %all-to-all-start.1) | async-done | bytes 1048608 | tf_op jit(solution)/shard_map/all_to_all | solution.py:211
  89.6 1.3 copy.50
  90.9 0.0 copy-start.1
  90.9 3.9 %fusion.53 = f32[512,2,8,16]{0,3,2,1:T(8,128)S(1)} fusion(f32[512,1024,1,1]{0,1,3,2:T(8,128)} %bitcast.53, f32[2,8,16,1024]{3,2,1,0:T(8,128)} %bitcast.56), kind=kOutput, calls=%fused_computation.95 | convolution fusion | flops 1610612736 | bytes 3670016 | tf_op jit(solution)/shard_map/dot_general | solution.py:222
  94.8 0.0 copy-done.1
  94.8 2.0 %fusion.54 = f32[512,2,8,16]{0,3,2,1:T(8,128)S(1)} fusion(f32[512,1024,1,1]{0,1,3,2:T(8,128)S(1)} %bitcast.52, f32[2,8,16,1024]{3,2,1,0:T(8,128)S(1)} %bitcast.57), kind=kOutput, calls=%fused_computation.96 | convolution fusion | flops 1610612736 | bytes 3670016 | tf_op jit(solution)/shard_map/dot_general | solution.py:223
  96.9 0.1 fusion.19
  97.0 0.0 copy-start.2
  97.1 2.0 copy.53
  99.0 2.9 %reshape.333 = bf16[64,2,1024]{2,1,0:T(2,128)(2,1)} reshape(bf16[512,2,8,16]{3,2,1,0:T(8,128)(2,1)S(1)} %bitcast.45) | data formatting | bytes 524288
  102.0 6.2 %all-to-all-start.2 = ((bf16[64,2,1024]{2,1,0:T(2,128)(2,1)}), bf16[64,2,1024]{2,1,0:T(2,128)(2,1)S(1)}, u32[]{:S(2)}, u32[]{:S(2)}) async-start(bf16[64,2,1024]{2,1,0:T(2,128)(2,1)} %reshape.333), calls=%async_computation.2 | async-start | bytes 524288 | tf_op jit(solution)/shard_map/all_to_all | solution.py:228
  108.2 0.0 copy-done.2
  108.2 0.8 maximum_bitcast_fusion.1.ph_ref
  109.0 9.9 %fusion.tm_ref = bf16[8,2,256,512]{3,2,1,0:T(8,128)(2,1)} fusion(bf16[256,2,8,512]{3,2,1,0:T(8,128)(2,1)} %param.7, pred[256,8]{0,1:T(8,128)(4,1)S(1)} %broadcast_compare_fusion), kind=kLoop, calls=%fused_computation.1 | loop fusion | flops 2097152 | bytes 8390656 | tf_op jit(solution)/shard_map/transpose | solution.py:76
  118.9 1.3 all-to-all-done.2
  120.2 1.4 reshape.334
  121.6 1.9 copy.68
  123.5 2.6 %copy.56.x_ref = bf16[16,2,8,512]{3,2,1,0:T(8,128)(2,1)} copy(bf16[16,2,8,512]{0,3,2,1:T(8,128)(2,1)} %bitcast.48) | data formatting | bytes 524288 | tf_op jit(solution)/shard_map/all_to_all | solution.py:228
  126.1 17.5 %shard_map.55 = bf16[4,16,2,8,512]{4,3,2,1,0:T(8,128)(2,1)} custom-call(bf16[16,2,8,512]{3,2,1,0:T(8,128)(2,1)} %copy.56.x_ref), custom_call_target="tpu_custom_call" | custom-call | tf_op jit(solution)/shard_map/pallas_call | solution.py:174
  143.6 2.8 %copy.57 = bf16[4,8,2,2,8,512]{5,1,0,2,3,4:T(8,128)(2,1)} copy(bf16[4,8,2,2,8,512]{5,4,3,2,1,0:T(8,128)(2,1)} %bitcast.50) | data formatting | bytes 2097152 | tf_op jit(solution)/shard_map/reshape;reshape | solution.py:237
  146.4 13.3 %shard_map.56.x_ref = f32[64,32,256]{2,1,0:T(8,128)} custom-call(f32[8,2,16,512]{3,2,1,0:T(8,128)} %maximum_bitcast_fusion.1.ph_ref, bf16[8,2,64,512]{3,2,1,0:T(8,128)(2,1)} %bitcast.58, bf16[8,2,256,512]{3,2,1,0:T(8,128)(2,1)} %fusion.tm_ref), custom_call_target="tpu_custom_call" | custom-call | flops 8589934592 | bytes 7864320 | tf_op jit(solution)/shard_map/pallas_call | solution.py:80
  159.7 6.3 %shard_map.57.x_ref = f32[32,32,256]{2,1,0:T(8,128)} custom-call(f32[64,32,256]{2,1,0:T(8,128)} %shard_map.56.x_ref), custom_call_target="tpu_custom_call" | custom-call | tf_op jit(solution)/shard_map/pallas_call | solution.py:131
  166.0 17.4 %shard_map.58.x_ref = f32[8,32,256]{2,1,0:T(8,128)} custom-call(f32[32,32,256]{2,1,0:T(8,128)} %shard_map.57.x_ref), custom_call_target="tpu_custom_call" | custom-call | tf_op jit(solution)/shard_map/pallas_call | solution.py:131
  183.4 12.3 %shard_map.59 = f32[1,32,256]{2,1,0:T(8,128)} custom-call(f32[8,32,256]{2,1,0:T(8,128)} %shard_map.58.x_ref), custom_call_target="tpu_custom_call" | custom-call | tf_op jit(solution)/shard_map/pallas_call | solution.py:131
  195.8 1.4 copy.70
  (5 shorter events, 0.1 us)
Async XLA Ops:
  7.7 30.3 %all-to-all-start = ((f32[64,8,256]{2,1,0:T(8,128)}), f32[64,8,256]{2,1,0:T(8,128)S(1)}, u32[]{:S(2)}, u32[]{:S(2)}) async-start(f32[64,8,256]{2,1,0:T(8,128)} %copy.41), calls=%async_computation | async-start | bytes 1048576 | tf_op jit(solution)/shard_map/all_to_all | solution.py:197
  38.0 1.8 copy-start
  52.9 8.4 %copy-start.5 = (s32[256]{0:T(256)S(1)}, s32[256]{0:T(256)}, u32[]{:S(2)}) copy-start(s32[256]{0:T(256)} %param.8) | copy-start | bytes 3076
  53.0 8.5 %copy-start.4 = (s32[16]{0:T(128)S(1)}, s32[16]{0:T(128)}, u32[]{:S(2)}) copy-start(s32[16]{0:T(128)} %param.9) | copy-start | bytes 196
  53.0 8.5 %copy-start.3 = (f32[512,8]{0,1:T(8,128)S(1)}, f32[512,8]{0,1:T(8,128)}, u32[]{:S(2)}) copy-start(f32[512,8]{0,1:T(8,128)} %param.6) | copy-start | bytes 49156
  54.7 34.8 %all-to-all-start.1 = ((f32[64,16,256]{2,1,0:T(8,128)}), f32[64,16,256]{2,1,0:T(8,128)S(1)}, u32[]{:S(2)}, u32[]{:S(2)}) async-start(f32[64,16,256]{2,1,0:T(8,128)} %copy.49), calls=%async_computation.1 | async-start | bytes 2097152 | tf_op jit(solution)/shard_map/all_to_all | solution.py:211
  90.9 3.9 %copy-start.1 = (f32[256,1024]{1,0:T(8,128)S(1)}, f32[256,1024]{1,0:T(8,128)}, u32[]{:S(2)}) copy-start(f32[256,1024]{1,0:T(8,128)} %copy.50) | copy-start | bytes 3145732
  97.0 11.1 %copy-start.2 = (f32[1,16,8,512]{3,1,0,2:T(8,128)S(1)}, f32[1,16,8,512]{3,1,0,2:T(8,128)}, u32[]{:S(2)}) copy-start(f32[1,16,8,512]{3,1,0,2:T(8,128)} %get-tuple-element.12) | copy-start | bytes 786436
  102.0 18.2 %all-to-all-start.2 = ((bf16[64,2,1024]{2,1,0:T(2,128)(2,1)}), bf16[64,2,1024]{2,1,0:T(2,128)(2,1)S(1)}, u32[]{:S(2)}, u32[]{:S(2)}) async-start(bf16[64,2,1024]{2,1,0:T(2,128)(2,1)} %reshape.333), calls=%async_computation.2 | async-start | bytes 524288 | tf_op jit(solution)/shard_map/all_to_all | solution.py:228

commit v18 on v12

--- a/solution.py
+++ b/solution.py
@@ -49,7 +49,7 @@
         lhs_ref[pl.ds(rows + r0, chunk * lag_total), :] = imag_q.reshape(chunk * lag_total, -1).astype(jnp.bfloat16)
         return carry
 
-    lax.fori_loop(0, seg_count // chunk, build, 0)
+    lax.fori_loop(0, seg_count // chunk, build, 0, unroll=True)
     dims = (((1,), (0,)), ((), ()))
     lhs = lhs_ref[...]
     with_re = lax.dot_general(lhs, tm_ref[0, 0], dims, preferred_element_type=jnp.float32)

time: 203 us -> 198 us (0.975)
  Pallas kernels: 71.1 us -> 65.7 us
    pallas_call x1, Pallas kernels: 18.4 us -> 13 us  [intersect(): pl.pallas_call(intersect_kernel, out_shape=jax.ShapeDtypeStruct((seg_coun...]
where the time goes in v18:
time: 198 us; the launch traced here: 196 us
  Pallas kernels  65.7 us (33%)
  local copies, waits for them, and re-layouts  47.4 us (24%)
  waiting for transfers between devices  34.6 us (17%)
  starting transfers between devices  25.5 us (13%)
  other arithmetic  14.8 us (7%)
  matrix products  7.78 us (4%)
    pallas_call x3, Pallas kernels, scatter_sum(): pl.pallas_call(functools.partial(scatter_kernel, axis, size), out_shape=j...  35.1 us
    pallas_call x1, Pallas kernels, gather_all(): pl.pallas_call(functools.partial(gather_kernel, axis, size), out_shape=ja...  17.5 us
    all_to_all x1, waiting for transfers between devices, spectrum_blocks(): lax.all_to_all(twisted, FREQ, 0, 0, tiled=True)  16.2 us
    unnamed x16, local copies, waits for them, and re-layouts  13.3 us
    pallas_call x1, Pallas kernels, intersect(): pl.pallas_call(intersect_kernel, out_shape=jax.ShapeDtypeStruct((seg_coun...  13 us
    all_to_all x1, starting transfers between devices, spectrum_blocks(): lax.all_to_all(sent, FREQ, 0, 0, tiled=True)  13 us
    another operation x4, local copies, waits for them, and re-layouts, spectrum_blocks(): jnp.stack([real_part * twist_cos + imag_part * twist_sin, imag_part * twi...  12.5 us
    all_to_all x1, waiting for transfers between devices, spectrum_blocks(): lax.all_to_all(sent, FREQ, 0, 0, tiled=True)  11.6 us
  transfers between devices with their start and end apart: 3, of which 3 were waited for; matrix products, arithmetic and copies ran while one was open for 12% of the time, Pallas kernels for 0%

profile of v18, /device:TPU:1, one launch (start us, length us, event | category | flops | bytes accessed | tf_op | source)
XLA Modules:
  0.0 196.0 jit_solution(1314436901375663915)
XLA Ops:
  0.0 3.7 %reshape.323 = f32[16,8,64,16]{3,2,1,0:T(8,128)} reshape(f32[16,8192]{1,0:T(8,128)} %param.5) | data formatting | bytes 1048576 | tf_op jit(solution)/shard_map/reshape | solution.py:195
  3.7 2.9 %copy.40 = f32[64,8,16,16]{0,3,2,1:T(8,128)S(1)} copy(f32[64,8,16,16]{2,0,1,3:T(8,128)} %bitcast.44) | data formatting | bytes 1048576 | tf_op jit(solution)/shard_map/transpose | solution.py:195
  6.6 1.1 copy.41
  7.7 13.0 %all-to-all-start = ((f32[64,8,256]{2,1,0:T(8,128)}), f32[64,8,256]{2,1,0:T(8,128)S(1)}, u32[]{:S(2)}, u32[]{:S(2)}) async-start(f32[64,8,256]{2,1,0:T(8,128)} %copy.41), calls=%async_computation | async-start | bytes 1048576 | tf_op jit(solution)/shard_map/all_to_all | solution.py:197
  20.7 0.2 fusion.48
  21.0 0.1 broadcast_in_dim.11
  21.0 0.2 copy.42
  21.2 0.1 broadcast_in_dim.12
  21.3 1.0 copy.43
  22.3 4.1 %sine_negate_fusion = (f32[512,512]{1,0:T(8,128)S(1)}, f32[512,512]{1,0:T(8,128)S(1)}) fusion(), kind=kLoop, calls=%fused_computation.15 | loop fusion | flops 3932160 | bytes 2097152 | tf_op jit(solution)/shard_map/neg | solution.py:194
  26.4 11.6 %all-to-all-done = f32[64,8,256]{2,1,0:T(8,128)S(1)} async-done(((f32[64,8,256]{2,1,0:T(8,128)}), f32[64,8,256]{2,1,0:T(8,128)S(1)}, u32[]{:S(2)}, u32[]{:S(2)}) %all-to-all-start) | async-done | bytes 524320 | tf_op jit(solution)/shard_map/all_to_all | solution.py:197
  38.0 0.0 copy-start
  38.0 1.8 fusion
  39.9 0.0 copy-done
  39.9 0.1 multiply_add_fusion.1
  40.0 2.6 %stack.21 = f32[1,64,8,16,16]{4,3,2,1,0:T(8,128)} reshape(f32[512,256]{1,0:T(8,128)S(1)} %get-tuple-element.5) | data formatting | bytes 1048576 | tf_op jit(solution)/shard_map/stack | solution.py:205
  42.6 3.6 %copy.46 = f32[1,64,8,16,16]{1,4,3,2,0:T(8,128)S(1)} copy(f32[1,64,8,16,16]{4,3,2,1,0:T(8,128)} %stack.21) | data formatting | bytes 1048576 | tf_op jit(solution)/shard_map/stack | solution.py:205
  46.3 2.6 %stack.22 = f32[1,64,8,16,16]{4,3,2,1,0:T(8,128)} reshape(f32[512,256]{1,0:T(8,128)S(1)} %get-tuple-element.6) | data formatting | bytes 1048576 | tf_op jit(solution)/shard_map/stack | solution.py:205
  48.9 3.6 %copy.47 = f32[1,64,8,16,16]{1,4,3,2,0:T(8,128)S(1)} copy(f32[1,64,8,16,16]{4,3,2,1,0:T(8,128)} %stack.22) | data formatting | bytes 1048576 | tf_op jit(solution)/shard_map/stack | solution.py:205
  52.5 0.2 maximum_bitcast_fusion
  52.7 0.2 copy.48
  52.9 1.8 copy.49
  54.7 6.3 %all-to-all-start.1 = ((f32[64,16,256]{2,1,0:T(8,128)}), f32[64,16,256]{2,1,0:T(8,128)S(1)}, u32[]{:S(2)}, u32[]{:S(2)}) async-start(f32[64,16,256]{2,1,0:T(8,128)} %copy.49), calls=%async_computation.1 | async-start | bytes 2097152 | tf_op jit(solution)/shard_map/all_to_all | solution.py:211
  61.0 0.0 copy-start.5
  61.0 0.0 copy-start.4
  61.0 0.0 copy-start.3
  61.0 7.5 %copy.58 = bf16[256,2,8,512]{0,3,1,2:T(8,128)(2,1)} copy(bf16[256,2,8,512]{3,2,1,0:T(8,128)(2,1)} %param.7) | data formatting | bytes 8388608 | tf_op args[2]
  68.6 0.3 fusion.39
  68.9 0.0 copy-done.5
  68.9 0.1 broadcast_compare_fusion
  69.0 0.0 copy-done.4
  69.0 0.1 fusion.49
  69.0 0.0 copy-done.3
  69.0 0.1 add_select_fusion.6
  69.1 0.3 fusion.42
  69.5 1.9 fusion.20
  71.4 2.0 %multiply_subtract_fusion = (f32[512,32,32]{0,2,1:T(8,128)}, f32[512,32,32]{0,2,1:T(8,128)S(1)}) fusion(f32[512,32]{0,1:T(8,128)S(1)} %get-tuple-element.17, f32[512,32]{0,1:T(8,128)S(1)} %get-tuple-element.16, f32[512,32]{0,1:T(8,128)S(1)} %get-tuple-element.18, f32[512,32]{0,1:T(8,128)S(1)} %get-tuple-element.15), kind=kLoop, calls=%fused_computation.8 | loop fusion | flops 3145728 | bytes 4456448 | tf_op jit(solution)/shard_map/sub | solution.py:217
  73.3 16.2 %all-to-all-done.1 = f32[64,16,256]{2,1,0:T(8,128)S(1)} async-done(((f32[64,16,256]{2,1,0:T(8,128)}), f32[64,16,256]{2,1,0:T(8,128)S(1)}, u32[]{:S(2)}, u32[]{:S(2)}) %all-to-all-start.1) | async-done | bytes 1048608 | tf_op jit(solution)/shard_map/all_to_all | solution.py:211
  89.6 1.3 copy.50
  90.9 0.0 copy-start.1
  90.9 3.9 %fusion.52 = f32[512,2,8,16]{0,3,2,1:T(8,128)S(1)} fusion(f32[512,1024,1,1]{0,1,3,2:T(8,128)} %bitcast.53, f32[2,8,16,1024]{3,2,1,0:T(8,128)} %bitcast.56), kind=kOutput, calls=%fused_computation.94 | convolution fusion | flops 1610612736 | bytes 3670016 | tf_op jit(solution)/shard_map/dot_general | solution.py:222
  94.8 0.0 copy-done.1
  94.8 2.0 %fusion.53 = f32[512,2,8,16]{0,3,2,1:T(8,128)S(1)} fusion(f32[512,1024,1,1]{0,1,3,2:T(8,128)S(1)} %bitcast.52, f32[2,8,16,1024]{3,2,1,0:T(8,128)S(1)} %bitcast.57), kind=kOutput, calls=%fused_computation.95 | convolution fusion | flops 1610612736 | bytes 3670016 | tf_op jit(solution)/shard_map/dot_general | solution.py:223
  96.9 0.1 fusion.18
  97.0 0.0 copy-start.2
  97.0 2.0 %copy.53 = bf16[16,2,512,8]{0,3,1,2:T(8,128)(2,1)S(1)} copy(bf16[16,2,512,8]{2,0,3,1:T(8,128)(2,1)S(1)} %maximum_bitcast_fusion.2) | data formatting | bytes 524288 | tf_op jit(solution)/shard_map/convert_element_type | solution.py:227
  99.0 2.9 %reshape.333 = bf16[64,2,1024]{2,1,0:T(2,128)(2,1)} reshape(bf16[512,2,8,16]{3,2,1,0:T(8,128)(2,1)S(1)} %bitcast.45) | data formatting | bytes 524288
  101.9 6.2 %all-to-all-start.2 = ((bf16[64,2,1024]{2,1,0:T(2,128)(2,1)}), bf16[64,2,1024]{2,1,0:T(2,128)(2,1)S(1)}, u32[]{:S(2)}, u32[]{:S(2)}) async-start(bf16[64,2,1024]{2,1,0:T(2,128)(2,1)} %reshape.333), calls=%async_computation.2 | async-start | bytes 524288 | tf_op jit(solution)/shard_map/all_to_all | solution.py:228
  108.2 0.0 copy-done.2
  108.2 0.8 maximum_bitcast_fusion.1.ph_ref
  109.0 4.4 %select_bitcast_fusion.tm_ref = bf16[8,2,512,256]{3,2,1,0:T(8,128)(2,1)} fusion(bf16[256,2,8,512]{0,3,1,2:T(8,128)(2,1)} %copy.58, pred[256,8]{0,1:T(8,128)(4,1)S(1)} %broadcast_compare_fusion), kind=kLoop, calls=%fused_computation | loop fusion | flops 2097152 | bytes 8390656 | tf_op jit(solution)/shard_map/transpose | solution.py:76
  113.4 6.7 %all-to-all-done.2 = bf16[64,2,1024]{2,1,0:T(2,128)(2,1)S(1)} async-done(((bf16[64,2,1024]{2,1,0:T(2,128)(2,1)}), bf16[64,2,1024]{2,1,0:T(2,128)(2,1)S(1)}, u32[]{:S(2)}, u32[]{:S(2)}) %all-to-all-start.2) | async-done | bytes 262176 | tf_op jit(solution)/shard_map/all_to_all | solution.py:228
  120.2 1.4 reshape.334
  121.6 1.9 copy.65
  123.5 2.6 %copy.56.x_ref = bf16[16,2,8,512]{3,2,1,0:T(8,128)(2,1)} copy(bf16[16,2,8,512]{0,3,2,1:T(8,128)(2,1)} %bitcast.48) | data formatting | bytes 524288 | tf_op jit(solution)/shard_map/all_to_all | solution.py:228
  126.1 17.5 %shard_map.55 = bf16[4,16,2,8,512]{4,3,2,1,0:T(8,128)(2,1)} custom-call(bf16[16,2,8,512]{3,2,1,0:T(8,128)(2,1)} %copy.56.x_ref), custom_call_target="tpu_custom_call" | custom-call | tf_op jit(solution)/shard_map/pallas_call | solution.py:174
  143.6 2.8 %copy.57 = bf16[4,8,2,2,8,512]{5,1,0,2,3,4:T(8,128)(2,1)} copy(bf16[4,8,2,2,8,512]{5,4,3,2,1,0:T(8,128)(2,1)} %bitcast.50) | data formatting | bytes 2097152 | tf_op jit(solution)/shard_map/reshape;reshape | solution.py:237
  146.4 13.0 %shard_map.56.x_ref = f32[64,32,256]{2,1,0:T(8,128)} custom-call(f32[8,2,16,512]{3,2,1,0:T(8,128)} %maximum_bitcast_fusion.1.ph_ref, bf16[8,2,64,512]{3,2,1,0:T(8,128)(2,1)} %bitcast.58, bf16[8,2,512,256]{3,2,1,0:T(8,128)(2,1)} %select_bitcast_fusion.tm_ref), custom_call_target="tpu_custom_call" | custom-call | flops 8589934592 | bytes 7864320 | tf_op jit(solution)/shard_map/pallas_call | solution.py:80
  159.4 6.3 %shard_map.57.x_ref = f32[32,32,256]{2,1,0:T(8,128)} custom-call(f32[64,32,256]{2,1,0:T(8,128)} %shard_map.56.x_ref), custom_call_target="tpu_custom_call" | custom-call | tf_op jit(solution)/shard_map/pallas_call | solution.py:131
  165.7 17.4 %shard_map.58.x_ref = f32[8,32,256]{2,1,0:T(8,128)} custom-call(f32[32,32,256]{2,1,0:T(8,128)} %shard_map.57.x_ref), custom_call_target="tpu_custom_call" | custom-call | tf_op jit(solution)/shard_map/pallas_call | solution.py:131
  183.1 11.5 %shard_map.59 = f32[1,32,256]{2,1,0:T(8,128)} custom-call(f32[8,32,256]{2,1,0:T(8,128)} %shard_map.58.x_ref), custom_call_target="tpu_custom_call" | custom-call | tf_op jit(solution)/shard_map/pallas_call | solution.py:131
  194.6 1.4 copy.67
  (5 shorter events, 0.0 us)
Async XLA Ops:
  7.7 30.3 %all-to-all-start = ((f32[64,8,256]{2,1,0:T(8,128)}), f32[64,8,256]{2,1,0:T(8,128)S(1)}, u32[]{:S(2)}, u32[]{:S(2)}) async-start(f32[64,8,256]{2,1,0:T(8,128)} %copy.41), calls=%async_computation | async-start | bytes 1048576 | tf_op jit(solution)/shard_map/all_to_all | solution.py:197
  38.0 1.8 copy-start
  54.7 34.8 %all-to-all-start.1 = ((f32[64,16,256]{2,1,0:T(8,128)}), f32[64,16,256]{2,1,0:T(8,128)S(1)}, u32[]{:S(2)}, u32[]{:S(2)}) async-start(f32[64,16,256]{2,1,0:T(8,128)} %copy.49), calls=%async_computation.1 | async-start | bytes 2097152 | tf_op jit(solution)/shard_map/all_to_all | solution.py:211
  61.0 7.9 %copy-start.5 = (s32[256]{0:T(256)S(1)}, s32[256]{0:T(256)}, u32[]{:S(2)}) copy-start(s32[256]{0:T(256)} %param.8) | copy-start | bytes 3076
  61.0 7.9 %copy-start.4 = (s32[16]{0:T(128)S(1)}, s32[16]{0:T(128)}, u32[]{:S(2)}) copy-start(s32[16]{0:T(128)} %param.9) | copy-start | bytes 196
  61.0 8.0 %copy-start.3 = (f32[512,8]{0,1:T(8,128)S(1)}, f32[512,8]{0,1:T(8,128)}, u32[]{:S(2)}) copy-start(f32[512,8]{0,1:T(8,128)} %param.6) | copy-start | bytes 49156
  90.9 3.9 %copy-start.1 = (f32[256,1024]{1,0:T(8,128)S(1)}, f32[256,1024]{1,0:T(8,128)}, u32[]{:S(2)}) copy-start(f32[256,1024]{1,0:T(8,128)} %copy.50) | copy-start | bytes 3145732
  97.0 11.1 %copy-start.2 = (f32[1,16,8,512]{3,1,0,2:T(8,128)S(1)}, f32[1,16,8,512]{3,1,0,2:T(8,128)}, u32[]{:S(2)}) copy-start(f32[1,16,8,512]{3,1,0,2:T(8,128)} %get-tuple-element.12) | copy-start | bytes 786436
  101.9 18.2 %all-to-all-start.2 = ((bf16[64,2,1024]{2,1,0:T(2,128)(2,1)}), bf16[64,2,1024]{2,1,0:T(2,128)(2,1)S(1)}, u32[]{:S(2)}, u32[]{:S(2)}) async-start(bf16[64,2,1024]{2,1,0:T(2,128)(2,1)} %reshape.333), calls=%async_computation.2 | async-start | bytes 524288 | tf_op jit(solution)/shard_map/all_to_all | solution.py:228
